TPU v7x, 32 devices: a whole 2x2x4 slice. The times are simulated.
32 devices in a mesh: dp: 8 (over y, x, core), ctx: 4 (over z).
Axes of the slice: x: 2, y: 2, z: 4, core: 2. Of those that a mesh axis runs over, the one named last changes fastest.
Arguments:
- tokens: bfloat16 [8192, 768], P(('dp', 'ctx')), may hold values from -6 to 6
- cotangent: bfloat16 [8192, 768], P(('dp', 'ctx')), may hold values from -6 to 6
- token_order: int32 [8192], P(('dp', 'ctx')), may hold values from 0 to 8191, as said below
- sequence_ids: int32 [8, 1024], P('dp'), may hold values from 0 to 3, never falling along the last dimension, each value on 1 to 512 neighbouring positions
- valid: int32 [8192], P(('dp', 'ctx')), may hold values from 0 to 1
- teacher: float32 [8192, 768], P(('dp', 'ctx')), may hold values from -6 to 6
- w_query: bfloat16 [768, 768], P('dp'), may hold values from -0.3125 to 0.3125
- b_query: bfloat16 [768], P('dp'), may hold values from -1.75 to 1.75
- w_key: bfloat16 [768, 768], P('dp'), may hold values from -0.3125 to 0.3125
- w_value: bfloat16 [768, 768], P('dp'), may hold values from -0.21875 to 0.21875
- b_value: bfloat16 [768], P('dp'), may hold values from -1.75 to 1.75
- w_out: bfloat16 [768, 768], P('dp'), may hold values from -0.875 to 0.875
- b_out: bfloat16 [768], P('dp'), may hold values from -3 to 3
- norm1_gain: bfloat16 [768], P('dp'), may hold values from 0.25 to 1.75
- norm1_bias: bfloat16 [768], P('dp'), may hold values from -1.75 to 1.75
- w_up: bfloat16 [768, 3072], P('dp'), may hold values from -0.21875 to 0.21875
- b_up: bfloat16 [3072], P('dp'), may hold values from -3 to 3
- w_down: bfloat16 [3072, 768], P('dp'), may hold values from -0.109375 to 0.109375
- b_down: bfloat16 [768], P('dp'), may hold values from -1.75 to 1.75
- norm2_gain: bfloat16 [768], P('dp'), may hold values from 0.25 to 1.75
- norm2_bias: bfloat16 [768], P('dp'), may hold values from -1.75 to 1.75
Outputs:
- output: float32 [8192, 768], P(('dp', 'ctx'))
- loss: float32 [], replicated
- input_grad: float32 [8192, 768], P(('dp', 'ctx'))
- grad_w_query: float32 [768, 768], P('dp')
- grad_b_query: float32 [768], P('dp')
- grad_w_key: float32 [768, 768], P('dp')
- grad_w_value: float32 [768, 768], P('dp')
- grad_b_value: float32 [768], P('dp')
- grad_w_out: float32 [768, 768], P('dp')
- grad_b_out: float32 [768], P('dp')
- grad_norm1_gain: float32 [768], P('dp')
- grad_norm1_bias: float32 [768], P('dp')
- grad_w_up: float32 [768, 3072], P('dp')
- grad_b_up: float32 [3072], P('dp')
- grad_w_down: float32 [3072, 768], P('dp')
- grad_b_down: float32 [768], P('dp')
- grad_norm2_gain: float32 [768], P('dp')
- grad_norm2_bias: float32 [768], P('dp')
Inputs may be any that keep to these rules, and one draw needn't show every extreme that they name: `token_order`: a permutation of the 8192 tokens; each aligned block of 256 packed positions takes exactly 8 tokens from each aligned block of 256 given tokens. `sequence_ids`: ids of a row never fall; a sequence has at most 512 tokens, and some has exactly that many.
All inputs are finite; a program needn't handle non-finite values.
Results may differ from a plain program's by a relative error of at most 0.023.
Values may be sent and summed in bfloat16 or wider, within the bound.
A program may use at most 128 MiB of HBM per device.

v0:
```python
from functools import partial
import math

import jax
import jax.numpy as jnp
from jax import lax
from jax.sharding import PartitionSpec as P

HEADS = 12


norm_eps = 1e-12
floor_score = -1e30
masked_score = -1e32


def product(left, right):
    return jnp.dot(left, right, preferred_element_type=jnp.float32)


def inner_rows(left, right):
    return lax.dot_general(
        left, right, (((0,), (0,)), ((), ())), preferred_element_type=jnp.float32
    )


def against(left, right):
    return lax.dot_general(
        left, right, (((1,), (1,)), ((), ())), preferred_element_type=jnp.float32
    )


def layer_norm(value, gain, shift):
    centre = value - jnp.mean(value, -1, keepdims=True)
    spread = jnp.mean(centre * centre, -1, keepdims=True)
    inverse_dev = lax.rsqrt(spread + norm_eps)
    scaled = centre * inverse_dev
    return (scaled * gain + shift, scaled, inverse_dev)


def norm_back(grad_norm, scaled, inverse_dev, gain):
    grad_scaled = grad_norm * gain
    centred = grad_scaled - jnp.mean(grad_scaled, -1, keepdims=True)
    return inverse_dev * (centred - scaled * jnp.mean(grad_scaled * scaled, -1, keepdims=True))


def per_device(
    tokens,
    cotangent,
    token_order,
    sequence_ids,
    valid,
    teacher,
    w_query,
    b_query,
    w_key,
    w_value,
    b_value,
    w_out,
    b_out,
    norm1_gain,
    norm1_bias,
    w_up,
    b_up,
    w_down,
    b_down,
    norm2_gain,
    norm2_bias,
):
    tok_rows, model_width = tokens.shape
    peer_count = lax.axis_size(("dp", "ctx"))
    per_peer = tok_rows // peer_count
    head_count = HEADS
    head_size = model_width // head_count
    score_scale = head_size ** (-0.5)
    gelu_exact = partial(jax.nn.gelu, approximate=False)
    positions = lax.iota(jnp.int32, tok_rows)
    source = token_order // tok_rows
    slot_sort = jnp.argsort(source * tok_rows + positions)
    requests = (token_order[slot_sort] % tok_rows).reshape(peer_count, per_peer)
    wanted = lax.all_to_all(requests, ("dp", "ctx"), split_axis=0, concat_axis=0, tiled=True)
    wanted_flat = wanted.reshape(tok_rows)
    packed_x, packed_cot = (
        lax.all_to_all(
            tokens[wanted_flat].reshape(peer_count, per_peer, model_width),
            ("dp", "ctx"),
            split_axis=0,
            concat_axis=0,
            tiled=True,
        ),
        lax.all_to_all(
            cotangent[wanted_flat].reshape(peer_count, per_peer, model_width),
            ("dp", "ctx"),
            split_axis=0,
            concat_axis=0,
            tiled=True,
        ),
    )
    arrival = jnp.argsort(slot_sort)
    inputs = packed_x.reshape(tok_rows, model_width)[arrival]
    cot_rows = packed_cot.reshape(tok_rows, model_width)[arrival].astype(jnp.float32)
    valid_rows = valid.astype(jnp.float32)
    valid_count = lax.psum(jnp.sum(valid_rows), ("dp", "ctx"))
    (
        query_weight,
        query_bias,
        key_weight,
        value_weight,
        value_bias,
        out_weight,
        out_bias,
        gain_one,
        shift_one,
        up_weight,
        up_bias,
        down_weight,
        down_bias,
        gain_two,
        shift_two,
    ) = (
        lax.all_gather(w_query, "dp", axis=0, tiled=True),
        lax.all_gather(b_query, "dp", axis=0, tiled=True),
        lax.all_gather(w_key, "dp", axis=0, tiled=True),
        lax.all_gather(w_value, "dp", axis=0, tiled=True),
        lax.all_gather(b_value, "dp", axis=0, tiled=True),
        lax.all_gather(w_out, "dp", axis=0, tiled=True),
        lax.all_gather(b_out, "dp", axis=0, tiled=True),
        lax.all_gather(norm1_gain, "dp", axis=0, tiled=True),
        lax.all_gather(norm1_bias, "dp", axis=0, tiled=True),
        lax.all_gather(w_up, "dp", axis=0, tiled=True),
        lax.all_gather(b_up, "dp", axis=0, tiled=True),
        lax.all_gather(w_down, "dp", axis=0, tiled=True),
        lax.all_gather(b_down, "dp", axis=0, tiled=True),
        lax.all_gather(norm2_gain, "dp", axis=0, tiled=True),
        lax.all_gather(norm2_bias, "dp", axis=0, tiled=True),
    )
    queries = (product(inputs, query_weight) + query_bias).astype(jnp.bfloat16)
    key_rows = product(inputs, key_weight).astype(jnp.bfloat16)
    values = (product(inputs, value_weight) + value_bias).astype(jnp.bfloat16)
    group_ids = sequence_ids.reshape(-1)
    cycle_index = lax.axis_index("ctx")
    query_ids = lax.dynamic_slice_in_dim(group_ids, cycle_index * tok_rows, tok_rows)
    query_heads = queries.reshape(tok_rows, head_count, head_size)
    initial = (
        jnp.full((head_count, tok_rows), floor_score, jnp.float32),
        jnp.zeros((head_count, tok_rows), jnp.float32),
        jnp.zeros((tok_rows, head_count, head_size), jnp.float32),
    )
    folded = initial
    key_piece = lax.all_gather(key_rows, "ctx", axis=0, tiled=True)
    value_piece = lax.all_gather(values, "ctx", axis=0, tiled=True)
    length = key_piece.shape[0]
    attend_block_rows = math.gcd(length, 512)
    block_count = length // attend_block_rows

    def one_block(carried, inputs_block):
        running_max, running_sum, summed = carried
        key_block, value_block, key_start = inputs_block
        key_ids = lax.dynamic_slice_in_dim(group_ids, key_start, attend_block_rows)
        scores = (
            jnp.einsum("qhd,khd->hqk", query_heads, key_block, preferred_element_type=jnp.float32)
            * score_scale
        )
        scores = jnp.where((query_ids[:, None] == key_ids[None, :])[None], scores, masked_score)
        new_max = jnp.maximum(running_max, jnp.max(scores, -1))
        factor = jnp.exp(running_max - new_max)
        weights = jnp.exp(scores - new_max[:, :, None])
        running_sum = running_sum * factor + jnp.sum(weights, -1)
        update = jnp.einsum(
            "hqk,khd->qhd",
            weights.astype(jnp.bfloat16),
            value_block,
            preferred_element_type=jnp.float32,
        )
        summed = summed * jnp.transpose(factor)[:, :, None] + update
        return ((new_max, running_sum, summed), None)

    key_starts = attend_block_rows * lax.iota(jnp.int32, block_count)
    folded, _ = lax.scan(
        one_block,
        folded,
        (
            key_piece.reshape(block_count, attend_block_rows, head_count, head_size),
            value_piece.reshape(block_count, attend_block_rows, head_count, head_size),
            key_starts,
        ),
    )
    running_max, running_sum, summed = folded
    attended = summed / jnp.transpose(running_sum)[:, :, None]
    log_total = running_max + jnp.log(running_sum)
    context = attended.reshape(tok_rows, model_width).astype(jnp.bfloat16)
    branch = product(context, out_weight) + out_bias
    normed, scaled_one, inverse_one = layer_norm(
        inputs.astype(jnp.float32) + branch, gain_one, shift_one
    )
    normed_low = normed.astype(jnp.bfloat16)
    pre_act = product(normed_low, up_weight) + up_bias
    activated = gelu_exact(pre_act).astype(jnp.bfloat16)
    ffn_out = product(activated, down_weight) + down_bias
    result, scaled_two, inverse_two = layer_norm(normed + ffn_out, gain_two, shift_two)
    difference = result - teacher
    loss_total = lax.psum(jnp.sum(valid_rows[:, None] * difference * difference), ("dp", "ctx"))
    loss_value = loss_total / (valid_count * model_width)
    grad_out = cot_rows + 2.0 / (valid_count * model_width) * valid_rows[:, None] * difference
    grad_gain_two = jnp.sum(grad_out * scaled_two, 0)
    grad_shift_two = jnp.sum(grad_out, 0)
    grad_res_two = norm_back(grad_out, scaled_two, inverse_two, gain_two)
    grad_ffn = grad_res_two.astype(jnp.bfloat16)
    grad_down = inner_rows(activated, grad_ffn)
    grad_down_bias = jnp.sum(grad_ffn.astype(jnp.float32), 0)
    grad_act = against(grad_ffn, down_weight)
    _, gelu_pull = jax.vjp(gelu_exact, pre_act)
    grad_pre = gelu_pull(grad_act)[0].astype(jnp.bfloat16)
    grad_up = inner_rows(normed_low, grad_pre)
    grad_up_bias = jnp.sum(grad_pre.astype(jnp.float32), 0)
    grad_normed = grad_res_two + against(grad_pre, up_weight)
    ffn_shards = (
        lax.psum_scatter(
            grad_up.astype(jnp.bfloat16), "dp", scatter_dimension=0, tiled=True
        ).astype(jnp.float32),
        lax.psum_scatter(
            grad_up_bias.astype(jnp.bfloat16), "dp", scatter_dimension=0, tiled=True
        ).astype(jnp.float32),
        lax.psum_scatter(
            grad_down.astype(jnp.bfloat16), "dp", scatter_dimension=0, tiled=True
        ).astype(jnp.float32),
        lax.psum_scatter(
            grad_down_bias.astype(jnp.bfloat16), "dp", scatter_dimension=0, tiled=True
        ).astype(jnp.float32),
        lax.psum_scatter(
            grad_gain_two.astype(jnp.bfloat16), "dp", scatter_dimension=0, tiled=True
        ).astype(jnp.float32),
        lax.psum_scatter(
            grad_shift_two.astype(jnp.bfloat16), "dp", scatter_dimension=0, tiled=True
        ).astype(jnp.float32),
    )
    grad_gain_one = jnp.sum(grad_normed * scaled_one, 0)
    grad_shift_one = jnp.sum(grad_normed, 0)
    grad_res_one = norm_back(grad_normed, scaled_one, inverse_one, gain_one)
    grad_branch = grad_res_one.astype(jnp.bfloat16)
    grad_out_w = inner_rows(context, grad_branch)
    grad_out_bias = jnp.sum(grad_branch.astype(jnp.float32), 0)
    grad_context = against(grad_branch, out_weight).astype(jnp.bfloat16)
    grad_heads = grad_context.reshape(tok_rows, head_count, head_size)
    delta = jnp.transpose(jnp.sum(grad_heads.astype(jnp.float32) * attended, -1))
    all_keys, all_values = (
        lax.all_gather(key_rows, "ctx", axis=0, tiled=True),
        lax.all_gather(values, "ctx", axis=0, tiled=True),
    )
    group_len = all_keys.shape[0]
    block_rows = math.gcd(group_len, 512)
    block_count = group_len // block_rows
    key_starts = block_rows * lax.iota(jnp.int32, block_count)
    key_blocks = all_keys.reshape(block_count, block_rows, head_count, head_size)
    value_blocks = all_values.reshape(block_count, block_rows, head_count, head_size)

    def query_side(key_block, value_block, key_start):
        key_ids = lax.dynamic_slice_in_dim(group_ids, key_start, block_rows)
        scores = (
            jnp.einsum("qhd,khd->hqk", query_heads, key_block, preferred_element_type=jnp.float32)
            * score_scale
        )
        scores = jnp.where((query_ids[:, None] == key_ids[None, :])[None], scores, masked_score)
        probs = jnp.exp(scores - log_total[:, :, None])
        grad_probs = jnp.einsum(
            "qhd,khd->hqk", grad_heads, value_block, preferred_element_type=jnp.float32
        )
        grad_scores = (probs * (grad_probs - delta[:, :, None])).astype(jnp.bfloat16)
        return (probs, grad_scores)

    def back_block(grad_query, inputs_block):
        key_block, value_block, key_start = inputs_block
        probs, grad_scores = query_side(key_block, value_block, key_start)
        grad_query = (
            grad_query
            + jnp.einsum("hqk,khd->qhd", grad_scores, key_block, preferred_element_type=jnp.float32)
            * score_scale
        )
        grad_key = (
            jnp.einsum("hqk,qhd->khd", grad_scores, query_heads, preferred_element_type=jnp.float32)
            * score_scale
        )
        grad_value = jnp.einsum(
            "hqk,qhd->khd",
            probs.astype(jnp.bfloat16),
            grad_heads,
            preferred_element_type=jnp.float32,
        )
        return (grad_query, (grad_key, grad_value))

    grad_query, (key_parts, value_parts) = lax.scan(
        back_block,
        jnp.zeros((tok_rows, head_count, head_size), jnp.float32),
        (key_blocks, value_blocks, key_starts),
    )
    key_total, value_total = (
        lax.psum_scatter(
            key_parts.reshape(group_len, model_width).astype(jnp.bfloat16),
            "ctx",
            scatter_dimension=0,
            tiled=True,
        ).astype(jnp.float32),
        lax.psum_scatter(
            value_parts.reshape(group_len, model_width).astype(jnp.bfloat16),
            "ctx",
            scatter_dimension=0,
            tiled=True,
        ).astype(jnp.float32),
    )
    grad_keys = key_total.astype(jnp.bfloat16)
    grad_values = value_total.astype(jnp.bfloat16)
    grad_queries = grad_query.reshape(tok_rows, model_width).astype(jnp.bfloat16)
    grad_query_w = inner_rows(inputs, grad_queries)
    grad_query_bias = jnp.sum(grad_queries.astype(jnp.float32), 0)
    grad_key_w = inner_rows(inputs, grad_keys)
    grad_value_w = inner_rows(inputs, grad_values)
    grad_value_bias = jnp.sum(grad_values.astype(jnp.float32), 0)
    grad_inputs = (
        grad_res_one
        + against(grad_queries, query_weight)
        + against(grad_keys, key_weight)
        + against(grad_values, value_weight)
    )
    attn_shards = (
        lax.psum_scatter(
            grad_query_w.astype(jnp.bfloat16), "dp", scatter_dimension=0, tiled=True
        ).astype(jnp.float32),
        lax.psum_scatter(
            grad_query_bias.astype(jnp.bfloat16), "dp", scatter_dimension=0, tiled=True
        ).astype(jnp.float32),
        lax.psum_scatter(
            grad_key_w.astype(jnp.bfloat16), "dp", scatter_dimension=0, tiled=True
        ).astype(jnp.float32),
        lax.psum_scatter(
            grad_value_w.astype(jnp.bfloat16), "dp", scatter_dimension=0, tiled=True
        ).astype(jnp.float32),
        lax.psum_scatter(
            grad_value_bias.astype(jnp.bfloat16), "dp", scatter_dimension=0, tiled=True
        ).astype(jnp.float32),
        lax.psum_scatter(
            grad_out_w.astype(jnp.bfloat16), "dp", scatter_dimension=0, tiled=True
        ).astype(jnp.float32),
        lax.psum_scatter(
            grad_out_bias.astype(jnp.bfloat16), "dp", scatter_dimension=0, tiled=True
        ).astype(jnp.float32),
        lax.psum_scatter(
            grad_gain_one.astype(jnp.bfloat16), "dp", scatter_dimension=0, tiled=True
        ).astype(jnp.float32),
        lax.psum_scatter(
            grad_shift_one.astype(jnp.bfloat16), "dp", scatter_dimension=0, tiled=True
        ).astype(jnp.float32),
    )
    totals = (
        lax.psum(attn_shards[0].astype(jnp.bfloat16), "ctx").astype(jnp.float32),
        lax.psum(attn_shards[1].astype(jnp.bfloat16), "ctx").astype(jnp.float32),
        lax.psum(attn_shards[2].astype(jnp.bfloat16), "ctx").astype(jnp.float32),
        lax.psum(attn_shards[3].astype(jnp.bfloat16), "ctx").astype(jnp.float32),
        lax.psum(attn_shards[4].astype(jnp.bfloat16), "ctx").astype(jnp.float32),
        lax.psum(attn_shards[5].astype(jnp.bfloat16), "ctx").astype(jnp.float32),
        lax.psum(attn_shards[6].astype(jnp.bfloat16), "ctx").astype(jnp.float32),
        lax.psum(attn_shards[7].astype(jnp.bfloat16), "ctx").astype(jnp.float32),
        lax.psum(attn_shards[8].astype(jnp.bfloat16), "ctx").astype(jnp.float32),
        lax.psum(ffn_shards[0].astype(jnp.bfloat16), "ctx").astype(jnp.float32),
        lax.psum(ffn_shards[1].astype(jnp.bfloat16), "ctx").astype(jnp.float32),
        lax.psum(ffn_shards[2].astype(jnp.bfloat16), "ctx").astype(jnp.float32),
        lax.psum(ffn_shards[3].astype(jnp.bfloat16), "ctx").astype(jnp.float32),
        lax.psum(ffn_shards[4].astype(jnp.bfloat16), "ctx").astype(jnp.float32),
        lax.psum(ffn_shards[5].astype(jnp.bfloat16), "ctx").astype(jnp.float32),
    )
    back_out, back_grad = (
        lax.all_to_all(
            result[slot_sort].reshape(peer_count, per_peer, model_width).astype(jnp.bfloat16),
            ("dp", "ctx"),
            split_axis=0,
            concat_axis=0,
            tiled=True,
        ).astype(jnp.float32),
        lax.all_to_all(
            grad_inputs[slot_sort].reshape(peer_count, per_peer, model_width).astype(jnp.bfloat16),
            ("dp", "ctx"),
            split_axis=0,
            concat_axis=0,
            tiled=True,
        ).astype(jnp.float32),
    )
    homeward = jnp.argsort(wanted_flat)
    output = back_out.reshape(tok_rows, model_width)[homeward]
    input_grad = back_grad.reshape(tok_rows, model_width)[homeward]
    return (
        output,
        loss_value,
        input_grad,
        totals[0],
        totals[1],
        totals[2],
        totals[3],
        totals[4],
        totals[5],
        totals[6],
        totals[7],
        totals[8],
        totals[9],
        totals[10],
        totals[11],
        totals[12],
        totals[13],
        totals[14],
    )


def solution(mesh):
    in_specs = (
        P(("dp", "ctx"), None),
        P(("dp", "ctx"), None),
        P(("dp", "ctx")),
        P("dp", None),
        P(("dp", "ctx")),
        P(("dp", "ctx"), None),
        P("dp", None),
        P("dp"),
        P("dp", None),
        P("dp", None),
        P("dp"),
        P("dp", None),
        P("dp"),
        P("dp"),
        P("dp"),
        P("dp", None),
        P("dp"),
        P("dp", None),
        P("dp"),
        P("dp"),
        P("dp"),
    )
    out_specs = (
        P(("dp", "ctx"), None),
        P(),
        P(("dp", "ctx"), None),
        P("dp", None),
        P("dp"),
        P("dp", None),
        P("dp", None),
        P("dp"),
        P("dp", None),
        P("dp"),
        P("dp"),
        P("dp"),
        P("dp", None),
        P("dp"),
        P("dp", None),
        P("dp"),
        P("dp"),
        P("dp"),
    )
    return jax.shard_map(
        per_device, mesh=mesh, in_specs=in_specs, out_specs=out_specs, check_vma=False
    )
```

profile of v0, /device:TPU:0, one launch (start us, length us, event | category | flops | bytes accessed | tf_op | source)
XLA Modules:
  0.0 836.9 jit_solution(15276789739319802982)
XLA Ops:
  16.1 14.3 %all_to_all.26 = s32[32,1,8]{2,1,0:T(1,128)S(1)} all-to-all(s32[32,1,8]{2,1,0:T(1,128)S(1)} %bitcast.216), channel_id=1, replica_groups=mesh['dp'=8,'ctx'=4] {'dp','ctx'}, dimensions={0} | all-to-all | bytes 2048 | tf_op jit(solution)/shard_map/all_to_all | solution.py:81
  39.4 24.9 %all-reduce.19 = (bf16[768]{0:T(1024)(128)(2,1)S(1)}, bf16[768]{0:T(1024)(128)(2,1)S(1)}, bf16[768]{0:T(1024)(128)(2,1)S(1)}, bf16[768]{0:T(1024)(128)(2,1)S(1)}...) all-reduce(bf16[768]{0:T(1024)(128)(2,1)S(1)} %dynamic-update-slice, ...), channel_id=1, replica_groups=mesh['dp'=8,'ctx'=4] {'dp'}, use_global_device_ids=true, to_apply=%add | all-reduce | flops 6144 | bytes 24576
  83.9 9.2 %all-gather = bf16[8,1,384]{2,1,0:T(2,128)(2,1)S(1)} all-gather(bf16[1,1,384]{2,1,0:T(2,128)(2,1)S(1)} %reshape.415), channel_id=1, replica_groups=mesh['dp'=8,'ctx'=4] {'dp'}, dimensions={0}, use_global_device_ids=true | all-gather | bytes 6912 | tf_op jit(solution)/shard_map/all_gather | solution.py:131
  100.4 31.3 %all-gather.18.cloned.1.call-done = bf16[1024,768]{1,0:T(8,128)(2,1)} async-done(((bf16[256,768]{1,0:T(8,128)(2,1)}), bf16[1024,768]{1,0:T(8,128)(2,1)}) %all-gather.18.cloned.1.call-update) | async-done | bytes 1572880 | tf_op jit(solution)/shard_map/all_gather | solution.py:151
  139.2 30.5 %all-gather.12.cloned.1.call-done = bf16[1024,768]{1,0:T(8,128)(2,1)} async-done(((bf16[256,768]{1,0:T(8,128)(2,1)}), bf16[1024,768]{1,0:T(8,128)(2,1)}) %all-gather.12.cloned.1.call-update) | async-done | bytes 1572880 | tf_op jit(solution)/shard_map/all_gather | solution.py:150
  175.6 25.6 %while.30 = (s32[]{:T(128)}, f32[12,256]{1,0:T(8,128)S(1)}, f32[12,256]{1,0:T(8,128)S(1)}, f32[256,12,64]{0,2,1:T(8,128)S(1)}, s32[256]{0:T(256)S(1)}, /*index=5...) while((s32[]{:T(128)}, f32[12,256]{1,0:T(8,128)S(1)}, ...), condition=%wide.region_5.6_spmd.clone, body=%wide.region_2.5_spmd.clone.sunk | while | flops 420694016 | bytes 48307928 | solution.py:179
  178.3 3.8 fusion.139
  182.2 4.8 fusion.143
  191.2 3.8 fusion.139
  195.0 4.9 fusion.143
  205.3 30.0 %all-gather.22.cloned.1.call-done = bf16[768,3072]{1,0:T(8,128)(2,1)} async-done(((bf16[96,3072]{1,0:T(8,128)(2,1)}), bf16[768,3072]{1,0:T(8,128)(2,1)}) %all-gather.22.cloned.1.call-update) | async-done | bytes 4718608 | tf_op jit(solution)/shard_map/all_gather | solution.py:130
  235.3 11.6 %multiply_convert_fusion = (bf16[256,3072]{1,0:T(8,128)(2,1)}, f32[256,3072]{1,0:T(8,128)}, f32[256,3072]{1,0:T(8,128)}) fusion(f32[3072]{0:T(1024)S(1)} %bitcast.218, bf16[768,3072]{1,0:T(8,128)(2,1)} %all-gather.22.cloned.1.call-done, f32[256,768]{1,0:T(8,128)S(1)} %get-tuple-element.403, f32[768]{0:T(1024)S(1)} %copy-done.53, f32[768]{0:T(1024)S(1)} %copy-done.42, ...), kind=kOutput, calls=%fused_computation.69 | convolution fusion | flops 1260847104 | bytes 13389824 | tf_op jit(solution)/shard_map/dot_general | solution.py:18
  246.9 29.2 %all-gather.24.cloned.1.call-done = bf16[3072,768]{1,0:T(8,128)(2,1)} async-done(((bf16[384,768]{1,0:T(8,128)(2,1)}), bf16[3072,768]{1,0:T(8,128)(2,1)}) %all-gather.24.cloned.1.call-update) | async-done | bytes 4718608 | tf_op jit(solution)/shard_map/all_gather | solution.py:132
  276.1 4.4 fusion.76
  282.4 39.8 %all-reduce.17 = (f32[]{:T(128)}, f32[]{:T(128)}) all-reduce(f32[]{:T(128)} %get-tuple-element.394, f32[]{:T(128)} %convert_reduce_fusion.2), channel_id=1, replica_groups=mesh['dp'=8,'ctx'=4] {'dp','ctx'}, use_global_device_ids=true, to_apply=%region_12.13 | all-reduce | flops 2 | bytes 16 | tf_op jit(solution)/shard_map/psum | solution.py:202
  326.7 6.1 fusion.77
  338.6 39.9 %while.31 = (s32[]{:T(128)}, f32[256,12,64]{0,2,1:T(8,128)}, bf16[2,512,12,64]{1,3,2,0:T(8,128)(2,1)}, bf16[2,512,12,64]{1,3,2,0:T(8,128)(2,1)}, bf16[2,512,12,6...) while((s32[]{:T(128)}, f32[256,12,64]{0,2,1:T(8,128)}, ...), condition=%wide.region_21.22_spmd.clone, body=%wide.region_20.21_spmd.clone.sunk | while | flops 1023475712 | bytes 85791776 | solution.py:291
  352.8 5.4 bitcast_dynamic-update-slice_fusion.5
  372.8 5.5 bitcast_dynamic-update-slice_fusion.5
  392.1 27.5 %reduce-scatter.9.cloned.1.call-done = bf16[256,768]{0,1:T(8,128)(2,1)} async-done(((bf16[1024,768]{0,1:T(8,128)(2,1)}), bf16[256,768]{0,1:T(8,128)(2,1)}) %reduce-scatter.9.cloned.1.call-update) | async-done | bytes 393232 | tf_op jit(solution)/shard_map/reduce_scatter | solution.py:297
  422.2 33.8 %reduce-scatter.11.cloned.1.call-done = bf16[256,768]{0,1:T(8,128)(2,1)} async-done(((bf16[1024,768]{0,1:T(8,128)(2,1)}), bf16[256,768]{0,1:T(8,128)(2,1)}) %reduce-scatter.11.cloned.1.call-update) | async-done | bytes 393232 | tf_op jit(solution)/shard_map/reduce_scatter | solution.py:303
  458.6 4.4 convolution_convert_fusion.1
  475.1 21.2 %reduce-scatter.19.cloned.1.call-done = bf16[96,768]{1,0:T(8,128)(2,1)} async-done(((bf16[768,768]{1,0:T(8,128)(2,1)}), bf16[96,768]{1,0:T(8,128)(2,1)}) %reduce-scatter.19.cloned.1.call-update) | async-done | bytes 147472 | tf_op jit(solution)/shard_map/reduce_scatter | solution.py:340
  496.3 40.8 %reduce-scatter.13.cloned.1.call-done = bf16[96,768]{1,0:T(8,128)(2,1)} async-done(((bf16[768,768]{1,0:T(8,128)(2,1)}), bf16[96,768]{1,0:T(8,128)(2,1)}) %reduce-scatter.13.cloned.1.call-update) | async-done | bytes 147472 | tf_op jit(solution)/shard_map/reduce_scatter | solution.py:325
  537.1 40.6 %reduce-scatter.15.cloned.1.call-done = bf16[96,768]{1,0:T(8,128)(2,1)} async-done(((bf16[768,768]{1,0:T(8,128)(2,1)}), bf16[96,768]{1,0:T(8,128)(2,1)}) %reduce-scatter.15.cloned.1.call-update) | async-done | bytes 147472 | tf_op jit(solution)/shard_map/reduce_scatter | solution.py:331
  577.7 40.2 %reduce-scatter.17.cloned.1.call-done = bf16[96,768]{1,0:T(8,128)(2,1)} async-done(((bf16[768,768]{1,0:T(8,128)(2,1)}), bf16[96,768]{1,0:T(8,128)(2,1)}) %reduce-scatter.17.cloned.1.call-update) | async-done | bytes 147472 | tf_op jit(solution)/shard_map/reduce_scatter | solution.py:334
  617.9 57.2 %reduce-scatter.21.cloned.1.call-done = bf16[96,3072]{1,0:T(8,128)(2,1)} async-done(((bf16[768,3072]{1,0:T(8,128)(2,1)}), bf16[96,3072]{1,0:T(8,128)(2,1)}) %reduce-scatter.21.cloned.1.call-update) | async-done | bytes 589840 | tf_op jit(solution)/shard_map/reduce_scatter | solution.py:218
  675.1 57.6 %reduce-scatter.23.cloned.1.call-done = bf16[384,768]{1,0:T(8,128)(2,1)} async-done(((bf16[3072,768]{1,0:T(8,128)(2,1)}), bf16[384,768]{1,0:T(8,128)(2,1)}) %reduce-scatter.23.cloned.1.call-update) | async-done | bytes 589840 | tf_op jit(solution)/shard_map/reduce_scatter | solution.py:224
  737.8 4.6 all-to-all-start.4
  751.0 26.2 %all-reduce.18 = (bf16[768]{0:T(1024)(128)(2,1)S(1)}, bf16[768]{0:T(1024)(128)(2,1)S(1)}, bf16[768]{0:T(1024)(128)(2,1)S(1)}, bf16[768]{0:T(1024)(128)(2,1)S(1)}...) all-reduce(bf16[768]{0:T(1024)(128)(2,1)S(1)} %reduce_sum.218, ...), channel_id=5, replica_groups=mesh['dp'=8,'ctx'=4] {'dp'}, use_global_device_ids=true, to_apply=%region_27.28.clone | all-reduce | flops 9216 | bytes 36864
  777.9 11.8 %all-reduce.20 = (bf16[96]{0:T(256)(128)(2,1)S(1)}, bf16[96]{0:T(256)(128)(2,1)S(1)}, bf16[96]{0:T(256)(128)(2,1)S(1)}, bf16[96]{0:T(256)(128)(2,1)S(1)}, bf16[9...) all-reduce(bf16[96]{0:T(256)(128)(2,1)S(1)} %dynamic-slice.10, ...), channel_id=1, replica_groups=mesh['dp'=8,'ctx'=4] {'ctx'}, use_global_device_ids=true, to_apply=%region_28.29 | all-reduce | flops 1152 | bytes 4608 | tf_op jit(solution)/shard_map/psum | solution.py:355
  796.5 25.0 %all-reduce.24.cloned.1.call-done = (bf16[96,768]{1,0:T(8,128)(2,1)}, bf16[96,768]{1,0:T(8,128)(2,1)}, bf16[96,768]{1,0:T(8,128)(2,1)}, bf16[96,768]{1,0:T(8,128...) async-done(((bf16[96,768]{1,0:T(8,128)(2,1)}, bf16[96,768]{1,0:T(8,128)(2,1)}, bf16[96,768]{1,0:T(8,128)(2,1)}, bf16[96,768]{1,0:T(8,128)(2,1)}, ...) | async-done | bytes 1769488 | tf_op jit(solution)/shard_map/psum | solution.py:354
  (423 shorter events, 158.2 us)
Async XLA Ops:
  7.3 61.5 %all-gather.16.cloned.1.call-start = ((), (), s32[]{:S(2)}) async-start(), calls=%async_computation.16 | async-start | bytes 1327104 | tf_op jit(solution)/shard_map/all_gather | solution.py:124
  8.0 63.6 %all-gather.10.cloned.1.call-start = ((), (), s32[]{:S(2)}) async-start(), calls=%async_computation.13 | async-start | bytes 1327104 | tf_op jit(solution)/shard_map/all_gather | solution.py:123
  8.8 89.7 %all-gather.14.cloned.1.call-start = ((), (), s32[]{:S(2)}) async-start(), calls=%async_computation.15 | async-start | bytes 1327104 | tf_op jit(solution)/shard_map/all_gather | solution.py:121
  33.6 33.9 %all-to-all-start.1 = ((bf16[32,8,768]{2,1,0:T(8,128)(2,1)}), bf16[32,8,768]{2,1,0:T(8,128)(2,1)S(1)}, u32[]{:S(2)}, u32[]{:S(2)}) async-start(bf16[32,8,768]{2,1,0:T(8,128)(2,1)} %bitcast.2), calls=%async_computation.1 | async-start | bytes 786432 | tf_op jit(solution)/shard_map/all_to_all | solution.py:84
  36.2 95.5 %all-gather.18.cloned.1.call-start = ((), (), s32[]{:S(2)}) async-start(), calls=%async_computation.17 | async-start | bytes 1966080 | tf_op jit(solution)/shard_map/all_gather | solution.py:151
  68.8 133.5 %copy-start.12 = (bf16[256,768]{1,0:T(8,128)(2,1)}, bf16[256,768]{1,0:T(8,128)(2,1)S(1)}, u32[]{:S(2)}) copy-start(bf16[256,768]{1,0:T(8,128)(2,1)S(1)} %gather_fusion.2) | copy-start | bytes 1179652
  71.5 98.2 %all-gather.12.cloned.1.call-start = ((), (), s32[]{:S(2)}) async-start(), calls=%async_computation.14 | async-start | bytes 1966080 | tf_op jit(solution)/shard_map/all_gather | solution.py:150
  74.1 128.1 %all-gather.20.cloned.1.call-start = ((), (), s32[]{:S(2)}) async-start(), calls=%async_computation.18 | async-start | bytes 1327104 | tf_op jit(solution)/shard_map/all_gather | solution.py:126
  74.7 160.6 %all-gather.22.cloned.1.call-start = ((), (), s32[]{:S(2)}) async-start(), calls=%async_computation.19 | async-start | bytes 5308416 | tf_op jit(solution)/shard_map/all_gather | solution.py:130
  77.4 19.2 %all-to-all-start.3 = ((bf16[32,8,768]{2,1,0:T(8,128)(2,1)}), bf16[32,8,768]{2,1,0:T(8,128)(2,1)S(1)}, u32[]{:S(2)}, u32[]{:S(2)}) async-start(bf16[32,8,768]{2,1,0:T(8,128)(2,1)} %bitcast.13), calls=%async_computation.3 | async-start | bytes 786432 | tf_op jit(solution)/shard_map/all_to_all | solution.py:91
  81.2 194.9 %all-gather.24.cloned.1.call-start = ((), (), s32[]{:S(2)}) async-start(), calls=%async_computation.20 | async-start | bytes 5308416 | tf_op jit(solution)/shard_map/all_gather | solution.py:132
  81.9 337.6 %reduce-scatter.9.cloned.1.call-start = ((), (), s32[]{:S(2)}) async-start(), calls=%async_computation.21 | async-start | bytes 1966080 | tf_op jit(solution)/shard_map/reduce_scatter | solution.py:297
  204.4 130.7 %copy-start.10 = (f32[256,768]{1,0:T(8,128)}, f32[256,768]{1,0:T(8,128)S(1)}, u32[]{:S(2)}) copy-start(f32[256,768]{1,0:T(8,128)S(1)} %get-tuple-element.403) | copy-start | bytes 2359300
  204.4 71.7 %copy-start.56 = (f32[256]{0:T(256)}, f32[256]{0:T(256)S(1)}, u32[]{:S(2)}) copy-start(f32[256]{0:T(256)S(1)} %broadcast_multiply_fusion.6) | copy-start | bytes 3076
  204.6 71.5 %copy-start.63 = (f32[256]{0:T(256)}, f32[256]{0:T(256)S(1)}, u32[]{:S(2)}) copy-start(f32[256]{0:T(256)S(1)} %add_rsqrt_fusion.1) | copy-start | bytes 3076
  383.1 72.9 %reduce-scatter.11.cloned.1.call-start = ((), (), s32[]{:S(2)}) async-start(), calls=%async_computation.22 | async-start | bytes 1966080 | tf_op jit(solution)/shard_map/reduce_scatter | solution.py:303
  387.9 108.4 %reduce-scatter.19.cloned.1.call-start = ((), (), s32[]{:S(2)}) async-start(), calls=%async_computation.26 | async-start | bytes 1327104 | tf_op jit(solution)/shard_map/reduce_scatter | solution.py:340
  389.4 147.6 %reduce-scatter.13.cloned.1.call-start = ((), (), s32[]{:S(2)}) async-start(), calls=%async_computation.23 | async-start | bytes 1327104 | tf_op jit(solution)/shard_map/reduce_scatter | solution.py:325
  392.0 66.6 %copy-start.11 = (f32[256,768]{1,0:T(8,128)S(1)}, f32[256,768]{1,0:T(8,128)}, u32[]{:S(2)}) copy-start(f32[256,768]{1,0:T(8,128)} %copy-done.10) | copy-start | bytes 2359300
  392.0 66.6 %copy-start.37 = (bf16[256,3072]{1,0:T(8,128)(2,1)S(1)}, bf16[256,3072]{1,0:T(8,128)(2,1)}, u32[]{:S(2)}) copy-start(bf16[256,3072]{1,0:T(8,128)(2,1)} %copy-done.36) | copy-start | bytes 4718596
  392.0 66.6 %copy-start.44 = (f32[768]{0:T(1024)S(1)}, f32[768]{0:T(1024)}, u32[]{:S(2)}) copy-start(f32[768]{0:T(1024)} %convert_element_type.244) | copy-start | bytes 9220
  392.0 66.6 %copy-start.54 = (f32[768]{0:T(1024)S(1)}, f32[768]{0:T(1024)}, u32[]{:S(2)}) copy-start(f32[768]{0:T(1024)} %convert_element_type.245) | copy-start | bytes 9220
  392.0 185.7 %reduce-scatter.15.cloned.1.call-start = ((), (), s32[]{:S(2)}) async-start(), calls=%async_computation.24 | async-start | bytes 1327104 | tf_op jit(solution)/shard_map/reduce_scatter | solution.py:331
  422.1 195.8 %reduce-scatter.17.cloned.1.call-start = ((), (), s32[]{:S(2)}) async-start(), calls=%async_computation.25 | async-start | bytes 1327104 | tf_op jit(solution)/shard_map/reduce_scatter | solution.py:334
  458.5 216.6 %reduce-scatter.21.cloned.1.call-start = ((), (), s32[]{:S(2)}) async-start(), calls=%async_computation.27 | async-start | bytes 5308416 | tf_op jit(solution)/shard_map/reduce_scatter | solution.py:218
  463.1 269.7 %reduce-scatter.23.cloned.1.call-start = ((), (), s32[]{:S(2)}) async-start(), calls=%async_computation.28 | async-start | bytes 5308416 | tf_op jit(solution)/shard_map/reduce_scatter | solution.py:224
  469.4 263.4 %copy-start.23 = (bf16[256,12,64]{0,2,1:T(8,128)(2,1)S(1)}, bf16[256,12,64]{0,2,1:T(8,128)(2,1)}, u32[]{:S(2)}) copy-start(bf16[256,12,64]{0,2,1:T(8,128)(2,1)} %copy-done.22) | copy-start | bytes 1179652
  471.3 263.5 %copy-start.18 = (bf16[768,768]{1,0:T(8,128)(2,1)S(1)}, bf16[768,768]{1,0:T(8,128)(2,1)}, u32[]{:S(2)}) copy-start(bf16[768,768]{1,0:T(8,128)(2,1)} %all-gather.10.cloned.1.call-done) | copy-start | bytes 3538948
  471.3 263.5 %copy-start.35 = (bf16[256,768]{0,1:T(8,128)(2,1)S(1)}, bf16[256,768]{0,1:T(8,128)(2,1)}, u32[]{:S(2)}) copy-start(bf16[256,768]{0,1:T(8,128)(2,1)} %reduce-scatter.9.cloned.1.call-done) | copy-start | bytes 1179652
  471.3 266.5 %all-to-all-start.2 = ((bf16[32,8,768]{2,1,0:T(8,128)(2,1)}), bf16[32,8,768]{2,1,0:T(8,128)(2,1)S(1)}, u32[]{:S(2)}, u32[]{:S(2)}) async-start(bf16[32,8,768]{2,1,0:T(8,128)(2,1)} %bitcast.107), calls=%async_computation.2 | async-start | bytes 786432 | tf_op jit(solution)/shard_map/all_to_all | solution.py:371
  474.8 346.7 %all-reduce.24.cloned.1.call-start = ((), (), s32[]{:S(2)}) async-start(), calls=%async_computation.29 | async-start | bytes 3538944 | tf_op jit(solution)/shard_map/psum | solution.py:354
  737.8 56.7 %all-to-all-start.4 = ((bf16[32,8,768]{2,1,0:T(8,128)(2,1)}), bf16[32,8,768]{2,1,0:T(8,128)(2,1)S(1)}, u32[]{:S(2)}, u32[]{:S(2)}) async-start(bf16[32,8,768]{2,1,0:T(8,128)(2,1)} %bitcast.106), calls=%async_computation.6 | async-start | bytes 786432 | tf_op jit(solution)/shard_map/all_to_all | solution.py:378
  (94 other events, 978.8 us)
Sparse Core Ops, SparseCore 0:
  10.0 26.7 all-gather.15
  38.7 24.1 all-gather.9
  64.8 27.9 all-gather.13
  94.8 36.8 all-gather.17
  133.7 35.9 all-gather.11
  171.5 22.9 all-gather.19
  196.3 38.9 all-gather.21
  237.1 38.9 all-gather.23
  383.2 36.2 reduce-scatter.8
  421.7 34.2 reduce-scatter.10
  459.2 37.0 reduce-scatter.18
  500.3 36.7 reduce-scatter.12
  540.9 36.7 reduce-scatter.14
  581.1 36.7 reduce-scatter.16
  621.2 53.8 reduce-scatter.20
  678.8 53.8 reduce-scatter.22
  735.5 85.9 all-reduce.23
where the time goes:
time: 845 us; the launch traced here: 837 us
  waiting for transfers between devices  469 us (56%)
  blocking collectives  126 us (15%)
  matrix products  99.4 us (12%)
  local copies, waits for them, and re-layouts  54.6 us (6%)
  other arithmetic  43.8 us (5%)
  between operations  20 us (2%)
  starting transfers between devices  15.5 us (2%)
    reduce_scatter x1, waiting for transfers between devices, per_device(): lax.psum_scatter(grad_down.astype(jnp.bfloat16), 'dp', scatter_dimension=...  57.6 us
    reduce_scatter x1, waiting for transfers between devices, per_device(): lax.psum_scatter(grad_up.astype(jnp.bfloat16), 'dp', scatter_dimension=0,...  57.2 us
    unnamed x2, blocking collectives  51.2 us
    reduce_scatter x1, waiting for transfers between devices, per_device(): lax.psum_scatter(grad_query_w.astype(jnp.bfloat16), 'dp', scatter_dimensi...  40.8 us
    reduce_scatter x1, waiting for transfers between devices, per_device(): lax.psum_scatter(grad_key_w.astype(jnp.bfloat16), 'dp', scatter_dimension...  40.6 us
    reduce_scatter x1, waiting for transfers between devices, per_device(): lax.psum_scatter(grad_value_w.astype(jnp.bfloat16), 'dp', scatter_dimensi...  40.2 us
    psum x1, blocking collectives, per_device(): lax.psum(jnp.sum(valid_rows[:, None] * difference * difference), ('dp', '...  39.8 us
    reduce_scatter x1, waiting for transfers between devices, per_device(): lax.psum_scatter(value_parts.reshape(group_len, model_width).astype(jnp.b...  33.8 us
  transfers between devices with their start and end apart: 21, of which 13 were waited for; matrix products, arithmetic and copies ran while one was open for 15% of the time, Pallas kernels for 0%

commit v1 on v0

--- a/solution.py
+++ b/solution.py
@@ -1,10 +1,350 @@
+import math
 from functools import partial
-import math
-
 import jax
 import jax.numpy as jnp
 from jax import lax
+from jax.experimental import pallas as pl
+from jax.experimental.pallas import tpu as pltpu
 from jax.sharding import PartitionSpec as P
+
+MESH = pl.DeviceIdType.MESH
+F32, BF16 = jnp.float32, jnp.bfloat16
+
+
+class Place:
+    def __init__(self, z_size):
+        dp, z = lax.axis_index("dp"), lax.axis_index("ctx")
+        self.dp, self.z, self.z_size = dp, z, z_size
+        core, x, y = dp % 2, dp // 2 % 2, dp // 4
+        self.core = core
+        self.mate = {"dp": dp + 1 - 2 * core}
+        self.across = {"dp": dp + 2 - 4 * x}
+        self.along = {"dp": dp + 4 - 8 * y}
+        self.j_own = y * 2 + x
+        self.j_x = y * 2 + 1 - x
+        self.j_y = (1 - y) * 2 + x
+        self.j_d = (1 - y) * 2 + 1 - x
+
+
+def greet(place):
+    barrier = pltpu.get_barrier_semaphore()
+    for other in (place.mate, place.across, place.along):
+        pl.semaphore_signal(barrier, inc=1, device_id=other, device_id_type=MESH)
+
+    @pl.when(place.z > 0)
+    def _():
+        pl.semaphore_signal(barrier, inc=1, device_id={"ctx": place.z - 1}, device_id_type=MESH)
+
+    @pl.when(place.z < place.z_size - 1)
+    def _():
+        pl.semaphore_signal(barrier, inc=1, device_id={"ctx": place.z + 1}, device_id_type=MESH)
+
+    last = place.z_size - 1
+    neighbours = (place.z + last) // place.z_size + (2 * last - place.z) // place.z_size
+    pl.semaphore_wait(barrier, 3 + neighbours)
+
+
+def remote(src, dst, send, recv, to):
+    return pltpu.make_async_remote_copy(
+        src_ref=src, dst_ref=dst, send_sem=send, recv_sem=recv, device_id=to, device_id_type=MESH
+    )
+
+
+UNITS = 12
+BLOCK = 96
+LEFT = (0, 1, 2, 3, 4, 4, 4, 4, 5, 6, 6, 6)
+
+
+def grad_scratch(tok_rows, width):
+    unit = (UNITS, BLOCK, width)
+    half = (UNITS, BLOCK // 2, width)
+    return [
+        pltpu.VMEM((7, 4 * BLOCK, 2 * tok_rows), BF16),
+        pltpu.VMEM((UNITS, 2 * tok_rows, width), BF16),
+        pltpu.VMEM((3, 4 * BLOCK, width), F32),
+        pltpu.VMEM(unit, BF16),
+        pltpu.VMEM(unit, BF16),
+        pltpu.VMEM(unit, BF16),
+        pltpu.VMEM(half, BF16),
+        pltpu.VMEM(half, BF16),
+        pltpu.VMEM(unit, BF16),
+        pltpu.VMEM(unit, BF16),
+        pltpu.VMEM(unit, F32),
+        pltpu.VMEM((2,) + unit, BF16),
+        pltpu.VMEM((2,) + unit, BF16),
+        pltpu.SemaphoreType.DMA((UNITS, 8)),
+        pltpu.SemaphoreType.DMA((UNITS, 8)),
+        pltpu.SemaphoreType.DMA((7, 4)),
+        pltpu.SemaphoreType.DMA((7, 4)),
+        pltpu.SemaphoreType.DMA((UNITS,)),
+        pltpu.SemaphoreType.DMA((UNITS,)),
+    ]
+
+
+class Grads:
+    def __init__(self, place, scratch):
+        self.place = place
+        (
+            self.left,
+            self.right,
+            self.partial,
+            self.out_d,
+            self.out_x,
+            self.out_y,
+            self.in_dx,
+            self.in_dy,
+            self.in_x,
+            self.in_y,
+            self.total,
+            self.out_z,
+            self.in_z,
+            self.send,
+            self.recv,
+            self.left_send,
+            self.left_recv,
+            self.right_send,
+            self.right_recv,
+        ) = scratch
+        self.tok_rows = self.left.shape[2] // 2
+        half = BLOCK // 2
+        self.low, self.high = slice(0, half), slice(half, BLOCK)
+
+    def rows(self, group, j, core):
+        shard = 2 * j + core
+        if group < 4:
+            return pl.ds(pl.multiple_of(4 * BLOCK * shard + BLOCK * group, 32), BLOCK)
+        return pl.ds(pl.multiple_of(BLOCK * shard, 32), BLOCK)
+
+    def left_copy(self, group, j, source):
+        mine, theirs = self.tok_rows, 2 * self.tok_rows
+        return remote(
+            source.at[self.rows(group, j, 1 - self.place.core), :],
+            self.left.at[group, BLOCK * j : BLOCK * (j + 1), mine:theirs],
+            self.left_send.at[group, j],
+            self.left_recv.at[group, j],
+            self.place.mate,
+        )
+
+    def right_copy(self, unit, source):
+        return remote(
+            source,
+            self.right.at[unit, self.tok_rows :, :],
+            self.right_send.at[unit],
+            self.right_recv.at[unit],
+            self.place.mate,
+        )
+
+    def give_left(self, group, source):
+        for j in range(4):
+            self.left_copy(group, j, source).start()
+            self.left[group, BLOCK * j : BLOCK * (j + 1), : self.tok_rows] = source[
+                self.rows(group, j, self.place.core), :
+            ]
+
+    def give_right(self, unit, source, value):
+        self.right_copy(unit, source).start()
+        self.right[unit, : self.tok_rows, :] = value
+
+    def copy(self, unit, kind):
+        place, low, high = self.place, self.low, self.high
+        source, target, to = (
+            (self.out_d.at[unit, low], self.in_dx.at[unit], place.across),
+            (self.out_d.at[unit, high], self.in_dy.at[unit], place.along),
+            (self.out_x.at[unit, low], self.in_x.at[unit, low], place.across),
+            (self.out_x.at[unit, high], self.in_x.at[unit, high], place.across),
+            (self.out_y.at[unit, low], self.in_y.at[unit, low], place.along),
+            (self.out_y.at[unit, high], self.in_y.at[unit, high], place.along),
+            (self.out_z.at[0, unit], self.in_z.at[0, unit], {"ctx": place.z + 1}),
+            (self.out_z.at[1, unit], self.in_z.at[1, unit], {"ctx": place.z - 1}),
+        )[kind]
+        return remote(source, target, self.send.at[unit, kind], self.recv.at[unit, kind], to)
+
+    def part(self, j):
+        return pl.ds(pl.multiple_of(BLOCK * j, 32), BLOCK)
+
+    def multiply(self, unit, left_source, right_source):
+        place, low, high = self.place, self.low, self.high
+        group, slot = LEFT[unit], unit % 3
+        if group not in LEFT[:unit]:
+            for j in range(4):
+                self.left_copy(group, j, left_source).wait_recv()
+        self.right_copy(unit, right_source).wait_recv()
+        self.partial[slot] = jnp.dot(
+            self.left[group], self.right[unit], preferred_element_type=F32
+        )
+        self.out_d[unit] = self.partial[slot, self.part(place.j_d), :].astype(BF16)
+        x_part = self.partial[slot, self.part(place.j_x), :]
+        y_part = self.partial[slot, self.part(place.j_y), :]
+        self.out_x[unit, low] = x_part[low].astype(BF16)
+        self.out_y[unit, high] = y_part[high].astype(BF16)
+        for kind in (0, 1, 2, 5):
+            self.copy(unit, kind).start()
+
+    def pass_on(self, unit):
+        place, low, high = self.place, self.low, self.high
+        slot = unit % 3
+        self.copy(unit, 0).wait_recv()
+        y_part = self.partial[slot, self.part(place.j_y), :][low]
+        self.out_y[unit, low] = (y_part + self.in_dx[unit].astype(F32)).astype(BF16)
+        self.copy(unit, 1).wait_recv()
+        x_part = self.partial[slot, self.part(place.j_x), :][high]
+        self.out_x[unit, high] = (x_part + self.in_dy[unit].astype(F32)).astype(BF16)
+        self.copy(unit, 4).start()
+        self.copy(unit, 3).start()
+
+    def gather(self, unit):
+        slot = unit % 3
+        own = self.partial[slot, self.part(self.place.j_own), :]
+        for kind in (2, 3, 4, 5):
+            self.copy(unit, kind).wait_recv()
+        self.total[unit] = own + self.in_x[unit].astype(F32) + self.in_y[unit].astype(F32)
+
+    def hop(self, unit, step):
+        place = self.place
+        for way, turn in ((0, step), (1, place.z_size - 1 - step)):
+
+            @pl.when(place.z == turn)
+            def _():
+                value = self.total[unit]
+                if step > 0:
+                    self.copy(unit, 6 + way).wait_recv()
+                    value = value + self.in_z[way, unit].astype(F32)
+                self.out_z[way, unit] = value.astype(BF16)
+                self.copy(unit, 6 + way).start()
+
+    def finish(self, unit, store):
+        place = self.place
+        last = place.z_size - 1
+
+        @pl.when(place.z == last)
+        def _():
+            self.copy(unit, 6).wait_recv()
+            store(self.total[unit] + self.in_z[0, unit].astype(F32))
+
+        @pl.when(place.z == 0)
+        def _():
+            self.copy(unit, 7).wait_recv()
+            store(self.total[unit] + self.in_z[1, unit].astype(F32))
+
+        @pl.when((place.z > 0) * (place.z < last) == 1)
+        def _():
+            store(
+                self.total[unit]
+                + self.in_z[0, unit].astype(F32)
+                + self.in_z[1, unit].astype(F32)
+            )
+
+    def drain(self, lefts, rights):
+        place = self.place
+        for unit in range(UNITS):
+            for kind in range(6):
+                self.copy(unit, kind).wait_send()
+            self.right_copy(unit, rights[unit]).wait_send()
+
+        @pl.when(place.z < place.z_size - 1)
+        def _():
+            for unit in range(UNITS):
+                self.copy(unit, 6).wait_send()
+
+        @pl.when(place.z > 0)
+        def _():
+            for unit in range(UNITS):
+                self.copy(unit, 7).wait_send()
+
+        for group in range(7):
+            for j in range(4):
+                self.left_copy(group, j, lefts[group]).wait_send()
+
+
+def grad_kernel(
+    z_size,
+    act_t,
+    normed_t,
+    context_t,
+    packed_t,
+    g_ffn,
+    g_pre,
+    g_branch,
+    g_query,
+    g_key,
+    g_value,
+    d_query,
+    d_key,
+    d_value,
+    d_out,
+    d_up,
+    d_down,
+    *scratch,
+):
+    place = Place(z_size)
+    greet(place)
+    grads = Grads(place, scratch)
+    lefts = (act_t,) * 4 + (normed_t, context_t, packed_t)
+    width = packed_t.shape[0]
+    columns = [slice(width * i, width * (i + 1)) for i in range(4)]
+    rights = (
+        [g_ffn] * 4
+        + [g_pre.at[:, part] for part in columns]
+        + [g_branch, g_query, g_key, g_value]
+    )
+
+    def store(unit, value):
+        if unit < 4:
+            d_down[BLOCK * unit : BLOCK * (unit + 1), :] = value
+        elif unit < 8:
+            d_up[:, columns[unit - 4]] = value
+        else:
+            (d_out, d_query, d_key, d_value)[unit - 8][...] = value
+
+    for unit in range(UNITS):
+        if LEFT[unit] not in LEFT[:unit]:
+            grads.give_left(LEFT[unit], lefts[LEFT[unit]])
+        grads.give_right(unit, rights[unit], rights[unit][...])
+    hops = z_size - 1
+    for tick in range(UNITS + 3 + hops):
+        if tick < UNITS:
+            unit = tick
+            grads.multiply(unit, lefts[LEFT[unit]], rights[unit])
+        if 0 <= tick - 1 < UNITS:
+            grads.pass_on(tick - 1)
+        if 0 <= tick - 2 < UNITS:
+            grads.gather(tick - 2)
+        for step in range(hops):
+            unit = tick - 2 - step
+            if 0 <= unit < UNITS:
+                grads.hop(unit, step)
+        unit = tick - 2 - hops
+        if 0 <= unit < UNITS:
+            grads.finish(unit, partial(store, unit))
+    grads.drain(lefts, rights)
+
+
+def weight_grads(z_size, *sources):
+    act_t, _, _, packed_t = sources[:4]
+    width, tok_rows = packed_t.shape
+    hidden = act_t.shape[0]
+    shard = width // 8
+    square = jax.ShapeDtypeStruct((shard, width), F32)
+    vmem = pl.BlockSpec(memory_space=pltpu.VMEM)
+    return pl.pallas_call(
+        partial(grad_kernel, z_size),
+        out_shape=(
+            square,
+            square,
+            square,
+            square,
+            jax.ShapeDtypeStruct((shard, hidden), F32),
+            jax.ShapeDtypeStruct((hidden // 8, width), F32),
+        ),
+        in_specs=[vmem] * len(sources),
+        out_specs=(vmem,) * 6,
+        scratch_shapes=grad_scratch(tok_rows, width),
+        compiler_params=pltpu.CompilerParams(
+            collective_id=1, has_side_effects=True, vmem_limit_bytes=62 * 2**20
+        ),
+        name="weight_grads",
+    )(*sources)
+
 
 HEADS = 12
 
@@ -408,6 +748,346 @@
     )
 
 
+def per_device_fast(
+    tokens,
+    cotangent,
+    token_order,
+    sequence_ids,
+    valid,
+    teacher,
+    w_query,
+    b_query,
+    w_key,
+    w_value,
+    b_value,
+    w_out,
+    b_out,
+    norm1_gain,
+    norm1_bias,
+    w_up,
+    b_up,
+    w_down,
+    b_down,
+    norm2_gain,
+    norm2_bias,
+):
+    tok_rows, model_width = tokens.shape
+    peer_count = lax.axis_size(("dp", "ctx"))
+    per_peer = tok_rows // peer_count
+    head_count = HEADS
+    head_size = model_width // head_count
+    score_scale = head_size ** (-0.5)
+    gelu_exact = partial(jax.nn.gelu, approximate=False)
+    positions = lax.iota(jnp.int32, tok_rows)
+    source = token_order // tok_rows
+    slot_sort = jnp.argsort(source * tok_rows + positions)
+    requests = (token_order[slot_sort] % tok_rows).reshape(peer_count, per_peer)
+    wanted = lax.all_to_all(requests, ("dp", "ctx"), split_axis=0, concat_axis=0, tiled=True)
+    wanted_flat = wanted.reshape(tok_rows)
+    packed_x, packed_cot = (
+        lax.all_to_all(
+            tokens[wanted_flat].reshape(peer_count, per_peer, model_width),
+            ("dp", "ctx"),
+            split_axis=0,
+            concat_axis=0,
+            tiled=True,
+        ),
+        lax.all_to_all(
+            cotangent[wanted_flat].reshape(peer_count, per_peer, model_width),
+            ("dp", "ctx"),
+            split_axis=0,
+            concat_axis=0,
+            tiled=True,
+        ),
+    )
+    arrival = jnp.argsort(slot_sort)
+    inputs = packed_x.reshape(tok_rows, model_width)[arrival]
+    cot_rows = packed_cot.reshape(tok_rows, model_width)[arrival].astype(jnp.float32)
+    valid_rows = valid.astype(jnp.float32)
+    valid_count = lax.psum(jnp.sum(valid_rows), ("dp", "ctx"))
+    (
+        query_weight,
+        query_bias,
+        key_weight,
+        value_weight,
+        value_bias,
+        out_weight,
+        out_bias,
+        gain_one,
+        shift_one,
+        up_weight,
+        up_bias,
+        down_weight,
+        down_bias,
+        gain_two,
+        shift_two,
+    ) = (
+        lax.all_gather(w_query, "dp", axis=0, tiled=True),
+        lax.all_gather(b_query, "dp", axis=0, tiled=True),
+        lax.all_gather(w_key, "dp", axis=0, tiled=True),
+        lax.all_gather(w_value, "dp", axis=0, tiled=True),
+        lax.all_gather(b_value, "dp", axis=0, tiled=True),
+        lax.all_gather(w_out, "dp", axis=0, tiled=True),
+        lax.all_gather(b_out, "dp", axis=0, tiled=True),
+        lax.all_gather(norm1_gain, "dp", axis=0, tiled=True),
+        lax.all_gather(norm1_bias, "dp", axis=0, tiled=True),
+        lax.all_gather(w_up, "dp", axis=0, tiled=True),
+        lax.all_gather(b_up, "dp", axis=0, tiled=True),
+        lax.all_gather(w_down, "dp", axis=0, tiled=True),
+        lax.all_gather(b_down, "dp", axis=0, tiled=True),
+        lax.all_gather(norm2_gain, "dp", axis=0, tiled=True),
+        lax.all_gather(norm2_bias, "dp", axis=0, tiled=True),
+    )
+    queries = (product(inputs, query_weight) + query_bias).astype(jnp.bfloat16)
+    key_rows = product(inputs, key_weight).astype(jnp.bfloat16)
+    values = (product(inputs, value_weight) + value_bias).astype(jnp.bfloat16)
+    group_ids = sequence_ids.reshape(-1)
+    cycle_index = lax.axis_index("ctx")
+    query_ids = lax.dynamic_slice_in_dim(group_ids, cycle_index * tok_rows, tok_rows)
+    query_heads = queries.reshape(tok_rows, head_count, head_size)
+    initial = (
+        jnp.full((head_count, tok_rows), floor_score, jnp.float32),
+        jnp.zeros((head_count, tok_rows), jnp.float32),
+        jnp.zeros((tok_rows, head_count, head_size), jnp.float32),
+    )
+    folded = initial
+    key_piece = lax.all_gather(key_rows, "ctx", axis=0, tiled=True)
+    value_piece = lax.all_gather(values, "ctx", axis=0, tiled=True)
+    length = key_piece.shape[0]
+    attend_block_rows = math.gcd(length, 512)
+    block_count = length // attend_block_rows
+
+    def one_block(carried, inputs_block):
+        running_max, running_sum, summed = carried
+        key_block, value_block, key_start = inputs_block
+        key_ids = lax.dynamic_slice_in_dim(group_ids, key_start, attend_block_rows)
+        scores = (
+            jnp.einsum("qhd,khd->hqk", query_heads, key_block, preferred_element_type=jnp.float32)
+            * score_scale
+        )
+        scores = jnp.where((query_ids[:, None] == key_ids[None, :])[None], scores, masked_score)
+        new_max = jnp.maximum(running_max, jnp.max(scores, -1))
+        factor = jnp.exp(running_max - new_max)
+        weights = jnp.exp(scores - new_max[:, :, None])
+        running_sum = running_sum * factor + jnp.sum(weights, -1)
+        update = jnp.einsum(
+            "hqk,khd->qhd",
+            weights.astype(jnp.bfloat16),
+            value_block,
+            preferred_element_type=jnp.float32,
+        )
+        summed = summed * jnp.transpose(factor)[:, :, None] + update
+        return ((new_max, running_sum, summed), None)
+
+    key_starts = attend_block_rows * lax.iota(jnp.int32, block_count)
+    folded, _ = lax.scan(
+        one_block,
+        folded,
+        (
+            key_piece.reshape(block_count, attend_block_rows, head_count, head_size),
+            value_piece.reshape(block_count, attend_block_rows, head_count, head_size),
+            key_starts,
+        ),
+    )
+    running_max, running_sum, summed = folded
+    attended = summed / jnp.transpose(running_sum)[:, :, None]
+    log_total = running_max + jnp.log(running_sum)
+    context = attended.reshape(tok_rows, model_width).astype(jnp.bfloat16)
+    branch = product(context, out_weight) + out_bias
+    normed, scaled_one, inverse_one = layer_norm(
+        inputs.astype(jnp.float32) + branch, gain_one, shift_one
+    )
+    normed_low = normed.astype(jnp.bfloat16)
+    pre_act = product(normed_low, up_weight) + up_bias
+    activated = gelu_exact(pre_act).astype(jnp.bfloat16)
+    ffn_out = product(activated, down_weight) + down_bias
+    result, scaled_two, inverse_two = layer_norm(normed + ffn_out, gain_two, shift_two)
+    difference = result - teacher
+    loss_total = lax.psum(jnp.sum(valid_rows[:, None] * difference * difference), ("dp", "ctx"))
+    loss_value = loss_total / (valid_count * model_width)
+    grad_out = cot_rows + 2.0 / (valid_count * model_width) * valid_rows[:, None] * difference
+    grad_gain_two = jnp.sum(grad_out * scaled_two, 0)
+    grad_shift_two = jnp.sum(grad_out, 0)
+    grad_res_two = norm_back(grad_out, scaled_two, inverse_two, gain_two)
+    grad_ffn = grad_res_two.astype(jnp.bfloat16)
+    grad_down_bias = jnp.sum(grad_ffn.astype(jnp.float32), 0)
+    grad_act = against(grad_ffn, down_weight)
+    _, gelu_pull = jax.vjp(gelu_exact, pre_act)
+    grad_pre = gelu_pull(grad_act)[0].astype(jnp.bfloat16)
+    grad_up_bias = jnp.sum(grad_pre.astype(jnp.float32), 0)
+    grad_normed = grad_res_two + against(grad_pre, up_weight)
+    grad_gain_one = jnp.sum(grad_normed * scaled_one, 0)
+    grad_shift_one = jnp.sum(grad_normed, 0)
+    grad_res_one = norm_back(grad_normed, scaled_one, inverse_one, gain_one)
+    grad_branch = grad_res_one.astype(jnp.bfloat16)
+    grad_out_bias = jnp.sum(grad_branch.astype(jnp.float32), 0)
+    grad_context = against(grad_branch, out_weight).astype(jnp.bfloat16)
+    grad_heads = grad_context.reshape(tok_rows, head_count, head_size)
+    delta = jnp.transpose(jnp.sum(grad_heads.astype(jnp.float32) * attended, -1))
+    all_keys, all_values = (
+        lax.all_gather(key_rows, "ctx", axis=0, tiled=True),
+        lax.all_gather(values, "ctx", axis=0, tiled=True),
+    )
+    group_len = all_keys.shape[0]
+    block_rows = math.gcd(group_len, 512)
+    block_count = group_len // block_rows
+    key_starts = block_rows * lax.iota(jnp.int32, block_count)
+    key_blocks = all_keys.reshape(block_count, block_rows, head_count, head_size)
+    value_blocks = all_values.reshape(block_count, block_rows, head_count, head_size)
+
+    def query_side(key_block, value_block, key_start):
+        key_ids = lax.dynamic_slice_in_dim(group_ids, key_start, block_rows)
+        scores = (
+            jnp.einsum("qhd,khd->hqk", query_heads, key_block, preferred_element_type=jnp.float32)
+            * score_scale
+        )
+        scores = jnp.where((query_ids[:, None] == key_ids[None, :])[None], scores, masked_score)
+        probs = jnp.exp(scores - log_total[:, :, None])
+        grad_probs = jnp.einsum(
+            "qhd,khd->hqk", grad_heads, value_block, preferred_element_type=jnp.float32
+        )
+        grad_scores = (probs * (grad_probs - delta[:, :, None])).astype(jnp.bfloat16)
+        return (probs, grad_scores)
+
+    def back_block(grad_query, inputs_block):
+        key_block, value_block, key_start = inputs_block
+        probs, grad_scores = query_side(key_block, value_block, key_start)
+        grad_query = (
+            grad_query
+            + jnp.einsum("hqk,khd->qhd", grad_scores, key_block, preferred_element_type=jnp.float32)
+            * score_scale
+        )
+        grad_key = (
+            jnp.einsum("hqk,qhd->khd", grad_scores, query_heads, preferred_element_type=jnp.float32)
+            * score_scale
+        )
+        grad_value = jnp.einsum(
+            "hqk,qhd->khd",
+            probs.astype(jnp.bfloat16),
+            grad_heads,
+            preferred_element_type=jnp.float32,
+        )
+        return (grad_query, (grad_key, grad_value))
+
+    grad_query, (key_parts, value_parts) = lax.scan(
+        back_block,
+        jnp.zeros((tok_rows, head_count, head_size), jnp.float32),
+        (key_blocks, value_blocks, key_starts),
+    )
+    key_total, value_total = (
+        lax.psum_scatter(
+            key_parts.reshape(group_len, model_width).astype(jnp.bfloat16),
+            "ctx",
+            scatter_dimension=0,
+            tiled=True,
+        ).astype(jnp.float32),
+        lax.psum_scatter(
+            value_parts.reshape(group_len, model_width).astype(jnp.bfloat16),
+            "ctx",
+            scatter_dimension=0,
+            tiled=True,
+        ).astype(jnp.float32),
+    )
+    grad_keys = key_total.astype(jnp.bfloat16)
+    grad_values = value_total.astype(jnp.bfloat16)
+    grad_queries = grad_query.reshape(tok_rows, model_width).astype(jnp.bfloat16)
+    grad_query_bias = jnp.sum(grad_queries.astype(jnp.float32), 0)
+    grad_value_bias = jnp.sum(grad_values.astype(jnp.float32), 0)
+    grad_inputs = (
+        grad_res_one
+        + against(grad_queries, query_weight)
+        + against(grad_keys, key_weight)
+        + against(grad_values, value_weight)
+    )
+    grad_query_w, grad_key_w, grad_value_w, grad_out_w, grad_up, grad_down = weight_grads(
+        lax.axis_size("ctx"),
+        activated.T,
+        normed_low.T,
+        context.T,
+        inputs.T,
+        grad_ffn,
+        grad_pre,
+        grad_branch,
+        grad_queries,
+        grad_keys,
+        grad_values,
+    )
+    small = jnp.stack(
+        [
+            grad_query_bias,
+            grad_value_bias,
+            grad_out_bias,
+            grad_gain_one,
+            grad_shift_one,
+            grad_down_bias,
+            grad_gain_two,
+            grad_shift_two,
+        ]
+        + list(grad_up_bias.reshape(4, model_width))
+    )
+    small = lax.psum(small, ("dp", "ctx"))
+    shard = model_width // 8
+    dp_index = lax.axis_index("dp")
+    own = lax.dynamic_slice_in_dim(small[:8], dp_index * shard, shard, axis=1)
+    own_up = lax.dynamic_slice_in_dim(small[8:].reshape(-1), dp_index * 4 * shard, 4 * shard)
+    totals = (
+        grad_query_w,
+        own[0],
+        grad_key_w,
+        grad_value_w,
+        own[1],
+        grad_out_w,
+        own[2],
+        own[3],
+        own[4],
+        grad_up,
+        own_up,
+        grad_down,
+        own[5],
+        own[6],
+        own[7],
+    )
+    back_out, back_grad = (
+        lax.all_to_all(
+            result[slot_sort].reshape(peer_count, per_peer, model_width).astype(jnp.bfloat16),
+            ("dp", "ctx"),
+            split_axis=0,
+            concat_axis=0,
+            tiled=True,
+        ).astype(jnp.float32),
+        lax.all_to_all(
+            grad_inputs[slot_sort].reshape(peer_count, per_peer, model_width).astype(jnp.bfloat16),
+            ("dp", "ctx"),
+            split_axis=0,
+            concat_axis=0,
+            tiled=True,
+        ).astype(jnp.float32),
+    )
+    homeward = jnp.argsort(wanted_flat)
+    output = back_out.reshape(tok_rows, model_width)[homeward]
+    input_grad = back_grad.reshape(tok_rows, model_width)[homeward]
+    return (
+        output,
+        loss_value,
+        input_grad,
+        totals[0],
+        totals[1],
+        totals[2],
+        totals[3],
+        totals[4],
+        totals[5],
+        totals[6],
+        totals[7],
+        totals[8],
+        totals[9],
+        totals[10],
+        totals[11],
+        totals[12],
+        totals[13],
+        totals[14],
+    )
+
+
 def solution(mesh):
     in_specs = (
         P(("dp", "ctx"), None),
@@ -452,6 +1132,7 @@
         P("dp"),
         P("dp"),
     )
+    fast = dict(mesh.shape) == {"dp": 8, "ctx": 4}
     return jax.shard_map(
-        per_device, mesh=mesh, in_specs=in_specs, out_specs=out_specs, check_vma=False
-    )
+        per_device_fast if fast else per_device, mesh=mesh, in_specs=in_specs, out_specs=out_specs, check_vma=False
+    )

time: 845 us -> 590 us (0.70)
  waiting for transfers between devices: 469 us -> 129 us
  Pallas kernels: 0 us -> 88.6 us
  matrix products: 99.4 us -> 87.4 us
    reduce_scatter x8 -> x2, waiting for transfers between devices: 319 us -> 49.7 us  [the longest x1 35 us: per_device_fast(): lax.psum_scatter(value_parts.reshape(group_len, model_width).astype(jnp.b...]
    pallas_call x0 -> x1, Pallas kernels: none -> 88.6 us  [weight_grads(): pl.pallas_call(partial(grad_kernel, z_size), out_shape=(square, square, s...]
    all_gather x8, waiting for transfers between devices: 121 us -> 75.8 us  [the longest x1 29 us: per_device_fast(): lax.all_gather(w_down, 'dp', axis=0, tiled=True)]
    psum x2, blocking collectives: 51.6 us -> 83.5 us  [the longest x1 42.3 us: per_device_fast(): valid_count = lax.psum(jnp.sum(valid_rows), ('dp', 'ctx'))]
    unnamed x2 -> x1, blocking collectives: 51.2 us -> 24.9 us
    psum x1 -> x0, waiting for transfers between devices: 25 us -> none  [per_device(): lax.psum(attn_shards[0].astype(jnp.bfloat16), 'ctx').astype(jnp.float32)]
    dot_general x6 -> x0, matrix products: 16.1 us -> none  [inner_rows(): lax.dot_general(left, right, (((0,), (0,)), ((), ())), preferred_element_...]
    gather x10 -> x11, local copies, waits for them, and re-layouts: 16.8 us -> 17.7 us  [the longest x2 2.11 us: per_device_fast(): inputs = packed_x.reshape(tok_rows, model_width)[arrival]]
  transfers between devices with their start and end apart: 21 -> 14, of which waited for: 13 -> 5; matrix products, arithmetic and copies ran while one was open for 15% -> 21% of each run, Pallas kernels for 0% -> 15%
where the time goes in v1:
time: 590 us; the launch traced here: 582 us
  blocking collectives  133 us (23%)
  waiting for transfers between devices  129 us (22%)
  Pallas kernels  88.6 us (15%)
  matrix products  87.4 us (15%)
  local copies, waits for them, and re-layouts  63 us (11%)
  other arithmetic  38.8 us (7%)
  between operations  18.9 us (3%)
  starting transfers between devices  15.1 us (3%)
  loops' own time  8.29 us (1%)
    pallas_call x1, Pallas kernels, weight_grads(): pl.pallas_call(partial(grad_kernel, z_size), out_shape=(square, square, s...  88.6 us
    psum x1, blocking collectives, per_device_fast(): valid_count = lax.psum(jnp.sum(valid_rows), ('dp', 'ctx'))  42.3 us
    psum x1, blocking collectives, per_device_fast(): lax.psum(jnp.sum(valid_rows[:, None] * difference * difference), ('dp', '...  41.1 us
    reduce_scatter x1, waiting for transfers between devices, per_device_fast(): lax.psum_scatter(value_parts.reshape(group_len, model_width).astype(jnp.b...  35 us
    all_gather x1, waiting for transfers between devices, per_device_fast(): lax.all_gather(w_down, 'dp', axis=0, tiled=True)  29 us
    dot_general x6, matrix products, product(): return jnp.dot(left, right, preferred_element_type=jnp.float32)  27.5 us
    all_gather x1, waiting for transfers between devices, per_device_fast(): lax.all_gather(w_up, 'dp', axis=0, tiled=True)  27.3 us
    unnamed x1, blocking collectives  24.9 us
  transfers between devices with their start and end apart: 14, of which 5 were waited for; matrix products, arithmetic and copies ran while one was open for 21% of the time, Pallas kernels for 15%

profile of v1, /device:TPU:0, one launch (start us, length us, event | category | flops | bytes accessed | tf_op | source)
XLA Modules:
  0.0 581.7 jit_solution(3040370538147429422)
XLA Ops:
  10.2 3.2 sort.45
  16.1 14.3 %all_to_all.26 = s32[32,1,8]{2,1,0:T(1,128)S(1)} all-to-all(s32[32,1,8]{2,1,0:T(1,128)S(1)} %bitcast.301), channel_id=1, replica_groups=mesh['dp'=8,'ctx'=4] {'dp','ctx'}, dimensions={0} | all-to-all | bytes 2048 | tf_op jit(solution)/shard_map/all_to_all | solution.py:785
  39.4 24.9 %all-reduce.9 = (bf16[768]{0:T(1024)(128)(2,1)S(1)}, bf16[768]{0:T(1024)(128)(2,1)S(1)}, bf16[768]{0:T(1024)(128)(2,1)S(1)}, bf16[768]{0:T(1024)(128)(2,1)S(1)},...) all-reduce(bf16[768]{0:T(1024)(128)(2,1)S(1)} %dynamic-update-slice, ...), channel_id=1, replica_groups=mesh['dp'=8,'ctx'=4] {'dp'}, use_global_device_ids=true, to_apply=%add | all-reduce | flops 6144 | bytes 24576
  64.4 3.2 sort.46
  77.4 3.8 all-to-all-start.3
  82.0 42.3 %psum.22 = f32[]{:T(128)} all-reduce(f32[]{:T(128)} %convert_reduce_fusion.5), channel_id=1, replica_groups=mesh['dp'=8,'ctx'=4] {'dp','ctx'}, use_global_device_ids=true, to_apply=%region_14.15 | all-reduce | flops 1 | bytes 8 | tf_op jit(solution)/shard_map/psum | solution.py:807
  127.9 9.8 %all-gather = bf16[8,1,384]{2,1,0:T(2,128)(2,1)S(1)} all-gather(bf16[1,1,384]{2,1,0:T(2,128)(2,1)S(1)} %reshape.425), channel_id=1, replica_groups=mesh['dp'=8,'ctx'=4] {'dp'}, dimensions={0}, use_global_device_ids=true | all-gather | bytes 6912 | tf_op jit(solution)/shard_map/all_gather | solution.py:835
  151.3 19.5 %all-gather.12.cloned.1.call-done = bf16[1024,768]{1,0:T(8,128)(2,1)} async-done(((bf16[256,768]{1,0:T(8,128)(2,1)}), bf16[1024,768]{1,0:T(8,128)(2,1)}) %all-gather.12.cloned.1.call-update) | async-done | bytes 1572880 | tf_op jit(solution)/shard_map/all_gather | solution.py:854
  176.6 27.3 %while.30 = (s32[]{:T(128)}, f32[12,256]{1,0:T(8,128)S(1)}, f32[12,256]{1,0:T(8,128)S(1)}, f32[256,12,64]{0,2,1:T(8,128)}, s32[256]{0:T(256)S(1)}, /*index=5*/s3...) while((s32[]{:T(128)}, f32[12,256]{1,0:T(8,128)S(1)}, ...), condition=%wide.region_5.6_spmd.clone, body=%wide.region_2.5_spmd.clone.sunk | while | flops 420694016 | bytes 48307928 | solution.py:883
  179.4 3.8 fusion.149
  183.2 5.7 fusion.153
  193.0 3.8 fusion.149
  196.8 5.8 fusion.153
  209.1 27.3 %all-gather.22.cloned.1.call-done = bf16[768,3072]{1,0:T(8,128)(2,1)} async-done(((bf16[96,3072]{1,0:T(8,128)(2,1)}), bf16[768,3072]{1,0:T(8,128)(2,1)}) %all-gather.22.cloned.1.call-update) | async-done | bytes 4718608 | tf_op jit(solution)/shard_map/all_gather | solution.py:834
  236.4 11.8 %fusion.49 = (f32[256,3072]{1,0:T(8,128)}, f32[256,3072]{1,0:T(8,128)}) fusion(f32[3072]{0:T(1024)} %bitcast.303, bf16[768,3072]{1,0:T(8,128)(2,1)} %all-gather.22.cloned.1.call-done, f32[256,768]{1,0:T(8,128)S(1)} %get-tuple-element.388, f32[768]{0:T(1024)} %convert_element_type.153, f32[768]{0:T(1024)} %convert_element_type.152, ...), kind=kOutput, calls=%fused_computation.66 | convolution fusion | flops 1258487808 | bytes 11816960 | tf_op jit(solution)/shard_map/dot_general | solution.py:358
  248.2 29.0 %all-gather.24.cloned.1.call-done = bf16[3072,768]{1,0:T(8,128)(2,1)} async-done(((bf16[384,768]{1,0:T(8,128)(2,1)}), bf16[3072,768]{1,0:T(8,128)(2,1)}) %all-gather.24.cloned.1.call-update) | async-done | bytes 4718608 | tf_op jit(solution)/shard_map/all_gather | solution.py:836
  277.3 5.9 %fusion.95 = (f32[256]{0:T(256)S(1)}, f32[256,768]{1,0:T(8,128)S(1)}) fusion(f32[768]{0:T(1024)S(1)} %copy-done.61, bf16[3072,768]{1,0:T(8,128)(2,1)} %all-gather.24.cloned.1.call-done, f32[256,3072]{1,0:T(8,128)} %get-tuple-element.404, f32[256,3072]{1,0:T(8,128)} %get-tuple-element.405, f32[768]{0:T(1024)S(1)} %copy-done.48, f32[768]{0:T(1024)S(1)} %copy-done.45, ...), kind=kOutput, calls=%fused_computation.201 | convolution fusion | flops 1211694848 | bytes 12595200 | tf_op jit(solution)/shard_map/dot_general | solution.py:358
  296.4 40.1 %while.31 = (s32[]{:T(128)}, f32[256,12,64]{0,2,1:T(8,128)}, bf16[2,512,12,64]{1,3,2,0:T(8,128)(2,1)}, bf16[2,512,12,64]{1,3,2,0:T(8,128)(2,1)}, bf16[2,512,12,6...) while((s32[]{:T(128)}, f32[256,12,64]{0,2,1:T(8,128)}, ...), condition=%wide.region_21.22_spmd.clone, body=%wide.region_20.21_spmd.clone.sunk | while | flops 1023475712 | bytes 85791776 | solution.py:972
  302.9 3.4 fusion.165
  311.0 5.4 bitcast_dynamic-update-slice_fusion.5
  322.8 3.4 fusion.165
  331.1 5.4 bitcast_dynamic-update-slice_fusion.5
  336.5 3.0 copy.90
  341.7 3.2 sort.47
  344.9 3.0 copy.92
  354.2 4.7 all-to-all-start.2
  359.2 8.0 %fusion.52 = bf16[3072,256]{0,1:T(8,128)(2,1)S(1)} fusion(f32[256,3072]{1,0:T(8,128)} %get-tuple-element.405), kind=kLoop, calls=%fused_computation.69 | loop fusion | flops 51118080 | bytes 4718592 | tf_op jit(solution)/shard_map/convert_element_type | solution.py:902
  368.6 14.8 %reduce-scatter.3.cloned.1.call-done.g_key = bf16[256,768]{1,0:T(8,128)(2,1)} async-done(((bf16[1024,768]{1,0:T(8,128)(2,1)}), bf16[256,768]{1,0:T(8,128)(2,1)}) %reduce-scatter.3.cloned.1.call-update) | async-done | bytes 393232 | tf_op jit(solution)/shard_map/reduce_scatter | solution.py:978
  386.0 35.0 %reduce-scatter.5.cloned.1.call-done.g_value = bf16[256,768]{1,0:T(8,128)(2,1)} async-done(((bf16[1024,768]{1,0:T(8,128)(2,1)}), bf16[256,768]{1,0:T(8,128)(2,1)}) %reduce-scatter.5.cloned.1.call-update) | async-done | bytes 393232 | tf_op jit(solution)/shard_map/reduce_scatter | solution.py:984
  425.1 3.6 all-to-all-start.4
  434.6 41.1 %all-reduce.8 = (f32[]{:T(128)}, f32[12,768]{1,0:T(8,128)S(1)}) all-reduce(f32[]{:T(128)} %get-tuple-element.409, f32[12,768]{1,0:T(8,128)S(1)} %stack.35), channel_id=1, replica_groups=mesh['dp'=8,'ctx'=4] {'dp','ctx'}, use_global_device_ids=true, to_apply=%region_12.13 | all-reduce | flops 9217 | bytes 73736 | tf_op jit(solution)/shard_map/psum | solution.py:906
  475.8 88.6 %weight_grads.1 = (f32[96,768]{1,0:T(8,128)}, f32[96,768]{1,0:T(8,128)}, f32[96,768]{1,0:T(8,128)}, f32[96,768]{1,0:T(8,128)}, f32[96,3072]{1,0:T(8,128)}, /*index=5*/f32[384,768]{1,0:T(8,128)}) custom-call(bf16[3072,256]{1,0:T(8,128)(2,1)} %copy.94.act_t, bf16[768,256]{1,0:T(8,128)(2,1)} %copy.95.normed_t, bf16[768,256]{1,0:T(8,128)(2,1)} %bitcast.290, ...), custom_call_target="tpu_custom_call" | custom-call | tf_op jit(solution)/shard_map/weight_grads/pallas_call | solution.py:329
  (394 shorter events, 117.8 us)
Async XLA Ops:
  7.2 30.6 %copy-start.74 = (bf16[96]{0:T(256)(128)(2,1)S(1)}, bf16[96]{0:T(256)(128)(2,1)}, u32[]{:S(2)}) copy-start(bf16[96]{0:T(256)(128)(2,1)} %param.35) | copy-start | bytes 580
  7.2 30.8 %copy-start.75 = (bf16[96]{0:T(256)(128)(2,1)S(1)}, bf16[96]{0:T(256)(128)(2,1)}, u32[]{:S(2)}) copy-start(bf16[96]{0:T(256)(128)(2,1)} %param.37) | copy-start | bytes 580
  7.3 31.0 %copy-start.76 = (bf16[96]{0:T(256)(128)(2,1)S(1)}, bf16[96]{0:T(256)(128)(2,1)}, u32[]{:S(2)}) copy-start(bf16[96]{0:T(256)(128)(2,1)} %param.38) | copy-start | bytes 580
  7.3 31.2 %copy-start.77 = (bf16[96]{0:T(256)(128)(2,1)S(1)}, bf16[96]{0:T(256)(128)(2,1)}, u32[]{:S(2)}) copy-start(bf16[96]{0:T(256)(128)(2,1)} %param.39) | copy-start | bytes 580
  7.3 31.5 %copy-start.78 = (bf16[96]{0:T(256)(128)(2,1)S(1)}, bf16[96]{0:T(256)(128)(2,1)}, u32[]{:S(2)}) copy-start(bf16[96]{0:T(256)(128)(2,1)} %param.43) | copy-start | bytes 580
  7.3 31.7 %copy-start.79 = (bf16[96]{0:T(256)(128)(2,1)S(1)}, bf16[96]{0:T(256)(128)(2,1)}, u32[]{:S(2)}) copy-start(bf16[96]{0:T(256)(128)(2,1)} %param.44) | copy-start | bytes 580
  7.3 31.9 %copy-start.80 = (bf16[96]{0:T(256)(128)(2,1)S(1)}, bf16[96]{0:T(256)(128)(2,1)}, u32[]{:S(2)}) copy-start(bf16[96]{0:T(256)(128)(2,1)} %param.45) | copy-start | bytes 580
  7.3 61.5 %all-gather.16.cloned.1.call-start = ((), (), s32[]{:S(2)}) async-start(), calls=%async_computation.10 | async-start | bytes 1327104 | tf_op jit(solution)/shard_map/all_gather | solution.py:828
  8.0 63.5 %all-gather.10.cloned.1.call-start = ((), (), s32[]{:S(2)}) async-start(), calls=%async_computation.7 | async-start | bytes 1327104 | tf_op jit(solution)/shard_map/all_gather | solution.py:827
  8.8 133.3 %all-gather.14.cloned.1.call-start = ((), (), s32[]{:S(2)}) async-start(), calls=%async_computation.9 | async-start | bytes 1327104 | tf_op jit(solution)/shard_map/all_gather | solution.py:825
  30.4 38.4 %copy-start.41 = (s32[32,1,8]{2,1,0:T(1,128)}, s32[32,1,8]{2,1,0:T(1,128)S(1)}, u32[]{:S(2)}) copy-start(s32[32,1,8]{2,1,0:T(1,128)S(1)} %all_to_all.26) | copy-start | bytes 3076
  33.6 33.9 %all-to-all-start.1 = ((bf16[32,8,768]{2,1,0:T(8,128)(2,1)}), bf16[32,8,768]{2,1,0:T(8,128)(2,1)S(1)}, u32[]{:S(2)}, u32[]{:S(2)}) async-start(bf16[32,8,768]{2,1,0:T(8,128)(2,1)} %bitcast.2), calls=%async_computation.1 | async-start | bytes 786432 | tf_op jit(solution)/shard_map/all_to_all | solution.py:788
  36.2 107.9 %all-gather.18.cloned.1.call-start = ((), (), s32[]{:S(2)}) async-start(), calls=%async_computation.11 | async-start | bytes 1966080 | tf_op jit(solution)/shard_map/all_gather | solution.py:855
  68.8 136.5 %copy-start.11 = (bf16[256,768]{1,0:T(8,128)(2,1)}, bf16[256,768]{1,0:T(8,128)(2,1)S(1)}, u32[]{:S(2)}) copy-start(bf16[256,768]{1,0:T(8,128)(2,1)S(1)} %gather_fusion.2) | copy-start | bytes 1179652
  71.5 99.3 %all-gather.12.cloned.1.call-start = ((), (), s32[]{:S(2)}) async-start(), calls=%async_computation.8 | async-start | bytes 1966080 | tf_op jit(solution)/shard_map/all_gather | solution.py:854
  74.1 53.8 %copy-start.72 = (bf16[384]{0:T(512)(128)(2,1)S(1)}, bf16[384]{0:T(512)(128)(2,1)}, u32[]{:S(2)}) copy-start(bf16[384]{0:T(512)(128)(2,1)} %param.41) | copy-start | bytes 2308
  74.1 66.1 %copy-start.44 = (s32[1,1024]{1,0:T(1,128)S(1)}, s32[1,1024]{1,0:T(1,128)}, u32[]{:S(2)}) copy-start(s32[1,1024]{1,0:T(1,128)} %param.28) | copy-start | bytes 12292
  74.1 131.1 %all-gather.20.cloned.1.call-start = ((), (), s32[]{:S(2)}) async-start(), calls=%async_computation.12 | async-start | bytes 1327104 | tf_op jit(solution)/shard_map/all_gather | solution.py:830
  74.7 161.6 %all-gather.22.cloned.1.call-start = ((), (), s32[]{:S(2)}) async-start(), calls=%async_computation.13 | async-start | bytes 5308416 | tf_op jit(solution)/shard_map/all_gather | solution.py:834
  77.4 62.8 %all-to-all-start.3 = ((bf16[32,8,768]{2,1,0:T(8,128)(2,1)}), bf16[32,8,768]{2,1,0:T(8,128)(2,1)S(1)}, u32[]{:S(2)}, u32[]{:S(2)}) async-start(bf16[32,8,768]{2,1,0:T(8,128)(2,1)} %bitcast.13), calls=%async_computation.3 | async-start | bytes 786432 | tf_op jit(solution)/shard_map/all_to_all | solution.py:795
  81.2 196.0 %all-gather.24.cloned.1.call-start = ((), (), s32[]{:S(2)}) async-start(), calls=%async_computation.14 | async-start | bytes 5308416 | tf_op jit(solution)/shard_map/all_gather | solution.py:836
  81.9 301.4 %reduce-scatter.3.cloned.1.call-start = ((), (), s32[]{:S(2)}) async-start(), calls=%async_computation.15 | async-start | bytes 1966080 | tf_op jit(solution)/shard_map/reduce_scatter | solution.py:978
  205.2 43.0 %copy-start.15 = (bf16[256,12,64]{0,2,1:T(8,128)(2,1)}, bf16[256,12,64]{0,2,1:T(8,128)(2,1)S(1)}, u32[]{:S(2)}) copy-start(bf16[256,12,64]{0,2,1:T(8,128)(2,1)S(1)} %fusion.90) | copy-start | bytes 1179652
  208.2 81.2 %copy-start.51 = (f32[256]{0:T(256)}, f32[256]{0:T(256)S(1)}, u32[]{:S(2)}) copy-start(f32[256]{0:T(256)S(1)} %broadcast_multiply_fusion.6) | copy-start | bytes 3076
  208.4 81.0 %copy-start.55 = (f32[256]{0:T(256)}, f32[256]{0:T(256)S(1)}, u32[]{:S(2)}) copy-start(f32[256]{0:T(256)S(1)} %add_rsqrt_fusion.1) | copy-start | bytes 3076
  236.3 40.8 %copy-start.45 = (f32[768]{0:T(1024)S(1)}, f32[768]{0:T(1024)}, u32[]{:S(2)}) copy-start(f32[768]{0:T(1024)} %convert_element_type.152) | copy-start | bytes 9220
  236.3 40.8 %copy-start.48 = (f32[768]{0:T(1024)S(1)}, f32[768]{0:T(1024)}, u32[]{:S(2)}) copy-start(f32[768]{0:T(1024)} %convert_element_type.153) | copy-start | bytes 9220
  236.4 40.8 %copy-start.61 = (f32[768]{0:T(1024)S(1)}, f32[768]{0:T(1024)}, u32[]{:S(2)}) copy-start(f32[768]{0:T(1024)} %convert_element_type.157) | copy-start | bytes 9220
  341.6 79.4 %reduce-scatter.5.cloned.1.call-start = ((), (), s32[]{:S(2)}) async-start(), calls=%async_computation.16 | async-start | bytes 1966080 | tf_op jit(solution)/shard_map/reduce_scatter | solution.py:984
  354.2 70.9 %all-to-all-start.2 = ((bf16[32,8,768]{2,1,0:T(8,128)(2,1)}), bf16[32,8,768]{2,1,0:T(8,128)(2,1)}, u32[]{:S(2)}, u32[]{:S(2)}) async-start(bf16[32,8,768]{2,1,0:T(8,128)(2,1)} %bitcast.197), calls=%async_computation.2 | async-start | bytes 786432 | tf_op jit(solution)/shard_map/all_to_all | solution.py:1051
  386.0 42.7 %copy-start.53 = (f32[3072]{0:T(1024)S(1)}, f32[3072]{0:T(1024)}, u32[]{:S(2)}) copy-start(f32[3072]{0:T(1024)} %get-tuple-element.375) | copy-start | bytes 36868
  425.1 141.3 %all-to-all-start.4 = ((bf16[32,8,768]{2,1,0:T(8,128)(2,1)}), bf16[32,8,768]{2,1,0:T(8,128)(2,1)S(1)}, u32[]{:S(2)}, u32[]{:S(2)}) async-start(bf16[32,8,768]{2,1,0:T(8,128)(2,1)} %bitcast.196), calls=%async_computation.6 | async-start | bytes 786432 | tf_op jit(solution)/shard_map/all_to_all | solution.py:1058
  (81 other events, 416.2 us)
Sparse Core Ops, SparseCore 0:
  10.0 26.7 all-gather.15
  38.7 24.1 all-gather.9
  64.8 28.2 all-gather.13
  95.1 37.6 all-gather.17
  134.8 35.9 all-gather.11
  172.5 22.9 all-gather.19
  197.4 38.9 all-gather.21
  238.2 38.9 all-gather.23
  341.7 41.6 reduce-scatter.2
  385.5 35.4 reduce-scatter.4

commit v2 on v0

--- a/solution.py
+++ b/solution.py
@@ -1,12 +1,1255 @@
+import math
 from functools import partial
-import math
+from types import SimpleNamespace
+from typing import NamedTuple
 
 import jax
 import jax.numpy as jnp
 from jax import lax
+from jax.experimental import pallas as pl
+from jax.experimental.pallas import tpu as pltpu
 from jax.sharding import PartitionSpec as P
 
+MESH = pl.DeviceIdType.MESH
+F32, BF16 = jnp.float32, jnp.bfloat16
+
+
+class Place:
+    def __init__(self, z_size):
+        dp, z = lax.axis_index("dp"), lax.axis_index("ctx")
+        self.dp, self.z, self.z_size = dp, z, z_size
+        core, x, y = dp % 2, dp // 2 % 2, dp // 4
+        self.core = core
+        self.mate = {"dp": dp + 1 - 2 * core}
+        self.across = {"dp": dp + 2 - 4 * x}
+        self.along = {"dp": dp + 4 - 8 * y}
+        self.j_own = y * 2 + x
+        self.j_x = y * 2 + 1 - x
+        self.j_y = (1 - y) * 2 + x
+        self.j_d = (1 - y) * 2 + 1 - x
+
+
+def remote(src, dst, send, recv, to):
+    return pltpu.make_async_remote_copy(
+        src_ref=src, dst_ref=dst, send_sem=send, recv_sem=recv, device_id=to, device_id_type=MESH
+    )
+
+
+UNITS = 12
+BLOCK = 96
+
+
+class Route:
+    def __init__(self, z_size):
+        place = Place(z_size)
+        self.place = place
+        dp, z, core = place.dp, place.z, place.core
+        self.blocks = 8 * z_size
+        self.home = dp * z_size + z
+        self.group_core = z // 2
+        self.quarter = 2 * (z % 2) + core
+        self.block = (dp - core + self.group_core) * z_size + self.quarter
+        self.mate_quarter = self.quarter + 1 - 2 * core
+        self.pair_quarter = self.quarter + 2 - 4 * (z % 2)
+        self.far_quarter = self.pair_quarter + 1 - 2 * core
+        self.pair = {"ctx": z + 1 - 2 * (z % 2)}
+
+    def worker(self, block):
+        group, quarter = block // self.place.z_size, block % self.place.z_size
+        return {"dp": group - group % 2 + quarter % 2, "ctx": 2 * (group % 2) + quarter // 2}
+
+    def owner(self, block):
+        return {"dp": block // self.place.z_size, "ctx": block % self.place.z_size}
+
+    def greet_all(self):
+        barrier = pltpu.get_barrier_semaphore()
+
+        def signal(step, carry):
+            other = (self.home + step) % self.blocks
+            pl.semaphore_signal(
+                barrier, inc=1, device_id=self.owner(other), device_id_type=MESH
+            )
+            return carry
+
+        lax.fori_loop(1, self.blocks, signal, 0)
+        pl.semaphore_wait(barrier, self.blocks - 1)
+
+
+def shard_rows(unit, shard, width):
+    start = width * unit + BLOCK * shard
+    start = start + unit // 8 * (3 * BLOCK * shard - (width - BLOCK) * (unit - 8))
+    return pl.multiple_of(start, 32)
+
+
+class Weights:
+    def __init__(self, place, full, send, recv):
+        self.place, self.full, self.send, self.recv = place, full, send, recv
+        self.width = full.shape[1]
+
+    def at(self, unit, shard, first=0, count=BLOCK):
+        start = shard_rows(unit, shard, self.width)
+        return self.full.at[pl.ds(pl.multiple_of(start + first, 16), count), :]
+
+    def copy(self, unit, kind, arriving):
+        place = self.place
+        own, across, along = place.dp, place.across["dp"], place.along["dp"]
+        corner = across + along - own
+        half = BLOCK // 2
+        mate = place.mate["dp"] - own
+        shard, first, count, to = (
+            (own, 0, BLOCK, place.across),
+            (own, 0, BLOCK, place.along),
+            (own, 0, BLOCK, place.mate),
+            (across, 0, half, place.along),
+            (along, half, half, place.across),
+            (across, 0, BLOCK, place.mate),
+            (along, 0, BLOCK, place.mate),
+            (corner, 0, BLOCK, place.mate),
+        )[kind]
+        if arriving:
+            shard = (across, along, own + mate, corner, corner, across + mate, along + mate, corner + mate)[kind]
+        ref = self.at(unit, shard, first, count)
+        return remote(ref, ref, self.send.at[unit, kind], self.recv.at[unit, kind], to)
+
+    def begin(self, unit):
+        for kind in (0, 1, 2):
+            self.copy(unit, kind, False).start()
+
+    def pass_on(self, unit):
+        self.copy(unit, 0, True).wait_recv()
+        self.copy(unit, 3, False).start()
+        self.copy(unit, 5, False).start()
+        self.copy(unit, 1, True).wait_recv()
+        self.copy(unit, 4, False).start()
+        self.copy(unit, 6, False).start()
+
+    def corner(self, unit):
+        self.copy(unit, 3, True).wait_recv()
+        self.copy(unit, 4, True).wait_recv()
+        self.copy(unit, 7, False).start()
+
+    def tick(self, step):
+        self.begin(step)
+        self.pass_on(step - 2)
+        if not isinstance(step, int) or step >= 3:
+            self.corner(step - 3)
+
+    def ready(self, unit):
+        for kind in (2, 5, 6, 7):
+            self.copy(unit, kind, True).wait_recv()
+
+    def drain(self):
+        def one(unit, carry):
+            for kind in range(8):
+                self.copy(unit, kind, False).wait_send()
+            return carry
+
+        lax.fori_loop(0, UNITS, one, 0)
+
+
+def iota(shape, axis):
+    return lax.broadcasted_iota(jnp.int32, shape, axis)
+
+
+def column(row):
+    n = row.shape[1]
+    return jnp.sum(jnp.where(iota((n, n), 0) == iota((n, n), 1), row, 0.0), 1, keepdims=True)
+
+
+def dot(left, right):
+    return jnp.dot(left, right, preferred_element_type=F32)
+
+
+def dot_nt(left, right):
+    return lax.dot_general(
+        left, right, (((1,), (1,)), ((), ())), preferred_element_type=F32
+    )
+
+
+def one_hot(condition):
+    return jnp.where(condition, 1.0, 0.0).astype(BF16)
+
+
+FORWARD_SCRATCH = dict(
+    ints=lambda t, w, b: pltpu.VMEM((b, 2, t), jnp.int32),
+    order=lambda t, w, b: pltpu.VMEM((b, t), jnp.int32),
+    ids=lambda t, w, b: pltpu.VMEM((2, 4, 1, t), jnp.int32),
+    pieces=lambda t, w, b: pltpu.VMEM((8, 16, w // 2), BF16),
+    vectors=lambda t, w, b: pltpu.VMEM((16, w), F32),
+    pack_out=lambda t, w, b: pltpu.VMEM((2 * t, w), BF16),
+    pack_in=lambda t, w, b: pltpu.VMEM((2 * t, w), BF16),
+    teach_out=lambda t, w, b: pltpu.VMEM((t, w), BF16),
+    teach_in=lambda t, w, b: pltpu.VMEM((t, w), BF16),
+    full=lambda t, w, b: pltpu.VMEM((12 * w, w), BF16),
+    packed=lambda t, w, b: pltpu.VMEM((t, w), BF16),
+    packed_t=lambda t, w, b: pltpu.VMEM((w, t), BF16),
+    cot=lambda t, w, b: pltpu.VMEM((t, w), BF16),
+    query=lambda t, w, b: pltpu.VMEM((t, w), BF16),
+    keys=lambda t, w, b: pltpu.VMEM((4, t, w), BF16),
+    values_t=lambda t, w, b: pltpu.VMEM((4, w, t), BF16),
+    mask=lambda t, w, b: pltpu.VMEM((4, t, t), F32),
+    scores=lambda t, w, b: pltpu.VMEM((2, 4, t, t), F32),
+    probs=lambda t, w, b: pltpu.VMEM((HEADS, 4, t, t), BF16),
+    keys_t=lambda t, w, b: pltpu.VMEM((4, w, t), BF16),
+    values=lambda t, w, b: pltpu.VMEM((4, t, w), BF16),
+    context_t=lambda t, w, b: pltpu.VMEM((w, t), BF16),
+    scaled=lambda t, w, b: pltpu.VMEM((t, w), F32),
+    inverse=lambda t, w, b: pltpu.VMEM((t, 128), F32),
+    normed=lambda t, w, b: pltpu.VMEM((t, w), F32),
+    low=lambda t, w, b: pltpu.VMEM((t, w), BF16),
+    low_t=lambda t, w, b: pltpu.VMEM((w, t), BF16),
+    act=lambda t, w, b: pltpu.VMEM((t, 4 * w), BF16),
+    act_t=lambda t, w, b: pltpu.VMEM((4 * w, t), BF16),
+    slope=lambda t, w, b: pltpu.VMEM((t, 4 * w), BF16),
+    result=lambda t, w, b: pltpu.VMEM((t, w), BF16),
+    grad_res=lambda t, w, b: pltpu.VMEM((t, w), F32),
+    grad_ffn=lambda t, w, b: pltpu.VMEM((t, w), BF16),
+    small=lambda t, w, b: pltpu.VMEM((16, w), F32),
+    routes=lambda t, w, b: pltpu.VMEM((8, t), F32),
+    ints_send=lambda t, w, b: pltpu.SemaphoreType.DMA((b,)),
+    ints_recv=lambda t, w, b: pltpu.SemaphoreType.DMA((b,)),
+    piece_send=lambda t, w, b: pltpu.SemaphoreType.DMA((8,)),
+    piece_recv=lambda t, w, b: pltpu.SemaphoreType.DMA((8,)),
+    pack_send=lambda t, w, b: pltpu.SemaphoreType.DMA((b,)),
+    pack_recv=lambda t, w, b: pltpu.SemaphoreType.DMA((b,)),
+    misc_send=lambda t, w, b: pltpu.SemaphoreType.DMA((8,)),
+    misc_recv=lambda t, w, b: pltpu.SemaphoreType.DMA((8,)),
+    weight_send=lambda t, w, b: pltpu.SemaphoreType.DMA((UNITS, 8)),
+    weight_recv=lambda t, w, b: pltpu.SemaphoreType.DMA((UNITS, 8)),
+    own_sem=lambda t, w, b: pltpu.SemaphoreType.DMA((UNITS,)),
+    store_sem=lambda t, w, b: pltpu.SemaphoreType.DMA((32,)),
+)
+
+class Kept(NamedTuple):
+    full: object
+    probs: object
+    keys_t: object
+    values: object
+    packed_t: object
+    query: object
+    context_t: object
+    scaled: object
+    inverse: object
+    low_t: object
+    act_t: object
+    slope: object
+    result: object
+    grad_res: object
+    grad_ffn: object
+    small: object
+    routes: object
+
+
 HEADS = 12
+NORM_EPS = 1e-12
+
+
+def normalize(value):
+    centre = value - jnp.mean(value, -1, keepdims=True)
+    spread = jnp.mean(centre * centre, -1, keepdims=True)
+    inverse = lax.rsqrt(spread + NORM_EPS)
+    return centre * inverse, inverse
+
+
+def forward_kernel(z_size, ints, ids, tokens, cotangent, teacher, pieces, w_query, w_key, w_value, w_out, w_up, w_down, *refs):
+    outs = Kept(*refs[: len(Kept._fields)])
+    s = SimpleNamespace(**dict(zip(FORWARD_SCRATCH, refs[len(Kept._fields) :])))
+    route = Route(z_size)
+    place = route.place
+    rows, width = tokens.shape
+    blocks = route.blocks
+    full = s.full
+    weights = Weights(place, full, s.weight_send, s.weight_recv)
+    stores = []
+
+    def keep(source, target):
+        copy = pltpu.make_async_copy(source, target, s.store_sem.at[len(stores)])
+        copy.start()
+        stores.append(copy)
+
+    sources = (
+        [w_key, w_value, w_query, w_out]
+        + [w_up.at[:, width * i : width * (i + 1)] for i in range(4)]
+        + [w_down.at[BLOCK * i : BLOCK * (i + 1), :] for i in range(4)]
+    )
+    own_copies = [
+        pltpu.make_async_copy(source, weights.at(unit, place.dp), s.own_sem.at[unit])
+        for unit, source in enumerate(sources)
+    ]
+    for copy in own_copies:
+        copy.start()
+    s.ints[route.home] = ints[...]
+    s.teach_out[...] = teacher[...].astype(BF16)
+    route.greet_all()
+
+    def ints_copy(other):
+        return remote(
+            ints,
+            s.ints.at[route.home],
+            s.ints_send.at[other],
+            s.ints_recv.at[route.home],
+            route.owner(other),
+        )
+
+    def ints_arrival(other):
+        ref = s.ints.at[other]
+        return remote(ref, ref, s.ints_send.at[other], s.ints_recv.at[other], route.owner(other))
+
+    def each_other(start, action):
+        def one(step, carry):
+            action((start + step) % blocks)
+            return carry
+
+        lax.fori_loop(1, blocks, one, 0)
+
+    each_other(route.home, lambda other: ints_copy(other).start())
+    for copy in own_copies[:2]:
+        copy.wait()
+    weights.begin(0)
+    weights.begin(1)
+
+    def piece_copy(step):
+        other = (place.dp + step) % 8
+        return remote(
+            pieces,
+            s.pieces.at[place.dp],
+            s.piece_send.at[step],
+            s.piece_recv.at[step],
+            {"dp": other},
+        )
+
+    for step in range(1, 8):
+        piece_copy(step).start()
+    s.pieces[place.dp] = pieces[...]
+    ids_copy = remote(ids, s.ids.at[1], s.misc_send.at[0], s.misc_recv.at[0], place.mate)
+    ids_copy.start()
+    s.ids[0] = ids[...]
+    for copy in own_copies[2:]:
+        copy.wait()
+
+    each_other(route.home, lambda other: ints_arrival(other).wait_recv())
+    count = jnp.zeros((1, rows), F32)
+    for other in range(blocks):
+        s.order[other : other + 1, :] = s.ints[other, 0:1, :]
+        count = count + s.ints[other, 1:2, :].astype(F32)
+    count = jnp.sum(count, 1, keepdims=True)
+    order = s.order[...]
+    source = lax.shift_right_logical(order, 8)
+    local = (order - source * rows).astype(F32)
+    mine = source == route.home
+    earlier = one_hot(iota((rows, rows), 0) < iota((rows, rows), 1))
+    rank = dot(one_hot(mine), earlier)
+    per_block = rows // blocks
+    slots = jnp.zeros((blocks, 128), F32)
+    for k in range(per_block):
+        picked = jnp.sum(jnp.where(mine & (rank == k), local, 0.0), 1, keepdims=True)
+        slots = jnp.where(iota((blocks, 128), 1) == k, picked, slots)
+    spread = one_hot(
+        lax.shift_right_logical(iota((2 * rows, blocks), 0), 4) == iota((2 * rows, blocks), 1)
+    )
+    slot_rows = dot(spread, slots.astype(BF16))
+    slot = iota((2 * rows, 128), 0)
+    picked = jnp.sum(
+        jnp.where(iota((2 * rows, 128), 1) == (slot & 7), slot_rows, 0.0), 1, keepdims=True
+    )
+    lane = iota((2 * rows, rows), 1).astype(F32)
+    first = (iota((2 * rows, rows), 0) & 8) == 0
+    hit = lane == picked
+    s.pack_out[...] = (
+        dot(one_hot(hit & first), tokens[...])
+        + dot(one_hot(hit & jnp.logical_not(first)), cotangent[...])
+    ).astype(BF16)
+    spread8 = one_hot(
+        lax.shift_right_logical(iota((rows, blocks), 0), 3) == iota((rows, blocks), 1)
+    )
+    slot8 = jnp.sum(
+        jnp.where(
+            iota((rows, 128), 1) == (iota((rows, 128), 0) & 7),
+            dot(spread8, slots.astype(BF16)),
+            0.0,
+        ),
+        1,
+        keepdims=True,
+    )
+    diagonal = iota((rows, rows), 0) == iota((rows, rows), 1)
+    s.routes[1:2, :] = jnp.sum(jnp.where(diagonal, slot8, 0.0), 0, keepdims=True)
+
+    def span(block):
+        return pl.ds(pl.multiple_of(16 * block, 16), 16)
+
+    def pack_copy(block):
+        return remote(
+            s.pack_out.at[span(block), :],
+            s.pack_in.at[span(route.home), :],
+            s.pack_send.at[block],
+            s.pack_recv.at[route.home],
+            route.worker(block),
+        )
+
+    def pack_arrival(other):
+        ref = s.pack_in.at[span(other), :]
+        return remote(ref, ref, s.pack_send.at[other], s.pack_recv.at[other], route.owner(other))
+
+    each_other(route.block, lambda block: pack_copy(block).start())
+    s.pack_in[span(route.home), :] = s.pack_out[span(route.block), :]
+    weights.tick(2)
+
+    moved_to = route.worker(route.home)
+    stays = route.block == route.home
+    teach_copy = remote(
+        s.teach_out, s.teach_in, s.misc_send.at[1], s.misc_recv.at[1], moved_to
+    )
+
+    for step in range(1, 8):
+        piece_copy(step).wait_recv()
+    wrapped = one_hot(
+        iota((BLOCK, width), 0) == iota((BLOCK, width), 1) - BLOCK * (iota((BLOCK, width), 1) // BLOCK)
+    )
+    owner = iota((16, width), 1) // BLOCK
+    vectors = jnp.zeros((16, width), F32)
+    for k in range(8):
+        vectors = vectors + jnp.where(owner == k, dot(s.pieces[k, :, :BLOCK], wrapped), 0.0)
+    s.vectors[...] = vectors
+    for k in range(8):
+        part = s.pieces[k, 8:9, :].astype(F32)
+        s.vectors[8 + k // 2 : 9 + k // 2, 4 * BLOCK * (k % 2) : 4 * BLOCK * (k % 2 + 1)] = part
+
+    def vector(index):
+        return s.vectors[index : index + 1, :]
+
+    ids_copy.wait_recv()
+    here = s.ints[route.block, 0:1, :]
+    source_row = lax.shift_right_logical(here, 8).astype(F32)
+    source_col = column(source_row)
+    same = source_col == source_row
+    before = iota((rows, rows), 1) < iota((rows, rows), 0)
+    rank_col = jnp.sum(jnp.where(same & before, 1.0, 0.0), 1, keepdims=True)
+    rank_row = jnp.sum(
+        jnp.where(same & jnp.logical_not(before | diagonal), 1.0, 0.0), 0, keepdims=True
+    )
+    s.routes[0:1, :] = source_row * 8 + rank_row
+    wide = iota((rows, 2 * rows), 1).astype(F32)
+    place_col = source_col * 16 + rank_col
+    each_other(route.home, lambda other: pack_arrival(other).wait_recv())
+    s.packed[...] = dot(one_hot(wide == place_col), s.pack_in[...]).astype(BF16)
+    s.cot[...] = dot(one_hot(wide == place_col + 8), s.pack_in[...]).astype(BF16)
+    s.packed_t[...] = s.packed[...].T
+    keep(s.packed_t, outs.packed_t)
+    weights.tick(3)
+    weights.tick(4)
+    weights.tick(5)
+
+    def kv_copy(kind):
+        buffer, half = (s.keys, s.values_t)[kind // 3], kind % 3
+        quarter, to = (
+            (route.quarter, route.pair),
+            (route.quarter, place.mate),
+            (route.pair_quarter, place.mate),
+        )[half]
+        ref = buffer.at[quarter]
+        return remote(ref, ref, s.misc_send.at[2 + kind], s.misc_recv.at[2 + kind], to)
+
+    def kv_arrival(kind):
+        buffer, half = (s.keys, s.values_t)[kind // 3], kind % 3
+        quarter = (route.pair_quarter, route.mate_quarter, route.far_quarter)[half]
+        ref = buffer.at[quarter]
+        to = (route.pair, place.mate, place.mate)[half]
+        return remote(ref, ref, s.misc_send.at[2 + kind], s.misc_recv.at[2 + kind], to)
+
+    packed = s.packed[...]
+
+    def whole(unit):
+        return full[width * unit : width * (unit + 1), :]
+
+    weights.ready(0)
+    s.keys[route.quarter] = dot(packed, whole(0)).astype(BF16)
+    weights.ready(1)
+    values = (dot(packed, whole(1)) + vector(1)).astype(BF16)
+    kv_copy(0).start()
+    kv_copy(1).start()
+    s.values_t[route.quarter] = values.T
+    weights.ready(2)
+    scale = (width // HEADS) ** -0.5
+    s.query[...] = (
+        (dot(packed, whole(2)) + vector(0)).astype(BF16).astype(F32) * scale
+    ).astype(BF16)
+    kv_copy(3).start()
+    kv_copy(4).start()
+    keep(s.query, outs.query)
+
+    @pl.when(jnp.logical_not(stays))
+    def _():
+        teach_copy.start()
+
+    @pl.when(stays)
+    def _():
+        s.teach_in[...] = s.teach_out[...]
+
+    from_own = place.core == route.group_core
+    query_row = jnp.where(
+        from_own, s.ids[0, route.quarter], s.ids[1, route.quarter]
+    ).astype(F32)
+    for quarter in range(4):
+        key_row = jnp.where(from_own, s.ids[0, quarter], s.ids[1, quarter]).astype(F32)
+        s.mask[quarter] = jnp.where(column(key_row) == query_row, 0.0, -1e30)
+    kv_arrival(0).wait_recv()
+    kv_copy(2).start()
+    kv_arrival(3).wait_recv()
+    kv_copy(5).start()
+    for kind in (1, 2, 4, 5):
+        kv_arrival(kind).wait_recv()
+
+    head = width // HEADS
+    left_half = iota((rows, 2 * head), 1) < head
+
+    def pair_of_heads(pair, carry):
+        weights.tick(pair + 6)
+        lanes = pl.ds(pl.multiple_of(2 * head * pair, 2 * head), 2 * head)
+        both = s.query[:, lanes]
+        for side in range(2):
+            keep_lane = left_half if side == 0 else jnp.logical_not(left_half)
+            chosen = jnp.where(keep_lane, both, jnp.zeros_like(both))
+            top = jnp.full((1, rows), -3e38, F32)
+            for quarter in range(4):
+                part = dot_nt(s.keys[quarter, :, lanes], chosen) + s.mask[quarter]
+                s.scores[side, quarter] = part
+                top = jnp.maximum(top, jnp.max(part, 0, keepdims=True))
+            total = jnp.zeros((1, rows), F32)
+            for quarter in range(4):
+                part = jnp.exp(s.scores[side, quarter] - top)
+                s.scores[side, quarter] = part
+                total = total + jnp.sum(part, 0, keepdims=True)
+            share = 1.0 / total
+            index = 2 * pair + side
+            down = pl.ds(pl.multiple_of(head * index, head), head)
+            summed = jnp.zeros((head, rows), F32)
+            for quarter in range(4):
+                part = (s.scores[side, quarter] * share).astype(BF16)
+                s.probs[index, quarter] = part
+                summed = summed + dot(s.values_t[quarter, down, :], part)
+            s.context_t[down, :] = summed.astype(BF16)
+        return carry
+
+    lax.fori_loop(0, HEADS // 2, pair_of_heads, 0)
+    keep(s.probs, outs.probs)
+    keep(s.context_t, outs.context_t)
+    weights.pass_on(10)
+    weights.corner(9)
+
+    weights.ready(3)
+    branch = dot(s.context_t[...].T, whole(3)) + vector(2)
+    scaled, inverse = normalize(s.packed[...].astype(F32) + branch)
+    s.scaled[...] = scaled
+    s.inverse[...] = jnp.broadcast_to(inverse, (rows, 128))
+    normed = scaled * vector(3) + vector(4)
+    s.normed[...] = normed
+    low = normed.astype(BF16)
+    s.low[...] = low
+    s.low_t[...] = low.T
+    keep(s.scaled, outs.scaled)
+    keep(s.inverse, outs.inverse)
+    keep(s.low_t, outs.low_t)
+    weights.pass_on(11)
+    weights.corner(10)
+    weights.corner(11)
+
+    for part in range(4):
+        weights.ready(4 + part)
+    root_half, norm = 2.0**-0.5, (2.0 * math.pi) ** -0.5
+    piece = width // 2
+
+    def up(step, carry):
+        lanes = pl.ds(pl.multiple_of(piece * (step % 2), piece), piece)
+        wide = pl.ds(pl.multiple_of(piece * step, piece), piece)
+        down = pl.ds(pl.multiple_of(width * (4 + step // 2), width), width)
+        bias = s.vectors[pl.ds(8 + step // 2, 1), lanes]
+        pre = dot(s.low[...], full[down, lanes]) + bias
+        phi = 0.5 + 0.5 * lax.erf(pre * root_half)
+        act = (pre * phi).astype(BF16)
+        s.act[:, wide] = act
+        s.act_t[wide, :] = act.T
+        s.slope[:, wide] = (phi + pre * (norm * jnp.exp(-0.5 * pre * pre))).astype(BF16)
+        return carry
+
+    lax.fori_loop(0, 8, up, 0)
+    keep(s.act_t, outs.act_t)
+    keep(s.slope, outs.slope)
+    for quarter in range(4):
+        s.keys_t[quarter] = s.keys[quarter].T
+        s.values[quarter] = s.values_t[quarter].T
+    keep(s.keys_t, outs.keys_t)
+    keep(s.values, outs.values)
+    for part in range(4):
+        weights.ready(8 + part)
+    keep(s.full, outs.full)
+    ffn = dot(s.act[...], full[8 * width :, :]) + vector(5)
+
+    scaled, inverse = normalize(s.normed[...] + ffn)
+    result = scaled * vector(6) + vector(7)
+    s.result[...] = result.astype(BF16)
+    keep(s.result, outs.result)
+
+    @pl.when(jnp.logical_not(stays))
+    def _():
+        teach_copy.wait_recv()
+
+    valid = column(s.ints[route.block, 1:2, :].astype(F32))
+    miss = valid * (result - s.teach_in[...].astype(F32))
+    factor = 1.0 / (count * width)
+    s.small[...] = jnp.zeros((16, width), F32)
+    s.small[12:13, :] = jnp.sum(miss * miss, 0, keepdims=True) * factor
+    grad_out = s.cot[...].astype(F32) + (2.0 * factor) * miss
+    s.small[6:7, :] = jnp.sum(grad_out * scaled, 0, keepdims=True)
+    s.small[7:8, :] = jnp.sum(grad_out, 0, keepdims=True)
+    s.small[13:14, :] = vector(3)
+    grad_scaled = grad_out * vector(6)
+    grad_res = inverse * (
+        grad_scaled
+        - jnp.mean(grad_scaled, -1, keepdims=True)
+        - scaled * jnp.mean(grad_scaled * scaled, -1, keepdims=True)
+    )
+    s.grad_res[...] = grad_res
+    grad_ffn = grad_res.astype(BF16)
+    s.grad_ffn[...] = grad_ffn
+    s.small[5:6, :] = jnp.sum(grad_ffn.astype(F32), 0, keepdims=True)
+    keep(s.grad_res, outs.grad_res)
+    keep(s.grad_ffn, outs.grad_ffn)
+    keep(s.small, outs.small)
+    keep(s.routes, outs.routes)
+
+    weights.drain()
+    each_other(route.home, lambda other: ints_copy(other).wait_send())
+    each_other(route.block, lambda block: pack_copy(block).wait_send())
+    for step in range(1, 8):
+        piece_copy(step).wait_send()
+    ids_copy.wait_send()
+    for kind in range(6):
+        kv_copy(kind).wait_send()
+
+    @pl.when(jnp.logical_not(stays))
+    def _():
+        teach_copy.wait_send()
+
+    for copy in stores:
+        copy.wait()
+
+
+def encoder_forward(z_size, ints, ids, tokens, cotangent, teacher, pieces, *shards):
+    rows, width = tokens.shape
+    blocks = 8 * z_size
+    scratch = {name: make(rows, width, blocks) for name, make in FORWARD_SCRATCH.items()}
+    vmem, anywhere = pl.BlockSpec(memory_space=pltpu.VMEM), pl.BlockSpec(memory_space=pl.ANY)
+    results = pl.pallas_call(
+        partial(forward_kernel, z_size),
+        out_shape=tuple(
+            jax.ShapeDtypeStruct(scratch[name].shape, scratch[name].dtype) for name in Kept._fields
+        ),
+        in_specs=[vmem] * 6 + [anywhere] * 6,
+        out_specs=(anywhere,) * len(Kept._fields),
+        scratch_shapes=list(scratch.values()),
+        compiler_params=pltpu.CompilerParams(
+            collective_id=0, has_side_effects=True, vmem_limit_bytes=62 * 2**20
+        ),
+        name="encoder_forward",
+    )(ints, ids, tokens, cotangent, teacher, pieces, *shards)
+    return Kept(*results)
+
+
+LEFT = (0, 1, 2, 3, 4, 4, 4, 4, 5, 6, 6, 6)
+RIGHT = (0, 0, 0, 0, 1, 2, 3, 4, 5, 6, 7, 8)
+
+
+class Grads:
+    def __init__(self, place, s, out):
+        self.place, self.s, self.out = place, s, out
+        self.tok_rows = s.left.shape[2] // 2
+        half = BLOCK // 2
+        self.low, self.high = slice(0, half), slice(half, BLOCK)
+
+    def source_rows(self, group, j, core):
+        shard = 2 * j + core
+        if group < 4:
+            return pl.ds(pl.multiple_of(4 * BLOCK * shard + BLOCK * group, 32), BLOCK)
+        return pl.ds(pl.multiple_of(BLOCK * shard, 32), BLOCK)
+
+    def left_copy(self, group, j, source):
+        return remote(
+            source.at[self.source_rows(group, j, 1 - self.place.core), :],
+            self.s.left.at[group, BLOCK * j : BLOCK * (j + 1), self.tok_rows :],
+            self.s.left_send.at[group, j],
+            self.s.left_recv.at[group, j],
+            self.place.mate,
+        )
+
+    def left_own(self, group, j, source):
+        return pltpu.make_async_copy(
+            source.at[self.source_rows(group, j, self.place.core), :],
+            self.s.left.at[group, BLOCK * j : BLOCK * (j + 1), : self.tok_rows],
+            self.s.left_own.at[group, j],
+        )
+
+    def give_left(self, group, source):
+        for j in range(4):
+            self.left_copy(group, j, source).start()
+            self.left_own(group, j, source).start()
+
+    def take_left(self, group, source):
+        for j in range(4):
+            self.left_copy(group, j, source).wait_recv()
+            self.left_own(group, j, source).wait()
+
+    def own_right(self, index):
+        return self.s.right.at[index, : self.tok_rows, :]
+
+    def right_copy(self, index):
+        return remote(
+            self.own_right(index),
+            self.s.right.at[index, self.tok_rows :, :],
+            self.s.right_send.at[index],
+            self.s.right_recv.at[index],
+            self.place.mate,
+        )
+
+    def copy(self, unit, kind):
+        place, low, high, s = self.place, self.low, self.high, self.s
+        source, target, to = (
+            (s.out_d.at[unit, low], s.in_dx.at[unit], place.across),
+            (s.out_d.at[unit, high], s.in_dy.at[unit], place.along),
+            (s.out_x.at[unit, low], s.in_x.at[unit, low], place.across),
+            (s.out_x.at[unit, high], s.in_x.at[unit, high], place.across),
+            (s.out_y.at[unit, low], s.in_y.at[unit, low], place.along),
+            (s.out_y.at[unit, high], s.in_y.at[unit, high], place.along),
+            (s.out_x.at[unit], s.in_z.at[0, unit], {"ctx": place.z + 1}),
+            (s.out_y.at[unit], s.in_z.at[1, unit], {"ctx": place.z - 1}),
+        )[kind]
+        return remote(source, target, s.send.at[unit, kind], s.recv.at[unit, kind], to)
+
+    def part(self, j):
+        return pl.ds(pl.multiple_of(BLOCK * j, 32), BLOCK)
+
+    def multiply(self, unit):
+        place, low, high, s = self.place, self.low, self.high, self.s
+        s.partial[...] = dot(s.left[LEFT[unit]], s.right[RIGHT[unit]])
+        s.out_d[unit] = s.partial[self.part(place.j_d), :].astype(BF16)
+        s.out_x[unit] = s.partial[self.part(place.j_x), :].astype(BF16)
+        s.out_y[unit] = s.partial[self.part(place.j_y), :].astype(BF16)
+        s.total[unit] = s.partial[self.part(place.j_own), :]
+        for kind in (0, 1, 2, 5):
+            self.copy(unit, kind).start()
+
+    def pass_on(self, unit):
+        low, high, s = self.low, self.high, self.s
+        self.copy(unit, 0).wait_recv()
+        s.out_y[unit, low] = (
+            s.out_y[unit, low].astype(F32) + s.in_dx[unit].astype(F32)
+        ).astype(BF16)
+        self.copy(unit, 1).wait_recv()
+        s.out_x[unit, high] = (
+            s.out_x[unit, high].astype(F32) + s.in_dy[unit].astype(F32)
+        ).astype(BF16)
+        self.copy(unit, 4).start()
+        self.copy(unit, 3).start()
+
+    def gather(self, unit):
+        s = self.s
+        for kind in (2, 3, 4, 5):
+            self.copy(unit, kind).wait_recv()
+        s.total[unit] = (
+            s.total[unit] + s.in_x[unit].astype(F32) + s.in_y[unit].astype(F32)
+        )
+        for kind in (2, 3, 4, 5):
+            self.copy(unit, kind).wait_send()
+
+    def hop(self, unit, step):
+        place, s = self.place, self.s
+        for way, turn in ((0, step), (1, place.z_size - 1 - step)):
+
+            @pl.when(place.z == turn)
+            def _():
+                value = s.total[unit]
+                if step > 0:
+                    self.copy(unit, 6 + way).wait_recv()
+                    value = value + s.in_z[way, unit].astype(F32)
+                (s.out_x, s.out_y)[way][unit] = value.astype(BF16)
+                self.copy(unit, 6 + way).start()
+
+    def result(self, unit):
+        return pltpu.make_async_copy(
+            self.s.total.at[unit], self.out.at[unit], self.s.out_sem.at[unit]
+        )
+
+    def finish(self, unit):
+        place, s = self.place, self.s
+        last = place.z_size - 1
+
+        @pl.when(place.z == last)
+        def _():
+            self.copy(unit, 6).wait_recv()
+
+        @pl.when(place.z == 0)
+        def _():
+            self.copy(unit, 7).wait_recv()
+
+        for way, present in ((0, place.z > 0), (1, place.z < last)):
+
+            @pl.when(present)
+            def _():
+                s.total[unit] = s.total[unit] + s.in_z[way, unit].astype(F32)
+
+        self.result(unit).start()
+
+    def drain(self, lefts):
+        place = self.place
+
+        def one(unit, carry):
+            self.copy(unit, 0).wait_send()
+            self.copy(unit, 1).wait_send()
+
+            @pl.when(place.z < place.z_size - 1)
+            def _():
+                self.copy(unit, 6).wait_send()
+
+            @pl.when(place.z > 0)
+            def _():
+                self.copy(unit, 7).wait_send()
+
+            self.result(unit).wait()
+            return carry
+
+        lax.fori_loop(0, UNITS, one, 0)
+        for group in range(7):
+            for j in range(4):
+                self.left_copy(group, j, lefts[group]).wait_send()
+        for index in range(9):
+            self.right_copy(index).wait_send()
+
+
+BACKWARD_SCRATCH = dict(
+    left=lambda t, w, b: pltpu.VMEM((7, 4 * BLOCK, 2 * t), BF16),
+    right=lambda t, w, b: pltpu.VMEM((9, 2 * t, w), BF16),
+    partial=lambda t, w, b: pltpu.VMEM((4 * BLOCK, w), F32),
+    out_d=lambda t, w, b: pltpu.VMEM((UNITS, BLOCK, w), BF16),
+    out_x=lambda t, w, b: pltpu.VMEM((UNITS, BLOCK, w), BF16),
+    out_y=lambda t, w, b: pltpu.VMEM((UNITS, BLOCK, w), BF16),
+    in_dx=lambda t, w, b: pltpu.VMEM((UNITS, BLOCK // 2, w), BF16),
+    in_dy=lambda t, w, b: pltpu.VMEM((UNITS, BLOCK // 2, w), BF16),
+    in_x=lambda t, w, b: pltpu.VMEM((UNITS, BLOCK, w), BF16),
+    in_y=lambda t, w, b: pltpu.VMEM((UNITS, BLOCK, w), BF16),
+    total=lambda t, w, b: pltpu.VMEM((UNITS, BLOCK, w), F32),
+    in_z=lambda t, w, b: pltpu.VMEM((2, UNITS, BLOCK, w), BF16),
+    weight_a=lambda t, w, b: pltpu.VMEM((4 * w, w), BF16),
+    weight_b=lambda t, w, b: pltpu.VMEM((4 * w, w), BF16),
+    probs=lambda t, w, b: pltpu.VMEM((2, 2, 4, t, t), BF16),
+    keys_t=lambda t, w, b: pltpu.VMEM((4, w, t), BF16),
+    values=lambda t, w, b: pltpu.VMEM((4, t, w), BF16),
+    query=lambda t, w, b: pltpu.VMEM((t, w), BF16),
+    context_t=lambda t, w, b: pltpu.VMEM((w, t), BF16),
+    scaled=lambda t, w, b: pltpu.VMEM((t, w), F32),
+    inverse=lambda t, w, b: pltpu.VMEM((t, 128), F32),
+    slope=lambda t, w, b: pltpu.VMEM((t, 4 * w), BF16),
+    result=lambda t, w, b: pltpu.VMEM((t, w), BF16),
+    grad_res=lambda t, w, b: pltpu.VMEM((t, w), F32),
+    small=lambda t, w, b: pltpu.VMEM((16, w), F32),
+    routes=lambda t, w, b: pltpu.VMEM((8, t), F32),
+    grad_context=lambda t, w, b: pltpu.VMEM((t, w), BF16),
+    grad_context_t=lambda t, w, b: pltpu.VMEM((w, t), BF16),
+    grad_query_t=lambda t, w, b: pltpu.VMEM((w, t), BF16),
+    kv_out=lambda t, w, b: pltpu.VMEM((HEADS // 2, 4, t, t), BF16),
+    kv_mate=lambda t, w, b: pltpu.VMEM((HEADS // 2, 2, t, t), BF16),
+    kv_pair=lambda t, w, b: pltpu.VMEM((HEADS // 2, t, t), BF16),
+    back_out=lambda t, w, b: pltpu.VMEM((2, b, t // b, w), BF16),
+    back_in=lambda t, w, b: pltpu.VMEM((2, b, t // b, w), BF16),
+    homes=lambda t, w, b: pltpu.VMEM((2, t, w), BF16),
+    sums=lambda t, w, b: pltpu.VMEM((3, 16, w), F32),
+    got_sums=lambda t, w, b: pltpu.VMEM((3, 16, w), F32),
+    got_z=lambda t, w, b: pltpu.VMEM((b // 8, 16, w), F32),
+    send=lambda t, w, b: pltpu.SemaphoreType.DMA((UNITS, 8)),
+    recv=lambda t, w, b: pltpu.SemaphoreType.DMA((UNITS, 8)),
+    left_send=lambda t, w, b: pltpu.SemaphoreType.DMA((7, 4)),
+    left_recv=lambda t, w, b: pltpu.SemaphoreType.DMA((7, 4)),
+    left_own=lambda t, w, b: pltpu.SemaphoreType.DMA((7, 4)),
+    right_send=lambda t, w, b: pltpu.SemaphoreType.DMA((9,)),
+    right_recv=lambda t, w, b: pltpu.SemaphoreType.DMA((9,)),
+    out_sem=lambda t, w, b: pltpu.SemaphoreType.DMA((UNITS,)),
+    load_sem=lambda t, w, b: pltpu.SemaphoreType.DMA((20,)),
+    probs_sem=lambda t, w, b: pltpu.SemaphoreType.DMA((2,)),
+    kv_send=lambda t, w, b: pltpu.SemaphoreType.DMA((HEADS // 2, 3)),
+    kv_recv=lambda t, w, b: pltpu.SemaphoreType.DMA((HEADS // 2, 3)),
+    back_send=lambda t, w, b: pltpu.SemaphoreType.DMA((2, b)),
+    back_recv=lambda t, w, b: pltpu.SemaphoreType.DMA((2, b)),
+    sum_send=lambda t, w, b: pltpu.SemaphoreType.DMA((3 + b // 8,)),
+    sum_recv=lambda t, w, b: pltpu.SemaphoreType.DMA((3 + b // 8,)),
+)
+
+
+def backward_kernel(z_size, *refs):
+    count = len(Kept._fields)
+    given = Kept(*refs[:count])
+    out_grads, out_homes, out_small = refs[count : count + 3]
+    s = SimpleNamespace(**dict(zip(BACKWARD_SCRATCH, refs[count + 3 :])))
+    route = Route(z_size)
+    place = route.place
+    rows, width = s.query.shape
+    blocks = route.blocks
+    grads = Grads(place, s, out_grads)
+    head = width // HEADS
+    pairs = HEADS // 2
+
+    count = [0]
+
+    def load(source, target):
+        copy = pltpu.make_async_copy(source, target, s.load_sem.at[count[0]])
+        count[0] += 1
+        copy.start()
+        return copy
+
+    def loaded(*copies):
+        for copy in copies:
+            copy.wait()
+
+    full = given.full
+    l_ffn = load(given.grad_ffn, grads.own_right(0))
+    l_down = load(full.at[2 * 4 * width :, :], s.weight_a)
+    l_up = load(full.at[4 * width : 8 * width, :], s.weight_b)
+    l_slope = load(given.slope, s.slope)
+    l_routes = load(given.routes, s.routes)
+    l_result = load(given.result, s.result)
+    l_small = load(given.small, s.small)
+    l_grad_res = load(given.grad_res, s.grad_res)
+    l_scaled = load(given.scaled, s.scaled)
+    l_inverse = load(given.inverse, s.inverse)
+    l_query = load(given.query, s.query)
+    l_context_t = load(given.context_t, s.context_t)
+    l_keys_t = load(given.keys_t, s.keys_t)
+    l_values = load(given.values, s.values)
+
+    def probs_copy(pair):
+        slot = pair % 2
+        return pltpu.make_async_copy(
+            given.probs.at[pl.ds(2 * pair, 2)], s.probs.at[slot], s.probs_sem.at[slot]
+        )
+
+    probs_copy(0).start()
+    lefts = (given.act_t,) * 4 + (given.low_t, given.context_t, given.packed_t)
+    route.greet_all()
+
+    def each_other(start, action):
+        def one(step, carry):
+            action((start + step) % blocks)
+            return carry
+
+        lax.fori_loop(1, blocks, one, 0)
+
+    loaded(l_ffn)
+    grads.right_copy(0).start()
+    for group in range(7):
+        grads.give_left(group, lefts[group])
+
+    def back_copy(which, other):
+        return remote(
+            s.back_out.at[which, other],
+            s.back_in.at[which, route.block],
+            s.back_send.at[which, other],
+            s.back_recv.at[which, route.block],
+            route.owner(other),
+        )
+
+    def back_arrival(which, block):
+        ref = s.back_in.at[which, block]
+        return remote(
+            ref, ref, s.back_send.at[which, block], s.back_recv.at[which, block], route.worker(block)
+        )
+
+    def send_back(which, value):
+        ordered = one_hot(iota((rows, rows), 0).astype(F32) == s.routes[0:1, :])
+        s.back_out[which] = (
+            dot(ordered, value).reshape(blocks, rows // blocks, width).astype(BF16)
+        )
+        each_other(route.home, lambda other: back_copy(which, other).start())
+        s.back_in[which, route.block] = s.back_out[which, route.home]
+
+    def take_back(which):
+        each_other(route.block, lambda block: back_arrival(which, block).wait_recv())
+        placed = one_hot(iota((rows, rows), 0).astype(F32) == s.routes[1:2, :])
+        flat = s.back_in[which].astype(F32).reshape(rows, width).astype(BF16)
+        s.homes[which] = dot(placed, flat).astype(BF16)
+
+    for group in range(4):
+        grads.take_left(group, lefts[group])
+    grads.right_copy(0).wait_recv()
+    for unit in range(4):
+        grads.multiply(unit)
+
+    loaded(l_routes, l_result)
+    send_back(0, s.result[...])
+    loaded(l_down, l_up, l_slope, l_small, l_grad_res, l_scaled, l_inverse)
+    grad_ffn = s.right[0, :rows, :]
+    grad_normed = s.grad_res[...]
+    for part in range(4):
+        block = slice(width * part, width * (part + 1))
+        grad_act = dot_nt(grad_ffn, s.weight_a[block, :])
+        grad_pre = (grad_act * s.slope[:, block].astype(F32)).astype(BF16)
+        s.right[1 + part, :rows, :] = grad_pre
+        s.small[8 + part : 9 + part, :] = jnp.sum(grad_pre.astype(F32), 0, keepdims=True)
+        grad_normed = grad_normed + dot_nt(grad_pre, s.weight_b[block, :])
+        grads.right_copy(1 + part).start()
+        grads.pass_on(part)
+    l_rest = load(full.at[: 4 * width, :], s.weight_a)
+
+    scaled = s.scaled[...]
+    s.small[3:4, :] = jnp.sum(grad_normed * scaled, 0, keepdims=True)
+    s.small[4:5, :] = jnp.sum(grad_normed, 0, keepdims=True)
+    grad_scaled = grad_normed * s.small[13:14, :]
+    grad_res = s.inverse[:, :1] * (
+        grad_scaled
+        - jnp.mean(grad_scaled, -1, keepdims=True)
+        - scaled * jnp.mean(grad_scaled * scaled, -1, keepdims=True)
+    )
+    s.grad_res[...] = grad_res
+    grad_branch = grad_res.astype(BF16)
+    s.right[5, :rows, :] = grad_branch
+    s.small[2:3, :] = jnp.sum(grad_branch.astype(F32), 0, keepdims=True)
+    grads.right_copy(5).start()
+    grads.take_left(4, lefts[4])
+    for part in range(4):
+        grads.right_copy(1 + part).wait_recv()
+        grads.multiply(4 + part)
+    loaded(l_rest)
+    grad_context = dot_nt(grad_branch, s.weight_a[3 * width :, :]).astype(BF16)
+    s.grad_context[...] = grad_context
+    s.grad_context_t[...] = grad_context.T
+    grads.take_left(5, lefts[5])
+    grads.right_copy(5).wait_recv()
+    grads.multiply(8)
+    for unit in range(3):
+        grads.gather(unit)
+    grads.hop(0, 0)
+    grads.hop(1, 0)
+    grads.hop(0, 1)
+    loaded(l_query, l_context_t, l_keys_t, l_values)
+
+    def kv_copy(pair, kind):
+        source, target, to = (
+            (s.kv_out.at[pair, route.mate_quarter], s.kv_mate.at[pair, 0], place.mate),
+            (s.kv_out.at[pair, route.far_quarter], s.kv_mate.at[pair, 1], place.mate),
+            (s.kv_out.at[pair, route.pair_quarter], s.kv_pair.at[pair], route.pair),
+        )[kind]
+        return remote(source, target, s.kv_send.at[pair, kind], s.kv_recv.at[pair, kind], to)
+
+    def kv_second(pair):
+        kv_copy(pair, 1).wait_recv()
+        s.kv_out[pair, route.pair_quarter] = (
+            s.kv_out[pair, route.pair_quarter].astype(F32) + s.kv_mate[pair, 1].astype(F32)
+        ).astype(BF16)
+        kv_copy(pair, 2).start()
+
+    def kv_third(pair):
+        kv_copy(pair, 0).wait_recv()
+        kv_copy(pair, 2).wait_recv()
+        summed = (
+            s.kv_out[pair, route.quarter].astype(F32)
+            + s.kv_mate[pair, 0].astype(F32)
+            + s.kv_pair[pair].astype(F32)
+        ).astype(BF16)
+        lanes = pl.ds(pl.multiple_of(2 * head * pair, 2 * head), 2 * head)
+        s.right[7, :rows, lanes] = summed[:, : 2 * head]
+        s.right[8, :rows, lanes] = summed[:, 2 * head :]
+
+    left_half = iota((rows, 2 * head), 1) < head
+    scale = head**-0.5
+
+    def pair_of_heads(pair, carry):
+        @pl.when(pair < pairs - 1)
+        def _():
+            probs_copy(pair + 1).start()
+            grads.pass_on(pair + 4)
+
+        grads.gather(pair + 3)
+        for step in range(3):
+            grads.hop(pair + 2 - step, step)
+
+        @pl.when(pair > 0)
+        def _():
+            grads.finish(pair - 1)
+            kv_second(pair - 1)
+
+        @pl.when(pair > 1)
+        def _():
+            kv_third(pair - 2)
+
+        probs_copy(pair).wait()
+        slot = pair % 2
+        lanes = pl.ds(pl.multiple_of(2 * head * pair, 2 * head), 2 * head)
+        both_c = s.grad_context[:, lanes]
+        both_q = s.query[:, lanes]
+        chosen_c, chosen_q, delta, grad_q = [], [], [], []
+        for side in range(2):
+            keep_lane = left_half if side == 0 else jnp.logical_not(left_half)
+            chosen_c.append(jnp.where(keep_lane, both_c, jnp.zeros_like(both_c)))
+            chosen_q.append(jnp.where(keep_lane, both_q, jnp.zeros_like(both_q)))
+            down = pl.ds(pl.multiple_of(head * (2 * pair + side), head), head)
+            delta.append(
+                jnp.sum(
+                    s.grad_context_t[down, :].astype(F32) * s.context_t[down, :].astype(F32),
+                    0,
+                    keepdims=True,
+                )
+            )
+            grad_q.append(jnp.zeros((head, rows), F32))
+        for quarter in range(4):
+            value = s.values[quarter, :, lanes]
+            grad_k = jnp.zeros((rows, 2 * head), F32)
+            grad_v = jnp.zeros((rows, 2 * head), F32)
+            for side in range(2):
+                down = pl.ds(pl.multiple_of(head * (2 * pair + side), head), head)
+                probs = s.probs[slot, side, quarter]
+                grad_probs = dot_nt(value, chosen_c[side])
+                grad_scores = (probs.astype(F32) * (grad_probs - delta[side])).astype(BF16)
+                grad_v = grad_v + dot(probs, chosen_c[side])
+                grad_k = grad_k + dot(grad_scores, chosen_q[side])
+                grad_q[side] = grad_q[side] + dot(s.keys_t[quarter, down, :], grad_scores)
+            s.kv_out[pair, quarter, :, : 2 * head] = grad_k.astype(BF16)
+            s.kv_out[pair, quarter, :, 2 * head :] = grad_v.astype(BF16)
+        kv_copy(pair, 0).start()
+        kv_copy(pair, 1).start()
+        for side in range(2):
+            down = pl.ds(pl.multiple_of(head * (2 * pair + side), head), head)
+            s.grad_query_t[down, :] = (grad_q[side] * scale).astype(BF16)
+        return carry
+
+    lax.fori_loop(0, pairs, pair_of_heads, 0)
+    grad_query = s.grad_query_t[...].T
+    s.right[6, :rows, :] = grad_query
+    s.small[0:1, :] = jnp.sum(grad_query.astype(F32), 0, keepdims=True)
+    grads.right_copy(6).start()
+    kv_second(pairs - 1)
+    kv_third(pairs - 2)
+    grads.finish(5)
+    grads.hop(8, 0)
+    grads.hop(7, 1)
+    grads.hop(6, 2)
+    grads.take_left(6, lefts[6])
+    grads.right_copy(6).wait_recv()
+    grads.multiply(9)
+    kv_third(pairs - 1)
+    grads.right_copy(7).start()
+    grads.right_copy(8).start()
+    grad_value = s.right[8, :rows, :]
+    s.small[1:2, :] = jnp.sum(grad_value.astype(F32), 0, keepdims=True)
+
+    def sum_copy(stage, to):
+        return remote(
+            s.small if stage == 0 else s.sums.at[stage - 1],
+            s.got_sums.at[stage],
+            s.sum_send.at[stage],
+            s.sum_recv.at[stage],
+            to,
+        )
+
+    sum_copies = [
+        sum_copy(stage, to) for stage, to in enumerate((place.mate, place.across, place.along))
+    ]
+    sum_copies[0].start()
+    for unit in (10, 11):
+        grads.right_copy(unit - 3).wait_recv()
+        grads.multiply(unit)
+    sum_copies[0].wait_recv()
+    s.sums[0] = s.small[...] + s.got_sums[0]
+    sum_copies[1].start()
+    grads.pass_on(9)
+    grad_input = (
+        s.grad_res[...]
+        + dot_nt(s.right[6, :rows, :], s.weight_a[2 * width : 3 * width, :])
+        + dot_nt(s.right[7, :rows, :], s.weight_a[:width, :])
+        + dot_nt(grad_value, s.weight_a[width : 2 * width, :])
+    )
+    send_back(1, grad_input.astype(BF16))
+    grads.pass_on(10)
+    grads.pass_on(11)
+    sum_copies[1].wait_recv()
+    s.sums[1] = s.sums[0] + s.got_sums[1]
+    sum_copies[2].start()
+    grads.gather(9)
+    grads.hop(9, 0)
+    grads.hop(8, 1)
+    grads.hop(7, 2)
+    grads.finish(6)
+    grads.gather(10)
+    sum_copies[2].wait_recv()
+    s.sums[2] = s.sums[1] + s.got_sums[2]
+
+    def z_copy(step):
+        other = (place.z + step) % z_size
+        return remote(
+            s.sums.at[2],
+            s.got_z.at[place.z],
+            s.sum_send.at[2 + step],
+            s.sum_recv.at[2 + step],
+            {"ctx": other},
+        )
+
+    for step in range(1, z_size):
+        z_copy(step).start()
+    s.got_z[place.z] = s.sums[2]
+    take_back(0)
+    grads.hop(10, 0)
+    grads.hop(9, 1)
+    grads.hop(8, 2)
+    grads.finish(7)
+    grads.gather(11)
+    grads.hop(11, 0)
+    grads.hop(10, 1)
+    grads.hop(9, 2)
+    grads.finish(8)
+    take_back(1)
+    home_copy = pltpu.make_async_copy(s.homes, out_homes, s.probs_sem.at[0])
+    home_copy.start()
+    grads.hop(11, 1)
+    grads.hop(10, 2)
+    grads.finish(9)
+    for step in range(1, z_size):
+        z_copy(step).wait_recv()
+    total = s.got_z[0]
+    for z in range(1, z_size):
+        total = total + s.got_z[z]
+    out_small[...] = total
+    grads.hop(11, 2)
+    grads.finish(10)
+    grads.finish(11)
+
+    grads.drain(lefts)
+    for pair in range(pairs):
+        for kind in range(3):
+            kv_copy(pair, kind).wait_send()
+    for which in range(2):
+        each_other(route.home, lambda other: back_copy(which, other).wait_send())
+    for copy in sum_copies:
+        copy.wait_send()
+    for step in range(1, z_size):
+        z_copy(step).wait_send()
+    home_copy.wait()
+
+
+def encoder_backward(z_size, kept):
+    rows, width = kept.query.shape
+    blocks = 8 * z_size
+    scratch = {name: make(rows, width, blocks) for name, make in BACKWARD_SCRATCH.items()}
+    vmem, anywhere = pl.BlockSpec(memory_space=pltpu.VMEM), pl.BlockSpec(memory_space=pl.ANY)
+    return pl.pallas_call(
+        partial(backward_kernel, z_size),
+        out_shape=(
+            jax.ShapeDtypeStruct((UNITS, BLOCK, width), F32),
+            jax.ShapeDtypeStruct((2, rows, width), BF16),
+            jax.ShapeDtypeStruct((16, width), F32),
+        ),
+        in_specs=[anywhere] * len(Kept._fields),
+        out_specs=(anywhere, anywhere, vmem),
+        scratch_shapes=list(scratch.values()),
+        compiler_params=pltpu.CompilerParams(
+            collective_id=1, has_side_effects=True, vmem_limit_bytes=62 * 2**20
+        ),
+        name="encoder_backward",
+    )(*kept)
 
 
 norm_eps = 1e-12
@@ -408,6 +1651,87 @@
     )
 
 
+def per_device_fast(
+    tokens,
+    cotangent,
+    token_order,
+    sequence_ids,
+    valid,
+    teacher,
+    w_query,
+    b_query,
+    w_key,
+    w_value,
+    b_value,
+    w_out,
+    b_out,
+    norm1_gain,
+    norm1_bias,
+    w_up,
+    b_up,
+    w_down,
+    b_down,
+    norm2_gain,
+    norm2_bias,
+):
+    rows, width = tokens.shape
+    z_size = lax.axis_size("ctx")
+    ints = jnp.stack([token_order, valid])
+    ids = sequence_ids.reshape(z_size, 1, rows)
+    narrow = jnp.stack(
+        [b_query, b_value, b_out, norm1_gain, norm1_bias, b_down, norm2_gain, norm2_bias]
+    )
+    pieces = jnp.concatenate(
+        [
+            jnp.pad(narrow, ((0, 0), (0, 3 * BLOCK))),
+            b_up[None],
+            jnp.zeros((7, 4 * BLOCK), BF16),
+        ]
+    )
+    kept = encoder_forward(
+        z_size,
+        ints,
+        ids,
+        tokens,
+        cotangent,
+        teacher,
+        pieces,
+        w_query,
+        w_key,
+        w_value,
+        w_out,
+        w_up,
+        w_down,
+    )
+    grads, homes, small = encoder_backward(z_size, kept)
+    dp_index = lax.axis_index("dp")
+    own = lax.dynamic_slice_in_dim(small[:8], dp_index * BLOCK, BLOCK, axis=1)
+    own_up = lax.dynamic_slice_in_dim(
+        small[8:12].reshape(-1), dp_index * 4 * BLOCK, 4 * BLOCK
+    )
+    homes = homes.astype(F32)
+    return (
+        homes[0],
+        jnp.sum(small[12]),
+        homes[1],
+        grads[9],
+        own[0],
+        grads[10],
+        grads[11],
+        own[1],
+        grads[8],
+        own[2],
+        own[3],
+        own[4],
+        jnp.concatenate(list(grads[4:8]), axis=1),
+        own_up,
+        grads[:4].reshape(4 * BLOCK, width),
+        own[5],
+        own[6],
+        own[7],
+    )
+
+
 def solution(mesh):
     in_specs = (
         P(("dp", "ctx"), None),
@@ -452,6 +1776,7 @@
         P("dp"),
         P("dp"),
     )
+    fast = dict(mesh.shape) == {"dp": 8, "ctx": 4}
     return jax.shard_map(
-        per_device, mesh=mesh, in_specs=in_specs, out_specs=out_specs, check_vma=False
-    )
+        per_device_fast if fast else per_device, mesh=mesh, in_specs=in_specs, out_specs=out_specs, check_vma=False
+    )

time: 845 us -> 263 us (0.31)
  waiting for transfers between devices: 469 us -> 0 us
  Pallas kernels: 0 us -> 248 us
  blocking collectives: 126 us -> 0 us
  matrix products: 99.4 us -> 0 us
  local copies, waits for them, and re-layouts: 54.6 us -> 9.38 us
  other arithmetic: 43.8 us -> 3.79 us
  between operations: 20 us -> 0.69 us
  starting transfers between devices: 15.5 us -> 0 us
    reduce_scatter x8 -> x0, waiting for transfers between devices: 319 us -> none  [the longest x1 57.6 us: per_device(): lax.psum_scatter(grad_down.astype(jnp.bfloat16), 'dp', scatter_dimension=...]
    pallas_call x0 -> x2, Pallas kernels: none -> 248 us  [the longest x1 135 us: encoder_backward(): pl.pallas_call(partial(backward_kernel, z_size), out_shape=(jax.ShapeDtyp...]
    all_gather x8 -> x0, waiting for transfers between devices: 121 us -> none  [the longest x1 31.3 us: per_device(): value_piece = lax.all_gather(values, 'ctx', axis=0, tiled=True)]
    dot_general x32 -> x0, matrix products: 99.4 us -> none  [the longest x6 24.9 us: product(): return jnp.dot(left, right, preferred_element_type=jnp.float32)]
    psum x2 -> x0, blocking collectives: 51.6 us -> none  [the longest x1 39.8 us: per_device(): lax.psum(jnp.sum(valid_rows[:, None] * difference * difference), ('dp', '...]
    unnamed x2 -> x0, blocking collectives: 51.2 us -> none
    psum x1 -> x0, waiting for transfers between devices: 25 us -> none  [per_device(): lax.psum(attn_shards[0].astype(jnp.bfloat16), 'ctx').astype(jnp.float32)]
    convert_element_type x26 -> x1, other arithmetic: 17.7 us -> 0.11 us  [per_device_fast(): homes = homes.astype(F32)]
  transfers between devices with their start and end apart: 21 -> 0, of which waited for: 13 -> 0; matrix products, arithmetic and copies ran while one was open for 15% -> 0% of each run, Pallas kernels for 0% -> 0%
where the time goes in v2:
time: 263 us; the launch traced here: 262 us
  Pallas kernels  248 us (94%)
  local copies, waits for them, and re-layouts  9.38 us (4%)
  other arithmetic  3.79 us (1%)
    pallas_call x1, Pallas kernels, encoder_backward(): pl.pallas_call(partial(backward_kernel, z_size), out_shape=(jax.ShapeDtyp...  135 us
    pallas_call x1, Pallas kernels, encoder_forward(): pl.pallas_call(partial(forward_kernel, z_size), out_shape=tuple((jax.Shap...  114 us

profile of v2, /device:TPU:0, one launch (start us, length us, event | category | flops | bytes accessed | tf_op | source)
XLA Modules:
  0.0 262.2 jit_solution(12377579476700357237)
XLA Ops:
  0.7 0.8 stack.47
  1.5 0.7 broadcast_in_dim.6
  2.1 0.1 pad.11.clone
  2.2 0.7 fusion.2.pieces
  2.9 1.3 pad_add_fusion.ints
  4.2 113.7 %encoder_forward.1 = (bf16[9216,768]{1,0:T(8,128)(2,1)}, bf16[12,4,256,256]{3,2,1,0:T(8,128)(2,1)}, bf16[4,768,256]{2,1,0:T(8,128)(2,1)}, bf16[4,256,768]{2,1,0:...) custom-call(s32[2,256]{1,0:T(2,128)} %pad_add_fusion.ints, ...), custom_call_target="tpu_custom_call" | custom-call | tf_op jit(solution)/shard_map/encoder_forward/pallas_call | solution.py:642
  117.9 134.7 %encoder_backward.1 = (f32[12,96,768]{2,1,0:T(8,128)}, bf16[2,256,768]{2,1,0:T(8,128)(2,1)}, f32[16,768]{1,0:T(8,128)}) custom-call(bf16[9216,768]{1,0:T(8,128)(2,1)} %get-tuple-element.38.refs_0_, bf16[12,4,256,256]{3,2,1,0:T(8,128)(2,1)} %get-tuple-element.39.refs_1_, bf16[4,768,256]{2,1,0:T(8,128)(2,1)} %get-tuple-element.40.refs_2_, ...), custom_call_target="tpu_custom_call" | custom-call | tf_op jit(solution)/shard_map/encoder_backward/pallas_call | solution.py:1238
  252.6 2.7 %slice_bitcast_fusion.5 = (f32[96,768]{1,0:T(8,128)S(1)}, f32[96,768]{1,0:T(8,128)S(1)}, f32[96,768]{1,0:T(8,128)S(1)}, f32[96,768]{1,0:T(8,128)S(1)}, f32[96,76...) fusion(f32[12,96,768]{2,1,0:T(8,128)} %get-tuple-element.57), kind=kLoop, calls=%fused_computation.6 | loop fusion | bytes 4718592 | tf_op jit(solution)/shard_map/unstack | solution.py:1726
  255.2 0.0 copy-start
  255.2 1.1 pad_maximum_fusion
  256.4 0.3 copy-done
  256.6 0.1 convert_element_type.5
  256.7 1.2 slice_bitcast_fusion
  258.0 0.0 copy-start.1
  258.0 2.4 slice.73
  260.3 0.0 copy-done.1
  260.4 0.1 constant_dynamic-slice_fusion
  260.4 0.5 slice_bitcast_fusion.10
  261.0 0.7 dynamic_slice.7
  261.6 0.6 slice_reduce_fusion
  (4 shorter events, 0.0 us)
Async XLA Ops:
  255.2 1.4 copy-start
  258.0 2.4 copy-start.1

commit v3 on v2

--- a/solution.py
+++ b/solution.py
@@ -176,14 +176,13 @@
     ids=lambda t, w, b: pltpu.VMEM((2, 4, 1, t), jnp.int32),
     pieces=lambda t, w, b: pltpu.VMEM((8, 16, w // 2), BF16),
     vectors=lambda t, w, b: pltpu.VMEM((16, w), F32),
-    pack_out=lambda t, w, b: pltpu.VMEM((2 * t, w), BF16),
-    pack_in=lambda t, w, b: pltpu.VMEM((2 * t, w), BF16),
+    pack_out=lambda t, w, b: pltpu.VMEM((2, b, t // b, w), BF16),
+    pack_in=lambda t, w, b: pltpu.VMEM((2, b, t // b, w), BF16),
     teach_out=lambda t, w, b: pltpu.VMEM((t, w), BF16),
     teach_in=lambda t, w, b: pltpu.VMEM((t, w), BF16),
     full=lambda t, w, b: pltpu.VMEM((12 * w, w), BF16),
-    packed=lambda t, w, b: pltpu.VMEM((t, w), BF16),
-    packed_t=lambda t, w, b: pltpu.VMEM((w, t), BF16),
-    cot=lambda t, w, b: pltpu.VMEM((t, w), BF16),
+    packed=lambda t, w, b: pltpu.VMEM((4, t, w), BF16),
+    packed_t=lambda t, w, b: pltpu.VMEM((2, w, t), BF16),
     query=lambda t, w, b: pltpu.VMEM((t, w), BF16),
     keys=lambda t, w, b: pltpu.VMEM((4, t, w), BF16),
     values_t=lambda t, w, b: pltpu.VMEM((4, w, t), BF16),
@@ -210,8 +209,8 @@
     ints_recv=lambda t, w, b: pltpu.SemaphoreType.DMA((b,)),
     piece_send=lambda t, w, b: pltpu.SemaphoreType.DMA((8,)),
     piece_recv=lambda t, w, b: pltpu.SemaphoreType.DMA((8,)),
-    pack_send=lambda t, w, b: pltpu.SemaphoreType.DMA((b,)),
-    pack_recv=lambda t, w, b: pltpu.SemaphoreType.DMA((b,)),
+    pack_send=lambda t, w, b: pltpu.SemaphoreType.DMA((2, b)),
+    pack_recv=lambda t, w, b: pltpu.SemaphoreType.DMA((2, b)),
     misc_send=lambda t, w, b: pltpu.SemaphoreType.DMA((8,)),
     misc_recv=lambda t, w, b: pltpu.SemaphoreType.DMA((8,)),
     weight_send=lambda t, w, b: pltpu.SemaphoreType.DMA((UNITS, 8)),
@@ -303,11 +302,6 @@
         lax.fori_loop(1, blocks, one, 0)
 
     each_other(route.home, lambda other: ints_copy(other).start())
-    for copy in own_copies[:2]:
-        copy.wait()
-    weights.begin(0)
-    weights.begin(1)
-
     def piece_copy(step):
         other = (place.dp + step) % 8
         return remote(
@@ -324,6 +318,10 @@
     ids_copy = remote(ids, s.ids.at[1], s.misc_send.at[0], s.misc_recv.at[0], place.mate)
     ids_copy.start()
     s.ids[0] = ids[...]
+    for copy in own_copies[:2]:
+        copy.wait()
+    weights.begin(0)
+    weights.begin(1)
     for copy in own_copies[2:]:
         copy.wait()
 
@@ -345,60 +343,59 @@
         picked = jnp.sum(jnp.where(mine & (rank == k), local, 0.0), 1, keepdims=True)
         slots = jnp.where(iota((blocks, 128), 1) == k, picked, slots)
     spread = one_hot(
-        lax.shift_right_logical(iota((2 * rows, blocks), 0), 4) == iota((2 * rows, blocks), 1)
-    )
-    slot_rows = dot(spread, slots.astype(BF16))
-    slot = iota((2 * rows, 128), 0)
+        lax.shift_right_logical(iota((rows, blocks), 0), 3) == iota((rows, blocks), 1)
+    )
     picked = jnp.sum(
-        jnp.where(iota((2 * rows, 128), 1) == (slot & 7), slot_rows, 0.0), 1, keepdims=True
-    )
-    lane = iota((2 * rows, rows), 1).astype(F32)
-    first = (iota((2 * rows, rows), 0) & 8) == 0
-    hit = lane == picked
-    s.pack_out[...] = (
-        dot(one_hot(hit & first), tokens[...])
-        + dot(one_hot(hit & jnp.logical_not(first)), cotangent[...])
-    ).astype(BF16)
-    spread8 = one_hot(
-        lax.shift_right_logical(iota((rows, blocks), 0), 3) == iota((rows, blocks), 1)
-    )
-    slot8 = jnp.sum(
         jnp.where(
             iota((rows, 128), 1) == (iota((rows, 128), 0) & 7),
-            dot(spread8, slots.astype(BF16)),
+            dot(spread, slots.astype(BF16)),
             0.0,
         ),
         1,
         keepdims=True,
     )
-    diagonal = iota((rows, rows), 0) == iota((rows, rows), 1)
-    s.routes[1:2, :] = jnp.sum(jnp.where(diagonal, slot8, 0.0), 0, keepdims=True)
-
-    def span(block):
-        return pl.ds(pl.multiple_of(16 * block, 16), 16)
-
-    def pack_copy(block):
+    lane = iota((rows, rows), 1)
+    diagonal = iota((rows, rows), 0) == lane
+    ordered = one_hot(lane.astype(F32) == picked)
+
+    def pack_copy(which, block):
         return remote(
-            s.pack_out.at[span(block), :],
-            s.pack_in.at[span(route.home), :],
-            s.pack_send.at[block],
-            s.pack_recv.at[route.home],
+            s.pack_out.at[which, block],
+            s.pack_in.at[which, route.home],
+            s.pack_send.at[which, block],
+            s.pack_recv.at[which, route.home],
             route.worker(block),
         )
 
-    def pack_arrival(other):
-        ref = s.pack_in.at[span(other), :]
-        return remote(ref, ref, s.pack_send.at[other], s.pack_recv.at[other], route.owner(other))
-
-    each_other(route.block, lambda block: pack_copy(block).start())
-    s.pack_in[span(route.home), :] = s.pack_out[span(route.block), :]
+    def pack_arrival(which, other):
+        ref = s.pack_in.at[which, other]
+        return remote(
+            ref, ref, s.pack_send.at[which, other], s.pack_recv.at[which, other], route.owner(other)
+        )
+
+    def pack(which, value):
+        s.pack_out[which] = (
+            dot(ordered, value).reshape(blocks, per_block, width).astype(BF16)
+        )
+
+    def send_pack(which):
+        each_other(route.block, lambda block: pack_copy(which, block).start())
+        s.pack_in[which, route.home] = s.pack_out[which, route.block]
+
+    def take_pack(which):
+        each_other(route.home, lambda other: pack_arrival(which, other).wait_recv())
+        flat = s.pack_in[which].astype(F32).reshape(rows, width).astype(BF16)
+        return dot(one_hot(lane.astype(F32) == place_col), flat).astype(BF16)
+
+    pack(0, tokens[...])
+    send_pack(0)
     weights.tick(2)
+    pack(1, cotangent[...])
+    s.routes[1:2, :] = jnp.sum(jnp.where(diagonal, picked, 0.0), 0, keepdims=True)
 
     moved_to = route.worker(route.home)
     stays = route.block == route.home
-    teach_copy = remote(
-        s.teach_out, s.teach_in, s.misc_send.at[1], s.misc_recv.at[1], moved_to
-    )
+    teach_copy = remote(s.teach_out, s.teach_in, s.misc_send.at[1], s.misc_recv.at[1], moved_to)
 
     for step in range(1, 8):
         piece_copy(step).wait_recv()
@@ -428,82 +425,86 @@
         jnp.where(same & jnp.logical_not(before | diagonal), 1.0, 0.0), 0, keepdims=True
     )
     s.routes[0:1, :] = source_row * 8 + rank_row
-    wide = iota((rows, 2 * rows), 1).astype(F32)
-    place_col = source_col * 16 + rank_col
-    each_other(route.home, lambda other: pack_arrival(other).wait_recv())
-    s.packed[...] = dot(one_hot(wide == place_col), s.pack_in[...]).astype(BF16)
-    s.cot[...] = dot(one_hot(wide == place_col + 8), s.pack_in[...]).astype(BF16)
-    s.packed_t[...] = s.packed[...].T
-    keep(s.packed_t, outs.packed_t)
-    weights.tick(3)
-    weights.tick(4)
-    weights.tick(5)
-
-    def kv_copy(kind):
-        buffer, half = (s.keys, s.values_t)[kind // 3], kind % 3
+    place_col = source_col * 8 + rank_col
+    from_own = place.core == route.group_core
+    query_row = jnp.where(from_own, s.ids[0, route.quarter], s.ids[1, route.quarter]).astype(F32)
+    for quarter in range(4):
+        key_row = jnp.where(from_own, s.ids[0, quarter], s.ids[1, quarter]).astype(F32)
+        s.mask[quarter] = jnp.where(column(key_row) == query_row, 0.0, -1e30)
+
+    def rows_copy(kind, arriving):
         quarter, to = (
             (route.quarter, route.pair),
             (route.quarter, place.mate),
             (route.pair_quarter, place.mate),
-        )[half]
-        ref = buffer.at[quarter]
+        )[kind]
+        if arriving:
+            quarter = (route.pair_quarter, route.mate_quarter, route.far_quarter)[kind]
+        ref = s.packed.at[quarter]
         return remote(ref, ref, s.misc_send.at[2 + kind], s.misc_recv.at[2 + kind], to)
 
-    def kv_arrival(kind):
-        buffer, half = (s.keys, s.values_t)[kind // 3], kind % 3
-        quarter = (route.pair_quarter, route.mate_quarter, route.far_quarter)[half]
-        ref = buffer.at[quarter]
-        to = (route.pair, place.mate, place.mate)[half]
-        return remote(ref, ref, s.misc_send.at[2 + kind], s.misc_recv.at[2 + kind], to)
-
-    packed = s.packed[...]
+    packed = take_pack(0)
+    s.packed[route.quarter] = packed
+    s.packed_t[0] = packed.T
+    rows_copy(0, False).start()
+    rows_copy(1, False).start()
+    weights.tick(3)
+    send_pack(1)
+
+    @pl.when(jnp.logical_not(stays))
+    def _():
+        teach_copy.start()
+
+    @pl.when(stays)
+    def _():
+        s.teach_in[...] = s.teach_out[...]
+
+    weights.tick(4)
+    weights.tick(5)
 
     def whole(unit):
         return full[width * unit : width * (unit + 1), :]
 
+    def keys_values(quarter):
+        value = s.packed[quarter]
+        keys = dot(value, whole(0)).astype(BF16)
+        s.keys[quarter] = keys
+        s.keys_t[quarter] = keys.T
+        values = (dot(value, whole(1)) + vector(1)).astype(BF16)
+        s.values[quarter] = values
+        s.values_t[quarter] = values.T
+
+    rows_copy(0, True).wait_recv()
+    rows_copy(2, False).start()
     weights.ready(0)
-    s.keys[route.quarter] = dot(packed, whole(0)).astype(BF16)
     weights.ready(1)
-    values = (dot(packed, whole(1)) + vector(1)).astype(BF16)
-    kv_copy(0).start()
-    kv_copy(1).start()
-    s.values_t[route.quarter] = values.T
+    keys_values(route.quarter)
+    rows_copy(1, True).wait_recv()
+    keys_values(route.mate_quarter)
+    weights.tick(6)
+    s.packed_t[1] = s.packed[route.pair_quarter].T
+    keep(s.packed_t, outs.packed_t)
+    keys_values(route.pair_quarter)
+    rows_copy(2, True).wait_recv()
+    keys_values(route.far_quarter)
     weights.ready(2)
     scale = (width // HEADS) ** -0.5
     s.query[...] = (
         (dot(packed, whole(2)) + vector(0)).astype(BF16).astype(F32) * scale
     ).astype(BF16)
-    kv_copy(3).start()
-    kv_copy(4).start()
     keep(s.query, outs.query)
-
-    @pl.when(jnp.logical_not(stays))
-    def _():
-        teach_copy.start()
-
-    @pl.when(stays)
-    def _():
-        s.teach_in[...] = s.teach_out[...]
-
-    from_own = place.core == route.group_core
-    query_row = jnp.where(
-        from_own, s.ids[0, route.quarter], s.ids[1, route.quarter]
-    ).astype(F32)
-    for quarter in range(4):
-        key_row = jnp.where(from_own, s.ids[0, quarter], s.ids[1, quarter]).astype(F32)
-        s.mask[quarter] = jnp.where(column(key_row) == query_row, 0.0, -1e30)
-    kv_arrival(0).wait_recv()
-    kv_copy(2).start()
-    kv_arrival(3).wait_recv()
-    kv_copy(5).start()
-    for kind in (1, 2, 4, 5):
-        kv_arrival(kind).wait_recv()
+    keep(s.keys_t, outs.keys_t)
+    keep(s.values, outs.values)
+    weights.tick(7)
 
     head = width // HEADS
     left_half = iota((rows, 2 * head), 1) < head
 
     def pair_of_heads(pair, carry):
-        weights.tick(pair + 6)
+        @pl.when(pair % 2 == 0)
+        def _():
+            weights.tick(pair // 2 + 8)
+
         lanes = pl.ds(pl.multiple_of(2 * head * pair, 2 * head), 2 * head)
         both = s.query[:, lanes]
         for side in range(2):
@@ -533,12 +534,11 @@
     lax.fori_loop(0, HEADS // 2, pair_of_heads, 0)
     keep(s.probs, outs.probs)
     keep(s.context_t, outs.context_t)
-    weights.pass_on(10)
-    weights.corner(9)
+    weights.tick(11)
 
     weights.ready(3)
     branch = dot(s.context_t[...].T, whole(3)) + vector(2)
-    scaled, inverse = normalize(s.packed[...].astype(F32) + branch)
+    scaled, inverse = normalize(packed.astype(F32) + branch)
     s.scaled[...] = scaled
     s.inverse[...] = jnp.broadcast_to(inverse, (rows, 128))
     normed = scaled * vector(3) + vector(4)
@@ -549,12 +549,7 @@
     keep(s.scaled, outs.scaled)
     keep(s.inverse, outs.inverse)
     keep(s.low_t, outs.low_t)
-    weights.pass_on(11)
-    weights.corner(10)
-    weights.corner(11)
-
-    for part in range(4):
-        weights.ready(4 + part)
+
     root_half, norm = 2.0**-0.5, (2.0 * math.pi) ** -0.5
     piece = width // 2
 
@@ -571,17 +566,19 @@
         s.slope[:, wide] = (phi + pre * (norm * jnp.exp(-0.5 * pre * pre))).astype(BF16)
         return carry
 
-    lax.fori_loop(0, 8, up, 0)
+    for part in range(4):
+        weights.ready(4 + part)
+        lax.fori_loop(2 * part, 2 * part + 2, up, 0)
+        if part % 2 == 1:
+            weights.pass_on(10 + part // 2)
+            weights.corner(9 + part // 2)
+    keep(full.at[: 8 * width, :], outs.full.at[: 8 * width, :])
+    weights.corner(11)
     keep(s.act_t, outs.act_t)
     keep(s.slope, outs.slope)
-    for quarter in range(4):
-        s.keys_t[quarter] = s.keys[quarter].T
-        s.values[quarter] = s.values_t[quarter].T
-    keep(s.keys_t, outs.keys_t)
-    keep(s.values, outs.values)
     for part in range(4):
         weights.ready(8 + part)
-    keep(s.full, outs.full)
+    keep(full.at[8 * width :, :], outs.full.at[8 * width :, :])
     ffn = dot(s.act[...], full[8 * width :, :]) + vector(5)
 
     scaled, inverse = normalize(s.normed[...] + ffn)
@@ -598,7 +595,7 @@
     factor = 1.0 / (count * width)
     s.small[...] = jnp.zeros((16, width), F32)
     s.small[12:13, :] = jnp.sum(miss * miss, 0, keepdims=True) * factor
-    grad_out = s.cot[...].astype(F32) + (2.0 * factor) * miss
+    grad_out = take_pack(1).astype(F32) + (2.0 * factor) * miss
     s.small[6:7, :] = jnp.sum(grad_out * scaled, 0, keepdims=True)
     s.small[7:8, :] = jnp.sum(grad_out, 0, keepdims=True)
     s.small[13:14, :] = vector(3)
@@ -619,12 +616,13 @@
 
     weights.drain()
     each_other(route.home, lambda other: ints_copy(other).wait_send())
-    each_other(route.block, lambda block: pack_copy(block).wait_send())
+    for which in range(2):
+        each_other(route.block, lambda block: pack_copy(which, block).wait_send())
     for step in range(1, 8):
         piece_copy(step).wait_send()
     ids_copy.wait_send()
-    for kind in range(6):
-        kv_copy(kind).wait_send()
+    for kind in range(3):
+        rows_copy(kind, False).wait_send()
 
     @pl.when(jnp.logical_not(stays))
     def _():
@@ -728,12 +726,14 @@
         return pl.ds(pl.multiple_of(BLOCK * j, 32), BLOCK)
 
     def multiply(self, unit):
-        place, low, high, s = self.place, self.low, self.high, self.s
+        place, s = self.place, self.s
         s.partial[...] = dot(s.left[LEFT[unit]], s.right[RIGHT[unit]])
         s.out_d[unit] = s.partial[self.part(place.j_d), :].astype(BF16)
         s.out_x[unit] = s.partial[self.part(place.j_x), :].astype(BF16)
         s.out_y[unit] = s.partial[self.part(place.j_y), :].astype(BF16)
         s.total[unit] = s.partial[self.part(place.j_own), :]
+
+    def begin(self, unit):
         for kind in (0, 1, 2, 5):
             self.copy(unit, kind).start()
 
@@ -797,6 +797,18 @@
                 s.total[unit] = s.total[unit] + s.in_z[way, unit].astype(F32)
 
         self.result(unit).start()
+
+    def tick(self, step):
+        def stage(lag, action):
+            if not isinstance(step, int) or 0 <= step - lag < UNITS:
+                action(step - lag)
+
+        stage(0, self.begin)
+        stage(1, self.pass_on)
+        stage(2, self.gather)
+        for hop in range(self.place.z_size - 1):
+            stage(2 + hop, lambda unit: self.hop(unit, hop))
+        stage(1 + self.place.z_size, self.finish)
 
     def drain(self, lefts):
         place = self.place
@@ -930,7 +942,7 @@
         )
 
     probs_copy(0).start()
-    lefts = (given.act_t,) * 4 + (given.low_t, given.context_t, given.packed_t)
+    lefts = (given.act_t,) * 4 + (given.low_t, given.context_t, given.packed_t.at[0])
     route.greet_all()
 
     def each_other(start, action):
@@ -974,11 +986,12 @@
         flat = s.back_in[which].astype(F32).reshape(rows, width).astype(BF16)
         s.homes[which] = dot(placed, flat).astype(BF16)
 
-    for group in range(4):
-        grads.take_left(group, lefts[group])
     grads.right_copy(0).wait_recv()
     for unit in range(4):
+        grads.take_left(unit, lefts[unit])
         grads.multiply(unit)
+        if unit in (0, 3):
+            grads.tick(unit // 3)
 
     loaded(l_routes, l_result)
     send_back(0, s.result[...])
@@ -993,7 +1006,8 @@
         s.small[8 + part : 9 + part, :] = jnp.sum(grad_pre.astype(F32), 0, keepdims=True)
         grad_normed = grad_normed + dot_nt(grad_pre, s.weight_b[block, :])
         grads.right_copy(1 + part).start()
-        grads.pass_on(part)
+        if part % 2 == 1:
+            grads.tick(2 + part // 2)
     l_rest = load(full.at[: 4 * width, :], s.weight_a)
 
     scaled = s.scaled[...]
@@ -1014,6 +1028,8 @@
     for part in range(4):
         grads.right_copy(1 + part).wait_recv()
         grads.multiply(4 + part)
+        if part == 1:
+            grads.tick(4)
     loaded(l_rest)
     grad_context = dot_nt(grad_branch, s.weight_a[3 * width :, :]).astype(BF16)
     s.grad_context[...] = grad_context
@@ -1021,11 +1037,7 @@
     grads.take_left(5, lefts[5])
     grads.right_copy(5).wait_recv()
     grads.multiply(8)
-    for unit in range(3):
-        grads.gather(unit)
-    grads.hop(0, 0)
-    grads.hop(1, 0)
-    grads.hop(0, 1)
+    grads.tick(5)
     loaded(l_query, l_context_t, l_keys_t, l_values)
 
     def kv_copy(pair, kind):
@@ -1062,20 +1074,18 @@
         @pl.when(pair < pairs - 1)
         def _():
             probs_copy(pair + 1).start()
-            grads.pass_on(pair + 4)
-
-        grads.gather(pair + 3)
-        for step in range(3):
-            grads.hop(pair + 2 - step, step)
-
-        @pl.when(pair > 0)
+
+        @pl.when(pair % 2 == 1)
         def _():
-            grads.finish(pair - 1)
-            kv_second(pair - 1)
+            grads.tick(pair // 2 + 6)
 
         @pl.when(pair > 1)
         def _():
-            kv_third(pair - 2)
+            kv_second(pair - 2)
+
+        @pl.when(pair > 3)
+        def _():
+            kv_third(pair - 4)
 
         probs_copy(pair).wait()
         slot = pair % 2
@@ -1122,15 +1132,15 @@
     s.right[6, :rows, :] = grad_query
     s.small[0:1, :] = jnp.sum(grad_query.astype(F32), 0, keepdims=True)
     grads.right_copy(6).start()
-    kv_second(pairs - 1)
-    kv_third(pairs - 2)
-    grads.finish(5)
-    grads.hop(8, 0)
-    grads.hop(7, 1)
-    grads.hop(6, 2)
     grads.take_left(6, lefts[6])
     grads.right_copy(6).wait_recv()
     grads.multiply(9)
+    kv_second(pairs - 2)
+    kv_second(pairs - 1)
+    kv_third(pairs - 4)
+    kv_third(pairs - 3)
+    grads.tick(9)
+    kv_third(pairs - 2)
     kv_third(pairs - 1)
     grads.right_copy(7).start()
     grads.right_copy(8).start()
@@ -1153,10 +1163,10 @@
     for unit in (10, 11):
         grads.right_copy(unit - 3).wait_recv()
         grads.multiply(unit)
+    grads.tick(10)
     sum_copies[0].wait_recv()
     s.sums[0] = s.small[...] + s.got_sums[0]
     sum_copies[1].start()
-    grads.pass_on(9)
     grad_input = (
         s.grad_res[...]
         + dot_nt(s.right[6, :rows, :], s.weight_a[2 * width : 3 * width, :])
@@ -1164,17 +1174,12 @@
         + dot_nt(grad_value, s.weight_a[width : 2 * width, :])
     )
     send_back(1, grad_input.astype(BF16))
-    grads.pass_on(10)
-    grads.pass_on(11)
+    grads.tick(11)
+    take_back(0)
     sum_copies[1].wait_recv()
     s.sums[1] = s.sums[0] + s.got_sums[1]
     sum_copies[2].start()
-    grads.gather(9)
-    grads.hop(9, 0)
-    grads.hop(8, 1)
-    grads.hop(7, 2)
-    grads.finish(6)
-    grads.gather(10)
+    grads.tick(12)
     sum_copies[2].wait_recv()
     s.sums[2] = s.sums[1] + s.got_sums[2]
 
@@ -1191,31 +1196,19 @@
     for step in range(1, z_size):
         z_copy(step).start()
     s.got_z[place.z] = s.sums[2]
-    take_back(0)
-    grads.hop(10, 0)
-    grads.hop(9, 1)
-    grads.hop(8, 2)
-    grads.finish(7)
-    grads.gather(11)
-    grads.hop(11, 0)
-    grads.hop(10, 1)
-    grads.hop(9, 2)
-    grads.finish(8)
+    grads.tick(13)
     take_back(1)
     home_copy = pltpu.make_async_copy(s.homes, out_homes, s.probs_sem.at[0])
     home_copy.start()
-    grads.hop(11, 1)
-    grads.hop(10, 2)
-    grads.finish(9)
+    grads.tick(14)
     for step in range(1, z_size):
         z_copy(step).wait_recv()
     total = s.got_z[0]
     for z in range(1, z_size):
         total = total + s.got_z[z]
     out_small[...] = total
-    grads.hop(11, 2)
-    grads.finish(10)
-    grads.finish(11)
+    grads.tick(15)
+    grads.tick(16)
 
     grads.drain(lefts)
     for pair in range(pairs):

time: 263 us -> 221 us (0.84)
  Pallas kernels: 248 us -> 206 us
    pallas_call x1, Pallas kernels: 114 us -> 89.4 us  [encoder_forward(): pl.pallas_call(partial(forward_kernel, z_size), out_shape=tuple((jax.Shap...]
    pallas_call x1, Pallas kernels: 135 us -> 117 us  [encoder_backward(): pl.pallas_call(partial(backward_kernel, z_size), out_shape=(jax.ShapeDtyp...]
where the time goes in v3:
time: 221 us; the launch traced here: 220 us
  Pallas kernels  206 us (93%)
  local copies, waits for them, and re-layouts  9.38 us (4%)
  other arithmetic  3.79 us (2%)
    pallas_call x1, Pallas kernels, encoder_backward(): pl.pallas_call(partial(backward_kernel, z_size), out_shape=(jax.ShapeDtyp...  117 us
    pallas_call x1, Pallas kernels, encoder_forward(): pl.pallas_call(partial(forward_kernel, z_size), out_shape=tuple((jax.Shap...  89.4 us

profile of v3, /device:TPU:0, one launch (start us, length us, event | category | flops | bytes accessed | tf_op | source)
XLA Modules:
  0.0 220.3 jit_solution(8682601508193243961)
XLA Ops:
  0.7 0.8 stack.47
  1.5 0.7 broadcast_in_dim.6
  2.1 0.1 pad.11.clone
  2.2 0.7 fusion.2.pieces
  2.9 1.3 pad_add_fusion.ints
  4.2 89.4 %encoder_forward.1 = (bf16[9216,768]{1,0:T(8,128)(2,1)}, bf16[12,4,256,256]{3,2,1,0:T(8,128)(2,1)}, bf16[4,768,256]{2,1,0:T(8,128)(2,1)}, bf16[4,256,768]{2,1,0:...) custom-call(s32[2,256]{1,0:T(2,128)} %pad_add_fusion.ints, ...), custom_call_target="tpu_custom_call" | custom-call | tf_op jit(solution)/shard_map/encoder_forward/pallas_call | solution.py:640
  93.6 117.0 %encoder_backward.1 = (f32[12,96,768]{2,1,0:T(8,128)}, bf16[2,256,768]{2,1,0:T(8,128)(2,1)}, f32[16,768]{1,0:T(8,128)}) custom-call(bf16[9216,768]{1,0:T(8,128)(2,1)} %get-tuple-element.38.refs_0_, bf16[12,4,256,256]{3,2,1,0:T(8,128)(2,1)} %get-tuple-element.39.refs_1_, bf16[4,768,256]{2,1,0:T(8,128)(2,1)} %get-tuple-element.40.refs_2_, ...), custom_call_target="tpu_custom_call" | custom-call | tf_op jit(solution)/shard_map/encoder_backward/pallas_call | solution.py:1231
  210.6 2.7 %slice_bitcast_fusion.5 = (f32[96,768]{1,0:T(8,128)S(1)}, f32[96,768]{1,0:T(8,128)S(1)}, f32[96,768]{1,0:T(8,128)S(1)}, f32[96,768]{1,0:T(8,128)S(1)}, f32[96,76...) fusion(f32[12,96,768]{2,1,0:T(8,128)} %get-tuple-element.57), kind=kLoop, calls=%fused_computation.6 | loop fusion | bytes 4718592 | tf_op jit(solution)/shard_map/unstack | solution.py:1719
  213.2 0.0 copy-start
  213.2 1.1 pad_maximum_fusion
  214.4 0.3 copy-done
  214.6 0.1 convert_element_type.5
  214.8 1.2 slice_bitcast_fusion
  216.0 0.0 copy-start.1
  216.0 2.4 %slice.73 = f32[4,96,768]{2,1,0:T(8,128)} slice(f32[12,96,768]{2,1,0:T(8,128)} %get-tuple-element.57), slice={[0:4], [0:96], [0:768]} | slice | bytes 2359296 | tf_op jit(solution)/shard_map/slice | solution.py:1721
  218.4 0.0 copy-done.1
  218.4 0.1 constant_dynamic-slice_fusion
  218.4 0.5 slice_bitcast_fusion.10
  219.0 0.7 dynamic_slice.7
  219.7 0.6 slice_reduce_fusion
  (4 shorter events, 0.0 us)
Async XLA Ops:
  213.2 1.4 copy-start
  216.0 2.4 %copy-start.1 = (f32[16,768]{1,0:T(8,128)S(1)}, f32[16,768]{1,0:T(8,128)}, u32[]{:S(2)}) copy-start(f32[16,768]{1,0:T(8,128)} %get-tuple-element.56) | copy-start | bytes 147460

commit v4 on v3

--- a/solution.py
+++ b/solution.py
@@ -653,8 +653,8 @@
     return Kept(*results)
 
 
-LEFT = (0, 1, 2, 3, 4, 4, 4, 4, 5, 6, 6, 6)
-RIGHT = (0, 0, 0, 0, 1, 2, 3, 4, 5, 6, 7, 8)
+LEFT = (0, 1, 2, 3, 4, 4, 4, 4, 5)
+RIGHT = (0, 0, 0, 0, 1, 2, 3, 4, 5, 6)
 
 
 class Grads:
@@ -671,18 +671,28 @@
         return pl.ds(pl.multiple_of(BLOCK * shard, 32), BLOCK)
 
     def left_copy(self, group, j, source):
+        if group < 6:
+            target = self.s.left.at[group, BLOCK * j : BLOCK * (j + 1), self.tok_rows :]
+        else:
+            first = self.tok_rows * (group - 4)
+            target = self.s.left_x.at[BLOCK * j : BLOCK * (j + 1), first : first + self.tok_rows]
         return remote(
             source.at[self.source_rows(group, j, 1 - self.place.core), :],
-            self.s.left.at[group, BLOCK * j : BLOCK * (j + 1), self.tok_rows :],
+            target,
             self.s.left_send.at[group, j],
             self.s.left_recv.at[group, j],
             self.place.mate,
         )
 
     def left_own(self, group, j, source):
+        if group < 6:
+            target = self.s.left.at[group, BLOCK * j : BLOCK * (j + 1), : self.tok_rows]
+        else:
+            first = self.tok_rows * (group - 6)
+            target = self.s.left_x.at[BLOCK * j : BLOCK * (j + 1), first : first + self.tok_rows]
         return pltpu.make_async_copy(
             source.at[self.source_rows(group, j, self.place.core), :],
-            self.s.left.at[group, BLOCK * j : BLOCK * (j + 1), : self.tok_rows],
+            target,
             self.s.left_own.at[group, j],
         )
 
@@ -700,9 +710,15 @@
         return self.s.right.at[index, : self.tok_rows, :]
 
     def right_copy(self, index):
+        if index < 7:
+            source, target = self.own_right(index), self.s.right.at[index, self.tok_rows :, :]
+        else:
+            half = 2 * self.tok_rows
+            source = self.s.right_kv.at[index - 7, :half, :]
+            target = self.s.right_kv.at[index - 7, half:, :]
         return remote(
-            self.own_right(index),
-            self.s.right.at[index, self.tok_rows :, :],
+            source,
+            target,
             self.s.right_send.at[index],
             self.s.right_recv.at[index],
             self.place.mate,
@@ -727,7 +743,15 @@
 
     def multiply(self, unit):
         place, s = self.place, self.s
-        s.partial[...] = dot(s.left[LEFT[unit]], s.right[RIGHT[unit]])
+        if unit < 9:
+            s.partial[...] = dot(s.left[LEFT[unit]], s.right[RIGHT[unit]])
+        elif unit == 9:
+            n = self.tok_rows
+            s.partial[...] = dot(s.left_x[:, :n], s.right[6, :n, :]) + dot(
+                s.left_x[:, 2 * n : 3 * n], s.right[6, n:, :]
+            )
+        else:
+            s.partial[...] = dot(s.left_x[...], s.right_kv[unit - 10])
         s.out_d[unit] = s.partial[self.part(place.j_d), :].astype(BF16)
         s.out_x[unit] = s.partial[self.part(place.j_x), :].astype(BF16)
         s.out_y[unit] = s.partial[self.part(place.j_y), :].astype(BF16)
@@ -798,17 +822,14 @@
 
         self.result(unit).start()
 
-    def tick(self, step):
-        def stage(lag, action):
-            if not isinstance(step, int) or 0 <= step - lag < UNITS:
-                action(step - lag)
-
-        stage(0, self.begin)
-        stage(1, self.pass_on)
-        stage(2, self.gather)
-        for hop in range(self.place.z_size - 1):
-            stage(2 + hop, lambda unit: self.hop(unit, hop))
-        stage(1 + self.place.z_size, self.finish)
+    def line(self, *work):
+        for unit, stage in work:
+            if stage == 0:
+                self.gather(unit)
+            if stage < self.place.z_size - 1:
+                self.hop(unit, stage)
+            else:
+                self.finish(unit)
 
     def drain(self, lefts):
         place = self.place
@@ -829,7 +850,7 @@
             return carry
 
         lax.fori_loop(0, UNITS, one, 0)
-        for group in range(7):
+        for group in range(8):
             for j in range(4):
                 self.left_copy(group, j, lefts[group]).wait_send()
         for index in range(9):
@@ -837,8 +858,10 @@
 
 
 BACKWARD_SCRATCH = dict(
-    left=lambda t, w, b: pltpu.VMEM((7, 4 * BLOCK, 2 * t), BF16),
-    right=lambda t, w, b: pltpu.VMEM((9, 2 * t, w), BF16),
+    left=lambda t, w, b: pltpu.VMEM((6, 4 * BLOCK, 2 * t), BF16),
+    left_x=lambda t, w, b: pltpu.VMEM((4 * BLOCK, 4 * t), BF16),
+    right=lambda t, w, b: pltpu.VMEM((7, 2 * t, w), BF16),
+    right_kv=lambda t, w, b: pltpu.VMEM((2, 4 * t, w), BF16),
     partial=lambda t, w, b: pltpu.VMEM((4 * BLOCK, w), F32),
     out_d=lambda t, w, b: pltpu.VMEM((UNITS, BLOCK, w), BF16),
     out_x=lambda t, w, b: pltpu.VMEM((UNITS, BLOCK, w), BF16),
@@ -868,7 +891,8 @@
     grad_query_t=lambda t, w, b: pltpu.VMEM((w, t), BF16),
     kv_out=lambda t, w, b: pltpu.VMEM((HEADS // 2, 4, t, t), BF16),
     kv_mate=lambda t, w, b: pltpu.VMEM((HEADS // 2, 2, t, t), BF16),
-    kv_pair=lambda t, w, b: pltpu.VMEM((HEADS // 2, t, t), BF16),
+    pair_out=lambda t, w, b: pltpu.VMEM((t, w), BF16),
+    pair_in=lambda t, w, b: pltpu.VMEM((t, w), BF16),
     back_out=lambda t, w, b: pltpu.VMEM((2, b, t // b, w), BF16),
     back_in=lambda t, w, b: pltpu.VMEM((2, b, t // b, w), BF16),
     homes=lambda t, w, b: pltpu.VMEM((2, t, w), BF16),
@@ -877,16 +901,18 @@
     got_z=lambda t, w, b: pltpu.VMEM((b // 8, 16, w), F32),
     send=lambda t, w, b: pltpu.SemaphoreType.DMA((UNITS, 8)),
     recv=lambda t, w, b: pltpu.SemaphoreType.DMA((UNITS, 8)),
-    left_send=lambda t, w, b: pltpu.SemaphoreType.DMA((7, 4)),
-    left_recv=lambda t, w, b: pltpu.SemaphoreType.DMA((7, 4)),
-    left_own=lambda t, w, b: pltpu.SemaphoreType.DMA((7, 4)),
+    left_send=lambda t, w, b: pltpu.SemaphoreType.DMA((8, 4)),
+    left_recv=lambda t, w, b: pltpu.SemaphoreType.DMA((8, 4)),
+    left_own=lambda t, w, b: pltpu.SemaphoreType.DMA((8, 4)),
     right_send=lambda t, w, b: pltpu.SemaphoreType.DMA((9,)),
     right_recv=lambda t, w, b: pltpu.SemaphoreType.DMA((9,)),
     out_sem=lambda t, w, b: pltpu.SemaphoreType.DMA((UNITS,)),
     load_sem=lambda t, w, b: pltpu.SemaphoreType.DMA((20,)),
     probs_sem=lambda t, w, b: pltpu.SemaphoreType.DMA((2,)),
-    kv_send=lambda t, w, b: pltpu.SemaphoreType.DMA((HEADS // 2, 3)),
-    kv_recv=lambda t, w, b: pltpu.SemaphoreType.DMA((HEADS // 2, 3)),
+    kv_send=lambda t, w, b: pltpu.SemaphoreType.DMA((HEADS // 2, 2)),
+    kv_recv=lambda t, w, b: pltpu.SemaphoreType.DMA((HEADS // 2, 2)),
+    pair_send=lambda t, w, b: pltpu.SemaphoreType.DMA((2,)),
+    pair_recv=lambda t, w, b: pltpu.SemaphoreType.DMA((2,)),
     back_send=lambda t, w, b: pltpu.SemaphoreType.DMA((2, b)),
     back_recv=lambda t, w, b: pltpu.SemaphoreType.DMA((2, b)),
     sum_send=lambda t, w, b: pltpu.SemaphoreType.DMA((3 + b // 8,)),
@@ -921,11 +947,11 @@
 
     full = given.full
     l_ffn = load(given.grad_ffn, grads.own_right(0))
+    l_routes = load(given.routes, s.routes)
+    l_result = load(given.result, s.result)
     l_down = load(full.at[2 * 4 * width :, :], s.weight_a)
     l_up = load(full.at[4 * width : 8 * width, :], s.weight_b)
     l_slope = load(given.slope, s.slope)
-    l_routes = load(given.routes, s.routes)
-    l_result = load(given.result, s.result)
     l_small = load(given.small, s.small)
     l_grad_res = load(given.grad_res, s.grad_res)
     l_scaled = load(given.scaled, s.scaled)
@@ -942,7 +968,8 @@
         )
 
     probs_copy(0).start()
-    lefts = (given.act_t,) * 4 + (given.low_t, given.context_t, given.packed_t.at[0])
+    lefts = (given.act_t,) * 4 + (given.low_t, given.context_t)
+    lefts += (given.packed_t.at[0], given.packed_t.at[1])
     route.greet_all()
 
     def each_other(start, action):
@@ -954,7 +981,7 @@
 
     loaded(l_ffn)
     grads.right_copy(0).start()
-    for group in range(7):
+    for group in range(8):
         grads.give_left(group, lefts[group])
 
     def back_copy(which, other):
@@ -972,13 +999,19 @@
             ref, ref, s.back_send.at[which, block], s.back_recv.at[which, block], route.worker(block)
         )
 
-    def send_back(which, value):
+    def order_back(which, value):
         ordered = one_hot(iota((rows, rows), 0).astype(F32) == s.routes[0:1, :])
         s.back_out[which] = (
             dot(ordered, value).reshape(blocks, rows // blocks, width).astype(BF16)
         )
-        each_other(route.home, lambda other: back_copy(which, other).start())
         s.back_in[which, route.block] = s.back_out[which, route.home]
+
+    def send_back(which, part=0, parts=1):
+        def one(step, carry):
+            back_copy(which, (route.home + step) % blocks).start()
+            return carry
+
+        lax.fori_loop(max(1, blocks * part // parts), blocks * (part + 1) // parts, one, 0)
 
     def take_back(which):
         each_other(route.block, lambda block: back_arrival(which, block).wait_recv())
@@ -986,15 +1019,16 @@
         flat = s.back_in[which].astype(F32).reshape(rows, width).astype(BF16)
         s.homes[which] = dot(placed, flat).astype(BF16)
 
+    loaded(l_routes, l_result)
+    order_back(0, s.result[...])
+    send_back(0)
     grads.right_copy(0).wait_recv()
     for unit in range(4):
         grads.take_left(unit, lefts[unit])
         grads.multiply(unit)
-        if unit in (0, 3):
-            grads.tick(unit // 3)
-
-    loaded(l_routes, l_result)
-    send_back(0, s.result[...])
+        if unit < 2:
+            grads.begin(unit)
+
     loaded(l_down, l_up, l_slope, l_small, l_grad_res, l_scaled, l_inverse)
     grad_ffn = s.right[0, :rows, :]
     grad_normed = s.grad_res[...]
@@ -1006,10 +1040,10 @@
         s.small[8 + part : 9 + part, :] = jnp.sum(grad_pre.astype(F32), 0, keepdims=True)
         grad_normed = grad_normed + dot_nt(grad_pre, s.weight_b[block, :])
         grads.right_copy(1 + part).start()
-        if part % 2 == 1:
-            grads.tick(2 + part // 2)
     l_rest = load(full.at[: 4 * width, :], s.weight_a)
 
+    grads.pass_on(0)
+    grads.begin(2)
     scaled = s.scaled[...]
     s.small[3:4, :] = jnp.sum(grad_normed * scaled, 0, keepdims=True)
     s.small[4:5, :] = jnp.sum(grad_normed, 0, keepdims=True)
@@ -1024,48 +1058,32 @@
     s.right[5, :rows, :] = grad_branch
     s.small[2:3, :] = jnp.sum(grad_branch.astype(F32), 0, keepdims=True)
     grads.right_copy(5).start()
-    grads.take_left(4, lefts[4])
-    for part in range(4):
-        grads.right_copy(1 + part).wait_recv()
-        grads.multiply(4 + part)
-        if part == 1:
-            grads.tick(4)
     loaded(l_rest)
     grad_context = dot_nt(grad_branch, s.weight_a[3 * width :, :]).astype(BF16)
     s.grad_context[...] = grad_context
     s.grad_context_t[...] = grad_context.T
-    grads.take_left(5, lefts[5])
-    grads.right_copy(5).wait_recv()
-    grads.multiply(8)
-    grads.tick(5)
     loaded(l_query, l_context_t, l_keys_t, l_values)
 
     def kv_copy(pair, kind):
-        source, target, to = (
-            (s.kv_out.at[pair, route.mate_quarter], s.kv_mate.at[pair, 0], place.mate),
-            (s.kv_out.at[pair, route.far_quarter], s.kv_mate.at[pair, 1], place.mate),
-            (s.kv_out.at[pair, route.pair_quarter], s.kv_pair.at[pair], route.pair),
-        )[kind]
-        return remote(source, target, s.kv_send.at[pair, kind], s.kv_recv.at[pair, kind], to)
-
-    def kv_second(pair):
-        kv_copy(pair, 1).wait_recv()
-        s.kv_out[pair, route.pair_quarter] = (
-            s.kv_out[pair, route.pair_quarter].astype(F32) + s.kv_mate[pair, 1].astype(F32)
-        ).astype(BF16)
-        kv_copy(pair, 2).start()
-
-    def kv_third(pair):
-        kv_copy(pair, 0).wait_recv()
-        kv_copy(pair, 2).wait_recv()
-        summed = (
-            s.kv_out[pair, route.quarter].astype(F32)
-            + s.kv_mate[pair, 0].astype(F32)
-            + s.kv_pair[pair].astype(F32)
-        ).astype(BF16)
+        quarter = (route.mate_quarter, route.far_quarter)[kind]
+        return remote(
+            s.kv_out.at[pair, quarter],
+            s.kv_mate.at[pair, kind],
+            s.kv_send.at[pair, kind],
+            s.kv_recv.at[pair, kind],
+            place.mate,
+        )
+
+    def kv_sum(pair):
         lanes = pl.ds(pl.multiple_of(2 * head * pair, 2 * head), 2 * head)
-        s.right[7, :rows, lanes] = summed[:, : 2 * head]
-        s.right[8, :rows, lanes] = summed[:, 2 * head :]
+        for kind, quarter in enumerate((route.quarter, route.pair_quarter)):
+            kv_copy(pair, kind).wait_recv()
+            summed = (
+                s.kv_out[pair, quarter].astype(F32) + s.kv_mate[pair, kind].astype(F32)
+            ).astype(BF16)
+            block = slice(rows * kind, rows * (kind + 1))
+            s.right_kv[0, block, lanes] = summed[:, : 2 * head]
+            s.right_kv[1, block, lanes] = summed[:, 2 * head :]
 
     left_half = iota((rows, 2 * head), 1) < head
     scale = head**-0.5
@@ -1075,17 +1093,23 @@
         def _():
             probs_copy(pair + 1).start()
 
-        @pl.when(pair % 2 == 1)
+        @pl.when(pair == 2)
         def _():
-            grads.tick(pair // 2 + 6)
+            grads.pass_on(1)
+            grads.begin(3)
+            grads.take_left(4, lefts[4])
+            grads.right_copy(1).wait_recv()
+            grads.multiply(4)
+
+        @pl.when(pair == 4)
+        def _():
+            grads.line((0, 0))
+            grads.pass_on(2)
+            grads.begin(4)
 
         @pl.when(pair > 1)
         def _():
-            kv_second(pair - 2)
-
-        @pl.when(pair > 3)
-        def _():
-            kv_third(pair - 4)
+            kv_sum(pair - 2)
 
         probs_copy(pair).wait()
         slot = pair % 2
@@ -1132,20 +1156,37 @@
     s.right[6, :rows, :] = grad_query
     s.small[0:1, :] = jnp.sum(grad_query.astype(F32), 0, keepdims=True)
     grads.right_copy(6).start()
-    grads.take_left(6, lefts[6])
-    grads.right_copy(6).wait_recv()
-    grads.multiply(9)
-    kv_second(pairs - 2)
-    kv_second(pairs - 1)
-    kv_third(pairs - 4)
-    kv_third(pairs - 3)
-    grads.tick(9)
-    kv_third(pairs - 2)
-    kv_third(pairs - 1)
+    kv_sum(pairs - 2)
+    kv_sum(pairs - 1)
     grads.right_copy(7).start()
     grads.right_copy(8).start()
-    grad_value = s.right[8, :rows, :]
+    grad_value = s.right_kv[1, : 2 * rows, :]
     s.small[1:2, :] = jnp.sum(grad_value.astype(F32), 0, keepdims=True)
+    grads.right_copy(2).wait_recv()
+    grads.multiply(5)
+    grads.line((1, 0), (0, 1))
+    grads.pass_on(3)
+    grads.begin(5)
+    from_keys = dot_nt(s.right_kv[0, : 2 * rows, :], s.weight_a[:width, :])
+    from_values = dot_nt(grad_value, s.weight_a[width : 2 * width, :])
+    s.pair_out[...] = (from_keys[rows:] + from_values[rows:]).astype(BF16)
+    s.grad_res[...] = (
+        s.grad_res[...]
+        + from_keys[:rows]
+        + from_values[:rows]
+        + dot_nt(s.right[6, :rows, :], s.weight_a[2 * width : 3 * width, :])
+    )
+    pair_copies = [
+        remote(
+            s.pair_out.at[block],
+            s.pair_in.at[block],
+            s.pair_send.at[i],
+            s.pair_recv.at[i],
+            route.pair,
+        )
+        for i, block in enumerate((slice(0, rows // 2), slice(rows // 2, rows)))
+    ]
+    pair_copies[0].start()
 
     def sum_copy(stage, to):
         return remote(
@@ -1159,29 +1200,38 @@
     sum_copies = [
         sum_copy(stage, to) for stage, to in enumerate((place.mate, place.across, place.along))
     ]
+    def sum_stage(stage):
+        sum_copies[stage].wait_recv()
+        before = s.small[...] if stage == 0 else s.sums[stage - 1]
+        s.sums[stage] = before + s.got_sums[stage]
+
     sum_copies[0].start()
-    for unit in (10, 11):
-        grads.right_copy(unit - 3).wait_recv()
-        grads.multiply(unit)
-    grads.tick(10)
-    sum_copies[0].wait_recv()
-    s.sums[0] = s.small[...] + s.got_sums[0]
+    grads.right_copy(3).wait_recv()
+    grads.multiply(6)
+    grads.line((2, 0), (1, 1), (0, 2))
+    grads.pass_on(4)
+    grads.begin(6)
+    pair_copies[1].start()
+    sum_stage(0)
     sum_copies[1].start()
-    grad_input = (
-        s.grad_res[...]
-        + dot_nt(s.right[6, :rows, :], s.weight_a[2 * width : 3 * width, :])
-        + dot_nt(s.right[7, :rows, :], s.weight_a[:width, :])
-        + dot_nt(grad_value, s.weight_a[width : 2 * width, :])
-    )
-    send_back(1, grad_input.astype(BF16))
-    grads.tick(11)
-    take_back(0)
-    sum_copies[1].wait_recv()
-    s.sums[1] = s.sums[0] + s.got_sums[1]
+    grads.right_copy(4).wait_recv()
+    grads.multiply(7)
+    grads.line((3, 0), (2, 1), (1, 2), (0, 3))
+    grads.pass_on(5)
+    grads.begin(7)
+    sum_stage(1)
     sum_copies[2].start()
-    grads.tick(12)
-    sum_copies[2].wait_recv()
-    s.sums[2] = s.sums[1] + s.got_sums[2]
+    for copy in pair_copies:
+        copy.wait_recv()
+    order_back(1, (s.grad_res[...] + s.pair_in[...].astype(F32)).astype(BF16))
+    grads.take_left(5, lefts[5])
+    grads.right_copy(5).wait_recv()
+    grads.multiply(8)
+    grads.line((4, 0), (3, 1), (2, 2), (1, 3))
+    grads.pass_on(6)
+    grads.begin(8)
+    send_back(1, 0, 5)
+    sum_stage(2)
 
     def z_copy(step):
         other = (place.z + step) % z_size
@@ -1196,24 +1246,53 @@
     for step in range(1, z_size):
         z_copy(step).start()
     s.got_z[place.z] = s.sums[2]
-    grads.tick(13)
-    take_back(1)
-    home_copy = pltpu.make_async_copy(s.homes, out_homes, s.probs_sem.at[0])
-    home_copy.start()
-    grads.tick(14)
+    take_back(0)
+    grads.take_left(6, lefts[6])
+    grads.take_left(7, lefts[7])
+    grads.right_copy(6).wait_recv()
+    grads.multiply(9)
+    grads.line((5, 0), (4, 1), (3, 2), (2, 3))
+    grads.pass_on(7)
+    grads.begin(9)
+    send_back(1, 1, 5)
+    grads.right_copy(7).wait_recv()
+    grads.multiply(10)
+    grads.line((6, 0), (5, 1), (4, 2), (3, 3))
+    grads.pass_on(8)
+    grads.begin(10)
+    send_back(1, 2, 5)
+    grads.right_copy(8).wait_recv()
+    grads.multiply(11)
+    grads.line((7, 0), (6, 1), (5, 2), (4, 3))
+    grads.pass_on(9)
+    grads.begin(11)
+    send_back(1, 3, 5)
+    grads.line((8, 0), (7, 1), (6, 2), (5, 3))
+    grads.pass_on(10)
+    send_back(1, 4, 5)
     for step in range(1, z_size):
         z_copy(step).wait_recv()
     total = s.got_z[0]
     for z in range(1, z_size):
         total = total + s.got_z[z]
     out_small[...] = total
-    grads.tick(15)
-    grads.tick(16)
+    grads.line((9, 0), (8, 1), (7, 2), (6, 3))
+    grads.pass_on(11)
+    grads.line((10, 0), (9, 1), (8, 2), (7, 3))
+    grads.line((11, 0), (10, 1), (9, 2), (8, 3))
+    take_back(1)
+    home_copy = pltpu.make_async_copy(s.homes, out_homes, s.probs_sem.at[0])
+    home_copy.start()
+    grads.line((11, 1), (10, 2), (9, 3))
+    grads.line((11, 2), (10, 3))
+    grads.line((11, 3))
 
     grads.drain(lefts)
     for pair in range(pairs):
-        for kind in range(3):
+        for kind in range(2):
             kv_copy(pair, kind).wait_send()
+    for copy in pair_copies:
+        copy.wait_send()
     for which in range(2):
         each_other(route.home, lambda other: back_copy(which, other).wait_send())
     for copy in sum_copies:

time: 221 us -> 206 us (0.932)
  Pallas kernels: 206 us -> 192 us
    pallas_call x1, Pallas kernels: 117 us -> 103 us  [encoder_backward(): pl.pallas_call(partial(backward_kernel, z_size), out_shape=(jax.ShapeDtyp...]
where the time goes in v4:
time: 206 us
  Pallas kernels  192 us (93%)
  local copies, waits for them, and re-layouts  9.38 us (5%)
  other arithmetic  3.79 us (2%)
    pallas_call x1, Pallas kernels, encoder_backward(): pl.pallas_call(partial(backward_kernel, z_size), out_shape=(jax.ShapeDtyp...  103 us
    pallas_call x1, Pallas kernels, encoder_forward(): pl.pallas_call(partial(forward_kernel, z_size), out_shape=tuple((jax.Shap...  89.4 us

profile of v4, /device:TPU:0, one launch (start us, length us, event | category | flops | bytes accessed | tf_op | source)
XLA Modules:
  0.0 205.8 jit_solution(10973974795990796442)
XLA Ops:
  0.7 0.8 stack.47
  1.5 0.7 broadcast_in_dim.6
  2.1 0.1 pad.11.clone
  2.2 0.7 fusion.2.pieces
  2.9 1.3 pad_add_fusion.ints
  4.2 89.4 %encoder_forward.1 = (bf16[9216,768]{1,0:T(8,128)(2,1)}, bf16[12,4,256,256]{3,2,1,0:T(8,128)(2,1)}, bf16[4,768,256]{2,1,0:T(8,128)(2,1)}, bf16[4,256,768]{2,1,0:...) custom-call(s32[2,256]{1,0:T(2,128)} %pad_add_fusion.ints, ...), custom_call_target="tpu_custom_call" | custom-call | tf_op jit(solution)/shard_map/encoder_forward/pallas_call | solution.py:640
  93.6 102.5 %encoder_backward.1 = (f32[12,96,768]{2,1,0:T(8,128)}, bf16[2,256,768]{2,1,0:T(8,128)(2,1)}, f32[16,768]{1,0:T(8,128)}) custom-call(bf16[9216,768]{1,0:T(8,128)(2,1)} %get-tuple-element.38.refs_0_, bf16[12,4,256,256]{3,2,1,0:T(8,128)(2,1)} %get-tuple-element.39.refs_1_, bf16[4,768,256]{2,1,0:T(8,128)(2,1)} %get-tuple-element.40.refs_2_, ...), custom_call_target="tpu_custom_call" | custom-call | tf_op jit(solution)/shard_map/encoder_backward/pallas_call | solution.py:1310
  196.1 2.7 %slice_bitcast_fusion.5 = (f32[96,768]{1,0:T(8,128)S(1)}, f32[96,768]{1,0:T(8,128)S(1)}, f32[96,768]{1,0:T(8,128)S(1)}, f32[96,768]{1,0:T(8,128)S(1)}, f32[96,76...) fusion(f32[12,96,768]{2,1,0:T(8,128)} %get-tuple-element.57), kind=kLoop, calls=%fused_computation.6 | loop fusion | bytes 4718592 | tf_op jit(solution)/shard_map/unstack | solution.py:1798
  198.8 0.0 copy-start
  198.8 1.1 pad_maximum_fusion
  199.9 0.3 copy-done
  200.2 0.1 convert_element_type.5
  200.3 1.2 slice_bitcast_fusion
  201.5 0.0 copy-start.1
  201.5 2.4 %slice.73 = f32[4,96,768]{2,1,0:T(8,128)} slice(f32[12,96,768]{2,1,0:T(8,128)} %get-tuple-element.57), slice={[0:4], [0:96], [0:768]} | slice | bytes 2359296 | tf_op jit(solution)/shard_map/slice | solution.py:1800
  203.9 0.0 copy-done.1
  203.9 0.1 constant_dynamic-slice_fusion
  204.0 0.5 slice_bitcast_fusion.10
  204.5 0.7 dynamic_slice.7
  205.2 0.6 slice_reduce_fusion
  (4 shorter events, 0.0 us)
Async XLA Ops:
  198.8 1.4 copy-start
  201.5 2.4 %copy-start.1 = (f32[16,768]{1,0:T(8,128)S(1)}, f32[16,768]{1,0:T(8,128)}, u32[]{:S(2)}) copy-start(f32[16,768]{1,0:T(8,128)} %get-tuple-element.56) | copy-start | bytes 147460

commit v5 on v4

--- a/solution.py
+++ b/solution.py
@@ -109,7 +109,8 @@
         if arriving:
             shard = (across, along, own + mate, corner, corner, across + mate, along + mate, corner + mate)[kind]
         ref = self.at(unit, shard, first, count)
-        return remote(ref, ref, self.send.at[unit, kind], self.recv.at[unit, kind], to)
+        slot = (0, 1, 3, 2, 2, 3, 3, 3)[kind]
+        return remote(ref, ref, self.send, self.recv.at[unit, slot], to)
 
     def begin(self, unit):
         for kind in (0, 1, 2):
@@ -123,9 +124,12 @@
         self.copy(unit, 4, False).start()
         self.copy(unit, 6, False).start()
 
+    def together(self, rows, recv):
+        ref = self.full.at[:rows, :]
+        return remote(ref, ref, self.send, recv, self.place.mate)
+
     def corner(self, unit):
-        self.copy(unit, 3, True).wait_recv()
-        self.copy(unit, 4, True).wait_recv()
+        self.together(BLOCK, self.recv.at[unit, 2]).wait_recv()
         self.copy(unit, 7, False).start()
 
     def tick(self, step):
@@ -135,16 +139,10 @@
             self.corner(step - 3)
 
     def ready(self, unit):
-        for kind in (2, 5, 6, 7):
-            self.copy(unit, kind, True).wait_recv()
+        self.together(4 * BLOCK, self.recv.at[unit, 3]).wait_recv()
 
     def drain(self):
-        def one(unit, carry):
-            for kind in range(8):
-                self.copy(unit, kind, False).wait_send()
-            return carry
-
-        lax.fori_loop(0, UNITS, one, 0)
+        self.together(UNITS * 7 * BLOCK, self.recv.at[0, 0]).wait_send()
 
 
 def iota(shape, axis):
@@ -174,7 +172,7 @@
     ints=lambda t, w, b: pltpu.VMEM((b, 2, t), jnp.int32),
     order=lambda t, w, b: pltpu.VMEM((b, t), jnp.int32),
     ids=lambda t, w, b: pltpu.VMEM((2, 4, 1, t), jnp.int32),
-    pieces=lambda t, w, b: pltpu.VMEM((8, 16, w // 2), BF16),
+    pieces=lambda t, w, b: pltpu.VMEM((8, 16, 128), F32),
     vectors=lambda t, w, b: pltpu.VMEM((16, w), F32),
     pack_out=lambda t, w, b: pltpu.VMEM((2, b, t // b, w), BF16),
     pack_in=lambda t, w, b: pltpu.VMEM((2, b, t // b, w), BF16),
@@ -205,18 +203,13 @@
     grad_ffn=lambda t, w, b: pltpu.VMEM((t, w), BF16),
     small=lambda t, w, b: pltpu.VMEM((16, w), F32),
     routes=lambda t, w, b: pltpu.VMEM((8, t), F32),
-    ints_send=lambda t, w, b: pltpu.SemaphoreType.DMA((b,)),
-    ints_recv=lambda t, w, b: pltpu.SemaphoreType.DMA((b,)),
-    piece_send=lambda t, w, b: pltpu.SemaphoreType.DMA((8,)),
-    piece_recv=lambda t, w, b: pltpu.SemaphoreType.DMA((8,)),
-    pack_send=lambda t, w, b: pltpu.SemaphoreType.DMA((2, b)),
-    pack_recv=lambda t, w, b: pltpu.SemaphoreType.DMA((2, b)),
-    misc_send=lambda t, w, b: pltpu.SemaphoreType.DMA((8,)),
-    misc_recv=lambda t, w, b: pltpu.SemaphoreType.DMA((8,)),
-    weight_send=lambda t, w, b: pltpu.SemaphoreType.DMA((UNITS, 8)),
-    weight_recv=lambda t, w, b: pltpu.SemaphoreType.DMA((UNITS, 8)),
-    own_sem=lambda t, w, b: pltpu.SemaphoreType.DMA((UNITS,)),
-    store_sem=lambda t, w, b: pltpu.SemaphoreType.DMA((32,)),
+    all_send=lambda t, w, b: pltpu.SemaphoreType.DMA((5,)),
+    all_recv=lambda t, w, b: pltpu.SemaphoreType.DMA((4,)),
+    misc_send=lambda t, w, b: pltpu.SemaphoreType.DMA((5,)),
+    misc_recv=lambda t, w, b: pltpu.SemaphoreType.DMA((5,)),
+    weight_recv=lambda t, w, b: pltpu.SemaphoreType.DMA((UNITS, 4)),
+    own_sem=lambda t, w, b: pltpu.SemaphoreType.DMA((2,)),
+    store_sem=lambda t, w, b: pltpu.SemaphoreType.DMA((18,)),
 )
 
 class Kept(NamedTuple):
@@ -250,7 +243,11 @@
     return centre * inverse, inverse
 
 
-def forward_kernel(z_size, ints, ids, tokens, cotangent, teacher, pieces, w_query, w_key, w_value, w_out, w_up, w_down, *refs):
+def forward_kernel(z_size, *refs):
+    order, valid, ids, tokens, cotangent, teacher = refs[:6]
+    narrow, up_bias = refs[6:14], refs[14]
+    w_query, w_key, w_value, w_out, w_up, w_down = refs[15:21]
+    refs = refs[21:]
     outs = Kept(*refs[: len(Kept._fields)])
     s = SimpleNamespace(**dict(zip(FORWARD_SCRATCH, refs[len(Kept._fields) :])))
     route = Route(z_size)
@@ -258,7 +255,7 @@
     rows, width = tokens.shape
     blocks = route.blocks
     full = s.full
-    weights = Weights(place, full, s.weight_send, s.weight_recv)
+    weights = Weights(place, full, s.all_send.at[4], s.weight_recv)
     stores = []
 
     def keep(source, target):
@@ -272,27 +269,32 @@
         + [w_down.at[BLOCK * i : BLOCK * (i + 1), :] for i in range(4)]
     )
     own_copies = [
-        pltpu.make_async_copy(source, weights.at(unit, place.dp), s.own_sem.at[unit])
+        pltpu.make_async_copy(source, weights.at(unit, place.dp), s.own_sem.at[min(unit // 2, 1)])
         for unit, source in enumerate(sources)
     ]
     for copy in own_copies:
         copy.start()
-    s.ints[route.home] = ints[...]
+    s.ints[route.home, 0:1, :] = order[...]
+    s.ints[route.home, 1:2, :] = valid[...]
+    s.pieces[place.dp] = jnp.zeros((16, 128), F32)
+    for index, ref in enumerate(narrow):
+        s.pieces[place.dp, index : index + 1, :BLOCK] = ref[...].astype(F32)
+    s.pieces[place.dp, 8:11, :] = up_bias[...].astype(F32)
     s.teach_out[...] = teacher[...].astype(BF16)
     route.greet_all()
 
     def ints_copy(other):
         return remote(
-            ints,
             s.ints.at[route.home],
-            s.ints_send.at[other],
-            s.ints_recv.at[route.home],
+            s.ints.at[route.home],
+            s.all_send.at[0],
+            s.all_recv.at[0],
             route.owner(other),
         )
 
-    def ints_arrival(other):
-        ref = s.ints.at[other]
-        return remote(ref, ref, s.ints_send.at[other], s.ints_recv.at[other], route.owner(other))
+    def all_others(ref, index):
+        ref = ref.at[: ref.shape[0] - 1]
+        return remote(ref, ref, s.all_send.at[index], s.all_recv.at[index], place.mate)
 
     def each_other(start, action):
         def one(step, carry):
@@ -305,35 +307,36 @@
     def piece_copy(step):
         other = (place.dp + step) % 8
         return remote(
-            pieces,
             s.pieces.at[place.dp],
-            s.piece_send.at[step],
-            s.piece_recv.at[step],
+            s.pieces.at[place.dp],
+            s.all_send.at[1],
+            s.all_recv.at[1],
             {"dp": other},
         )
 
     for step in range(1, 8):
         piece_copy(step).start()
-    s.pieces[place.dp] = pieces[...]
     ids_copy = remote(ids, s.ids.at[1], s.misc_send.at[0], s.misc_recv.at[0], place.mate)
     ids_copy.start()
     s.ids[0] = ids[...]
-    for copy in own_copies[:2]:
-        copy.wait()
+    def own_wait(units, index):
+        ref = full.at[: BLOCK * units, :]
+        pltpu.make_async_copy(ref, ref, s.own_sem.at[index]).wait()
+
+    own_wait(2, 0)
     weights.begin(0)
     weights.begin(1)
-    for copy in own_copies[2:]:
-        copy.wait()
-
-    each_other(route.home, lambda other: ints_arrival(other).wait_recv())
+    own_wait(UNITS - 2, 1)
+
+    all_others(s.ints, 0).wait_recv()
     count = jnp.zeros((1, rows), F32)
     for other in range(blocks):
         s.order[other : other + 1, :] = s.ints[other, 0:1, :]
         count = count + s.ints[other, 1:2, :].astype(F32)
     count = jnp.sum(count, 1, keepdims=True)
-    order = s.order[...]
-    source = lax.shift_right_logical(order, 8)
-    local = (order - source * rows).astype(F32)
+    orders = s.order[...]
+    source = lax.shift_right_logical(orders, 8)
+    local = (orders - source * rows).astype(F32)
     mine = source == route.home
     earlier = one_hot(iota((rows, rows), 0) < iota((rows, rows), 1))
     rank = dot(one_hot(mine), earlier)
@@ -362,15 +365,9 @@
         return remote(
             s.pack_out.at[which, block],
             s.pack_in.at[which, route.home],
-            s.pack_send.at[which, block],
-            s.pack_recv.at[which, route.home],
+            s.all_send.at[2 + which],
+            s.all_recv.at[2 + which],
             route.worker(block),
-        )
-
-    def pack_arrival(which, other):
-        ref = s.pack_in.at[which, other]
-        return remote(
-            ref, ref, s.pack_send.at[which, other], s.pack_recv.at[which, other], route.owner(other)
         )
 
     def pack(which, value):
@@ -383,7 +380,7 @@
         s.pack_in[which, route.home] = s.pack_out[which, route.block]
 
     def take_pack(which):
-        each_other(route.home, lambda other: pack_arrival(which, other).wait_recv())
+        all_others(s.pack_in.at[which], 2 + which).wait_recv()
         flat = s.pack_in[which].astype(F32).reshape(rows, width).astype(BF16)
         return dot(one_hot(lane.astype(F32) == place_col), flat).astype(BF16)
 
@@ -397,19 +394,19 @@
     stays = route.block == route.home
     teach_copy = remote(s.teach_out, s.teach_in, s.misc_send.at[1], s.misc_recv.at[1], moved_to)
 
-    for step in range(1, 8):
-        piece_copy(step).wait_recv()
+    all_others(s.pieces, 1).wait_recv()
     wrapped = one_hot(
         iota((BLOCK, width), 0) == iota((BLOCK, width), 1) - BLOCK * (iota((BLOCK, width), 1) // BLOCK)
     )
     owner = iota((16, width), 1) // BLOCK
     vectors = jnp.zeros((16, width), F32)
     for k in range(8):
-        vectors = vectors + jnp.where(owner == k, dot(s.pieces[k, :, :BLOCK], wrapped), 0.0)
+        vectors = vectors + jnp.where(owner == k, dot(s.pieces[k, :, :BLOCK].astype(BF16), wrapped), 0.0)
     s.vectors[...] = vectors
     for k in range(8):
-        part = s.pieces[k, 8:9, :].astype(F32)
-        s.vectors[8 + k // 2 : 9 + k // 2, 4 * BLOCK * (k % 2) : 4 * BLOCK * (k % 2 + 1)] = part
+        for i in range(3):
+            first = 4 * BLOCK * (k % 2) + 128 * i
+            s.vectors[8 + k // 2 : 9 + k // 2, first : first + 128] = s.pieces[k, 8 + i : 9 + i, :]
 
     def vector(index):
         return s.vectors[index : index + 1, :]
@@ -590,8 +587,8 @@
     def _():
         teach_copy.wait_recv()
 
-    valid = column(s.ints[route.block, 1:2, :].astype(F32))
-    miss = valid * (result - s.teach_in[...].astype(F32))
+    counts = column(s.ints[route.block, 1:2, :].astype(F32))
+    miss = counts * (result - s.teach_in[...].astype(F32))
     factor = 1.0 / (count * width)
     s.small[...] = jnp.zeros((16, width), F32)
     s.small[12:13, :] = jnp.sum(miss * miss, 0, keepdims=True) * factor
@@ -615,11 +612,8 @@
     keep(s.routes, outs.routes)
 
     weights.drain()
-    each_other(route.home, lambda other: ints_copy(other).wait_send())
-    for which in range(2):
-        each_other(route.block, lambda block: pack_copy(which, block).wait_send())
-    for step in range(1, 8):
-        piece_copy(step).wait_send()
+    for index, ref in enumerate((s.ints, s.pieces, s.pack_out.at[0], s.pack_out.at[1])):
+        all_others(ref, index).wait_send()
     ids_copy.wait_send()
     for kind in range(3):
         rows_copy(kind, False).wait_send()
@@ -632,8 +626,8 @@
         copy.wait()
 
 
-def encoder_forward(z_size, ints, ids, tokens, cotangent, teacher, pieces, *shards):
-    rows, width = tokens.shape
+def encoder_forward(z_size, *inputs):
+    rows, width = inputs[3].shape
     blocks = 8 * z_size
     scratch = {name: make(rows, width, blocks) for name, make in FORWARD_SCRATCH.items()}
     vmem, anywhere = pl.BlockSpec(memory_space=pltpu.VMEM), pl.BlockSpec(memory_space=pl.ANY)
@@ -642,14 +636,14 @@
         out_shape=tuple(
             jax.ShapeDtypeStruct(scratch[name].shape, scratch[name].dtype) for name in Kept._fields
         ),
-        in_specs=[vmem] * 6 + [anywhere] * 6,
+        in_specs=[vmem] * 15 + [anywhere] * 6,
         out_specs=(anywhere,) * len(Kept._fields),
         scratch_shapes=list(scratch.values()),
         compiler_params=pltpu.CompilerParams(
             collective_id=0, has_side_effects=True, vmem_limit_bytes=62 * 2**20
         ),
         name="encoder_forward",
-    )(ints, ids, tokens, cotangent, teacher, pieces, *shards)
+    )(*inputs)
     return Kept(*results)
 
 
@@ -679,8 +673,8 @@
         return remote(
             source.at[self.source_rows(group, j, 1 - self.place.core), :],
             target,
-            self.s.left_send.at[group, j],
-            self.s.left_recv.at[group, j],
+            self.s.end_send.at[4],
+            self.s.left_recv.at[group],
             self.place.mate,
         )
 
@@ -693,7 +687,7 @@
         return pltpu.make_async_copy(
             source.at[self.source_rows(group, j, self.place.core), :],
             target,
-            self.s.left_own.at[group, j],
+            self.s.left_own.at[group],
         )
 
     def give_left(self, group, source):
@@ -702,9 +696,16 @@
             self.left_own(group, j, source).start()
 
     def take_left(self, group, source):
-        for j in range(4):
-            self.left_copy(group, j, source).wait_recv()
-            self.left_own(group, j, source).wait()
+        if group < 6:
+            mine = self.s.left.at[group, :, : self.tok_rows]
+            theirs = self.s.left.at[group, :, self.tok_rows :]
+        else:
+            mine = self.s.left_x.at[:, : self.tok_rows]
+            theirs = self.s.left_x.at[:, self.tok_rows * 2 : self.tok_rows * 3]
+        remote(
+            theirs, theirs, self.s.end_send.at[4], self.s.left_recv.at[group], self.place.mate
+        ).wait_recv()
+        pltpu.make_async_copy(mine, mine, self.s.left_own.at[group]).wait()
 
     def own_right(self, index):
         return self.s.right.at[index, : self.tok_rows, :]
@@ -719,7 +720,7 @@
         return remote(
             source,
             target,
-            self.s.right_send.at[index],
+            self.s.end_send.at[5] if index < 7 else self.s.end_send.at[3],
             self.s.right_recv.at[index],
             self.place.mate,
         )
@@ -736,7 +737,15 @@
             (s.out_x.at[unit], s.in_z.at[0, unit], {"ctx": place.z + 1}),
             (s.out_y.at[unit], s.in_z.at[1, unit], {"ctx": place.z - 1}),
         )[kind]
-        return remote(source, target, s.send.at[unit, kind], s.recv.at[unit, kind], to)
+        if 2 <= kind < 6:
+            send = s.send.at[unit]
+        else:
+            send = s.end_send.at[(0, 0, 0, 0, 0, 0, 1, 2)[kind]]
+        recv = s.recv.at[unit, (0, 0, 1, 1, 1, 1, 2, 3)[kind]]
+        return remote(source, target, send, recv, to)
+
+    def together(self, ref, send, recv):
+        return remote(ref, ref, send, recv, self.place.mate)
 
     def part(self, j):
         return pl.ds(pl.multiple_of(BLOCK * j, 32), BLOCK)
@@ -763,11 +772,10 @@
 
     def pass_on(self, unit):
         low, high, s = self.low, self.high, self.s
-        self.copy(unit, 0).wait_recv()
+        self.together(s.out_d.at[unit], s.send.at[unit], s.recv.at[unit, 0]).wait_recv()
         s.out_y[unit, low] = (
             s.out_y[unit, low].astype(F32) + s.in_dx[unit].astype(F32)
         ).astype(BF16)
-        self.copy(unit, 1).wait_recv()
         s.out_x[unit, high] = (
             s.out_x[unit, high].astype(F32) + s.in_dy[unit].astype(F32)
         ).astype(BF16)
@@ -776,13 +784,12 @@
 
     def gather(self, unit):
         s = self.s
-        for kind in (2, 3, 4, 5):
-            self.copy(unit, kind).wait_recv()
+        both = self.together(s.in_x.at[:2], s.send.at[unit], s.recv.at[unit, 1])
+        both.wait_recv()
         s.total[unit] = (
             s.total[unit] + s.in_x[unit].astype(F32) + s.in_y[unit].astype(F32)
         )
-        for kind in (2, 3, 4, 5):
-            self.copy(unit, kind).wait_send()
+        both.wait_send()
 
     def hop(self, unit, step):
         place, s = self.place, self.s
@@ -799,7 +806,7 @@
 
     def result(self, unit):
         return pltpu.make_async_copy(
-            self.s.total.at[unit], self.out.at[unit], self.s.out_sem.at[unit]
+            self.s.total.at[unit], self.out.at[unit], self.s.out_sem.at[0]
         )
 
     def finish(self, unit):
@@ -832,29 +839,25 @@
                 self.finish(unit)
 
     def drain(self, lefts):
-        place = self.place
-
-        def one(unit, carry):
-            self.copy(unit, 0).wait_send()
-            self.copy(unit, 1).wait_send()
-
-            @pl.when(place.z < place.z_size - 1)
-            def _():
-                self.copy(unit, 6).wait_send()
-
-            @pl.when(place.z > 0)
-            def _():
-                self.copy(unit, 7).wait_send()
-
-            self.result(unit).wait()
-            return carry
-
-        lax.fori_loop(0, UNITS, one, 0)
-        for group in range(8):
-            for j in range(4):
-                self.left_copy(group, j, lefts[group]).wait_send()
-        for index in range(9):
-            self.right_copy(index).wait_send()
+        place, s = self.place, self.s
+
+        def sent(ref, index):
+            self.together(ref, s.end_send.at[index], s.recv.at[0, 0]).wait_send()
+
+        sent(s.out_d, 0)
+
+        @pl.when(place.z < place.z_size - 1)
+        def _():
+            sent(s.out_x, 1)
+
+        @pl.when(place.z > 0)
+        def _():
+            sent(s.out_y, 2)
+
+        pltpu.make_async_copy(s.total, s.total, s.out_sem.at[0]).wait()
+        sent(s.right_kv.at[:, : 2 * self.tok_rows, :], 3)
+        sent(lefts[0], 4)
+        sent(s.right.at[:, : self.tok_rows, :], 5)
 
 
 BACKWARD_SCRATCH = dict(
@@ -899,24 +902,22 @@
     sums=lambda t, w, b: pltpu.VMEM((3, 16, w), F32),
     got_sums=lambda t, w, b: pltpu.VMEM((3, 16, w), F32),
     got_z=lambda t, w, b: pltpu.VMEM((b // 8, 16, w), F32),
-    send=lambda t, w, b: pltpu.SemaphoreType.DMA((UNITS, 8)),
-    recv=lambda t, w, b: pltpu.SemaphoreType.DMA((UNITS, 8)),
-    left_send=lambda t, w, b: pltpu.SemaphoreType.DMA((8, 4)),
-    left_recv=lambda t, w, b: pltpu.SemaphoreType.DMA((8, 4)),
-    left_own=lambda t, w, b: pltpu.SemaphoreType.DMA((8, 4)),
-    right_send=lambda t, w, b: pltpu.SemaphoreType.DMA((9,)),
+    send=lambda t, w, b: pltpu.SemaphoreType.DMA((UNITS,)),
+    end_send=lambda t, w, b: pltpu.SemaphoreType.DMA((6,)),
+    recv=lambda t, w, b: pltpu.SemaphoreType.DMA((UNITS, 4)),
+    left_recv=lambda t, w, b: pltpu.SemaphoreType.DMA((8,)),
+    left_own=lambda t, w, b: pltpu.SemaphoreType.DMA((8,)),
     right_recv=lambda t, w, b: pltpu.SemaphoreType.DMA((9,)),
-    out_sem=lambda t, w, b: pltpu.SemaphoreType.DMA((UNITS,)),
-    load_sem=lambda t, w, b: pltpu.SemaphoreType.DMA((20,)),
+    out_sem=lambda t, w, b: pltpu.SemaphoreType.DMA((1,)),
+    load_sem=lambda t, w, b: pltpu.SemaphoreType.DMA((15,)),
     probs_sem=lambda t, w, b: pltpu.SemaphoreType.DMA((2,)),
-    kv_send=lambda t, w, b: pltpu.SemaphoreType.DMA((HEADS // 2, 2)),
-    kv_recv=lambda t, w, b: pltpu.SemaphoreType.DMA((HEADS // 2, 2)),
-    pair_send=lambda t, w, b: pltpu.SemaphoreType.DMA((2,)),
-    pair_recv=lambda t, w, b: pltpu.SemaphoreType.DMA((2,)),
-    back_send=lambda t, w, b: pltpu.SemaphoreType.DMA((2, b)),
-    back_recv=lambda t, w, b: pltpu.SemaphoreType.DMA((2, b)),
-    sum_send=lambda t, w, b: pltpu.SemaphoreType.DMA((3 + b // 8,)),
-    sum_recv=lambda t, w, b: pltpu.SemaphoreType.DMA((3 + b // 8,)),
+    kv_send=lambda t, w, b: pltpu.SemaphoreType.DMA((1,)),
+    kv_recv=lambda t, w, b: pltpu.SemaphoreType.DMA((HEADS // 2,)),
+    pair_sem=lambda t, w, b: pltpu.SemaphoreType.DMA((2,)),
+    back_send=lambda t, w, b: pltpu.SemaphoreType.DMA((2,)),
+    back_recv=lambda t, w, b: pltpu.SemaphoreType.DMA((2,)),
+    sum_send=lambda t, w, b: pltpu.SemaphoreType.DMA((4,)),
+    sum_recv=lambda t, w, b: pltpu.SemaphoreType.DMA((4,)),
 )
 
 
@@ -988,16 +989,14 @@
         return remote(
             s.back_out.at[which, other],
             s.back_in.at[which, route.block],
-            s.back_send.at[which, other],
-            s.back_recv.at[which, route.block],
+            s.back_send.at[which],
+            s.back_recv.at[which],
             route.owner(other),
         )
 
-    def back_arrival(which, block):
-        ref = s.back_in.at[which, block]
-        return remote(
-            ref, ref, s.back_send.at[which, block], s.back_recv.at[which, block], route.worker(block)
-        )
+    def all_back(ref, which):
+        ref = ref.at[which, : blocks - 1]
+        return remote(ref, ref, s.back_send.at[which], s.back_recv.at[which], place.mate)
 
     def order_back(which, value):
         ordered = one_hot(iota((rows, rows), 0).astype(F32) == s.routes[0:1, :])
@@ -1014,7 +1013,7 @@
         lax.fori_loop(max(1, blocks * part // parts), blocks * (part + 1) // parts, one, 0)
 
     def take_back(which):
-        each_other(route.block, lambda block: back_arrival(which, block).wait_recv())
+        all_back(s.back_in, which).wait_recv()
         placed = one_hot(iota((rows, rows), 0).astype(F32) == s.routes[1:2, :])
         flat = s.back_in[which].astype(F32).reshape(rows, width).astype(BF16)
         s.homes[which] = dot(placed, flat).astype(BF16)
@@ -1069,15 +1068,16 @@
         return remote(
             s.kv_out.at[pair, quarter],
             s.kv_mate.at[pair, kind],
-            s.kv_send.at[pair, kind],
-            s.kv_recv.at[pair, kind],
+            s.kv_send.at[0],
+            s.kv_recv.at[pair],
             place.mate,
         )
 
     def kv_sum(pair):
         lanes = pl.ds(pl.multiple_of(2 * head * pair, 2 * head), 2 * head)
+        got = s.kv_mate.at[pair]
+        remote(got, got, s.kv_send.at[0], s.kv_recv.at[pair], place.mate).wait_recv()
         for kind, quarter in enumerate((route.quarter, route.pair_quarter)):
-            kv_copy(pair, kind).wait_recv()
             summed = (
                 s.kv_out[pair, quarter].astype(F32) + s.kv_mate[pair, kind].astype(F32)
             ).astype(BF16)
@@ -1100,10 +1100,11 @@
             grads.take_left(4, lefts[4])
             grads.right_copy(1).wait_recv()
             grads.multiply(4)
+            grads.line((0, 0))
 
         @pl.when(pair == 4)
         def _():
-            grads.line((0, 0))
+            grads.line((1, 0), (0, 1))
             grads.pass_on(2)
             grads.begin(4)
 
@@ -1164,9 +1165,9 @@
     s.small[1:2, :] = jnp.sum(grad_value.astype(F32), 0, keepdims=True)
     grads.right_copy(2).wait_recv()
     grads.multiply(5)
-    grads.line((1, 0), (0, 1))
     grads.pass_on(3)
     grads.begin(5)
+    grads.line((2, 0), (1, 1), (0, 2))
     from_keys = dot_nt(s.right_kv[0, : 2 * rows, :], s.weight_a[:width, :])
     from_values = dot_nt(grad_value, s.weight_a[width : 2 * width, :])
     s.pair_out[...] = (from_keys[rows:] + from_values[rows:]).astype(BF16)
@@ -1180,11 +1181,11 @@
         remote(
             s.pair_out.at[block],
             s.pair_in.at[block],
-            s.pair_send.at[i],
-            s.pair_recv.at[i],
+            s.pair_sem.at[0],
+            s.pair_sem.at[1],
             route.pair,
         )
-        for i, block in enumerate((slice(0, rows // 2), slice(rows // 2, rows)))
+        for block in (slice(rows // 4 * j, rows // 4 * (j + 1)) for j in range(4))
     ]
     pair_copies[0].start()
 
@@ -1206,31 +1207,54 @@
         s.sums[stage] = before + s.got_sums[stage]
 
     sum_copies[0].start()
+    pair_copies[1].start()
     grads.right_copy(3).wait_recv()
     grads.multiply(6)
-    grads.line((2, 0), (1, 1), (0, 2))
     grads.pass_on(4)
     grads.begin(6)
-    pair_copies[1].start()
-    sum_stage(0)
-    sum_copies[1].start()
+    grads.line((3, 0), (2, 1), (1, 2))
+    pair_copies[2].start()
+    pair_copies[3].start()
     grads.right_copy(4).wait_recv()
     grads.multiply(7)
-    grads.line((3, 0), (2, 1), (1, 2), (0, 3))
     grads.pass_on(5)
     grads.begin(7)
-    sum_stage(1)
-    sum_copies[2].start()
-    for copy in pair_copies:
-        copy.wait_recv()
-    order_back(1, (s.grad_res[...] + s.pair_in[...].astype(F32)).astype(BF16))
+    grads.line((4, 0), (3, 1), (2, 2))
     grads.take_left(5, lefts[5])
     grads.right_copy(5).wait_recv()
     grads.multiply(8)
-    grads.line((4, 0), (3, 1), (2, 2), (1, 3))
     grads.pass_on(6)
     grads.begin(8)
-    send_back(1, 0, 5)
+    grads.line((5, 0), (4, 1), (3, 2))
+    sum_stage(0)
+    sum_copies[1].start()
+    remote(
+        s.pair_out, s.pair_in, s.pair_sem.at[0], s.pair_sem.at[1], route.pair
+    ).wait_recv()
+    order_back(1, (s.grad_res[...] + s.pair_in[...].astype(F32)).astype(BF16))
+    send_back(1, 0, 2)
+    grads.take_left(6, lefts[6])
+    grads.take_left(7, lefts[7])
+    grads.right_copy(6).wait_recv()
+    grads.multiply(9)
+    grads.pass_on(7)
+    grads.begin(9)
+    grads.line((6, 0), (5, 1), (4, 2))
+    grads.right_copy(7).wait_recv()
+    grads.multiply(10)
+    grads.pass_on(8)
+    grads.begin(10)
+    grads.line((7, 0), (6, 1), (5, 2))
+    send_back(1, 1, 2)
+    sum_stage(1)
+    sum_copies[2].start()
+    grads.right_copy(8).wait_recv()
+    grads.multiply(11)
+    grads.pass_on(9)
+    grads.begin(11)
+    grads.line((8, 0), (7, 1), (6, 2))
+    grads.pass_on(10)
+    grads.line((9, 0), (8, 1), (7, 2))
     sum_stage(2)
 
     def z_copy(step):
@@ -1238,67 +1262,41 @@
         return remote(
             s.sums.at[2],
             s.got_z.at[place.z],
-            s.sum_send.at[2 + step],
-            s.sum_recv.at[2 + step],
+            s.sum_send.at[3],
+            s.sum_recv.at[3],
             {"ctx": other},
         )
 
     for step in range(1, z_size):
         z_copy(step).start()
     s.got_z[place.z] = s.sums[2]
+    grads.pass_on(11)
+    grads.line((10, 0), (9, 1), (8, 2))
     take_back(0)
-    grads.take_left(6, lefts[6])
-    grads.take_left(7, lefts[7])
-    grads.right_copy(6).wait_recv()
-    grads.multiply(9)
-    grads.line((5, 0), (4, 1), (3, 2), (2, 3))
-    grads.pass_on(7)
-    grads.begin(9)
-    send_back(1, 1, 5)
-    grads.right_copy(7).wait_recv()
-    grads.multiply(10)
-    grads.line((6, 0), (5, 1), (4, 2), (3, 3))
-    grads.pass_on(8)
-    grads.begin(10)
-    send_back(1, 2, 5)
-    grads.right_copy(8).wait_recv()
-    grads.multiply(11)
-    grads.line((7, 0), (6, 1), (5, 2), (4, 3))
-    grads.pass_on(9)
-    grads.begin(11)
-    send_back(1, 3, 5)
-    grads.line((8, 0), (7, 1), (6, 2), (5, 3))
-    grads.pass_on(10)
-    send_back(1, 4, 5)
-    for step in range(1, z_size):
-        z_copy(step).wait_recv()
+    grads.line((11, 0), (10, 1), (9, 2), (0, 3), (1, 3), (2, 3), (3, 3))
+    grads.line((11, 1), (10, 2), (4, 3), (5, 3), (6, 3), (7, 3))
+    take_back(1)
+    home_copy = pltpu.make_async_copy(s.homes, out_homes, s.probs_sem.at[0])
+    home_copy.start()
+    grads.line((11, 2), (8, 3), (9, 3))
+    z_all = s.got_z.at[: z_size - 1]
+    z_all = remote(z_all, z_all, s.sum_send.at[3], s.sum_recv.at[3], place.mate)
+    z_all.wait_recv()
     total = s.got_z[0]
     for z in range(1, z_size):
         total = total + s.got_z[z]
     out_small[...] = total
-    grads.line((9, 0), (8, 1), (7, 2), (6, 3))
-    grads.pass_on(11)
-    grads.line((10, 0), (9, 1), (8, 2), (7, 3))
-    grads.line((11, 0), (10, 1), (9, 2), (8, 3))
-    take_back(1)
-    home_copy = pltpu.make_async_copy(s.homes, out_homes, s.probs_sem.at[0])
-    home_copy.start()
-    grads.line((11, 1), (10, 2), (9, 3))
-    grads.line((11, 2), (10, 3))
-    grads.line((11, 3))
+    grads.line((10, 3), (11, 3))
 
     grads.drain(lefts)
-    for pair in range(pairs):
-        for kind in range(2):
-            kv_copy(pair, kind).wait_send()
-    for copy in pair_copies:
-        copy.wait_send()
+    remote(s.kv_mate, s.kv_mate, s.kv_send.at[0], s.kv_recv.at[0], place.mate).wait_send()
+    pair_all = remote(s.pair_out, s.pair_in, s.pair_sem.at[0], s.pair_sem.at[1], route.pair)
+    pair_all.wait_send()
     for which in range(2):
-        each_other(route.home, lambda other: back_copy(which, other).wait_send())
+        all_back(s.back_out, which).wait_send()
     for copy in sum_copies:
         copy.wait_send()
-    for step in range(1, z_size):
-        z_copy(step).wait_send()
+    z_all.wait_send()
     home_copy.wait()
 
 
@@ -1322,6 +1320,82 @@
         ),
         name="encoder_backward",
     )(*kept)
+
+
+def finish_kernel(grads, homes, small, *refs):
+    out, loss, input_grad, g_query, g_key, g_value, g_out, g_up, g_down = refs[:9]
+    narrow, up_bias = refs[9:17], refs[17]
+    units, rows_in, rows_out, in_sem, out_sem = refs[18:]
+    width = units.shape[2]
+    row_loads = [
+        pltpu.make_async_copy(homes.at[i], rows_in.at[i], in_sem.at[UNITS + i]) for i in range(2)
+    ]
+    unit_loads = [
+        pltpu.make_async_copy(grads.at[i], units.at[i], in_sem.at[i]) for i in range(UNITS)
+    ]
+    for copy in row_loads + unit_loads:
+        copy.start()
+    dp = lax.axis_index("dp")
+    turned = pltpu.roll(small[...], (width - BLOCK * dp) % width, 1)
+    for index, ref in enumerate(narrow):
+        ref[...] = turned[index : index + 1, :BLOCK]
+    up_row = small[pl.ds(8 + dp // 2, 1), :]
+    up_row = jnp.where(dp % 2 == 0, up_row[:, : 4 * BLOCK], up_row[:, 4 * BLOCK :])
+    for i in range(3):
+        up_bias[i : i + 1, :] = up_row[:, 128 * i : 128 * (i + 1)]
+    loss[...] = jnp.sum(small[12:13, :], 1, keepdims=True)
+    stores = []
+
+    def store(source, target):
+        copy = pltpu.make_async_copy(source, target, out_sem.at[len(stores)])
+        copy.start()
+        stores.append(copy)
+
+    for i, target in enumerate((out, input_grad)):
+        row_loads[i].wait()
+        rows_out[i] = rows_in[i].astype(F32)
+        store(rows_out.at[i], target)
+    targets = [g_down.at[BLOCK * i : BLOCK * (i + 1), :] for i in range(4)]
+    targets += [g_up.at[:, width * i : width * (i + 1)] for i in range(4)]
+    targets += [g_out, g_query, g_key, g_value]
+    for i, target in enumerate(targets):
+        unit_loads[i].wait()
+        store(units.at[i], target)
+    for copy in stores:
+        copy.wait()
+
+
+def finish(grads, homes, small):
+    _, rows, width = homes.shape
+    vmem, anywhere = pl.BlockSpec(memory_space=pltpu.VMEM), pl.BlockSpec(memory_space=pl.ANY)
+    row = jax.ShapeDtypeStruct((rows, width), F32)
+    square = jax.ShapeDtypeStruct((BLOCK, width), F32)
+    return pl.pallas_call(
+        finish_kernel,
+        out_shape=(
+            row,
+            jax.ShapeDtypeStruct((1, 1), F32),
+            row,
+            square,
+            square,
+            square,
+            square,
+            jax.ShapeDtypeStruct((BLOCK, 4 * width), F32),
+            jax.ShapeDtypeStruct((4 * BLOCK, width), F32),
+        )
+        + (jax.ShapeDtypeStruct((1, BLOCK), F32),) * 8
+        + (jax.ShapeDtypeStruct((3, 128), F32),),
+        in_specs=[anywhere, anywhere, vmem],
+        out_specs=(anywhere, vmem) + (anywhere,) * 7 + (vmem,) * 9,
+        scratch_shapes=[
+            pltpu.VMEM((UNITS, BLOCK, width), F32),
+            pltpu.VMEM((2, rows, width), BF16),
+            pltpu.VMEM((2, rows, width), F32),
+            pltpu.SemaphoreType.DMA((UNITS + 2,)),
+            pltpu.SemaphoreType.DMA((UNITS + 2,)),
+        ],
+        name="finish",
+    )(grads, homes, small)
 
 
 norm_eps = 1e-12
@@ -1748,26 +1822,17 @@
 ):
     rows, width = tokens.shape
     z_size = lax.axis_size("ctx")
-    ints = jnp.stack([token_order, valid])
-    ids = sequence_ids.reshape(z_size, 1, rows)
-    narrow = jnp.stack(
-        [b_query, b_value, b_out, norm1_gain, norm1_bias, b_down, norm2_gain, norm2_bias]
-    )
-    pieces = jnp.concatenate(
-        [
-            jnp.pad(narrow, ((0, 0), (0, 3 * BLOCK))),
-            b_up[None],
-            jnp.zeros((7, 4 * BLOCK), BF16),
-        ]
-    )
+    narrow = (b_query, b_value, b_out, norm1_gain, norm1_bias, b_down, norm2_gain, norm2_bias)
     kept = encoder_forward(
         z_size,
-        ints,
-        ids,
+        token_order.reshape(1, rows),
+        valid.reshape(1, rows),
+        sequence_ids.reshape(z_size, 1, rows),
         tokens,
         cotangent,
         teacher,
-        pieces,
+        *(vector.reshape(1, BLOCK) for vector in narrow),
+        b_up.reshape(3, 128),
         w_query,
         w_key,
         w_value,
@@ -1775,32 +1840,30 @@
         w_up,
         w_down,
     )
-    grads, homes, small = encoder_backward(z_size, kept)
-    dp_index = lax.axis_index("dp")
-    own = lax.dynamic_slice_in_dim(small[:8], dp_index * BLOCK, BLOCK, axis=1)
-    own_up = lax.dynamic_slice_in_dim(
-        small[8:12].reshape(-1), dp_index * 4 * BLOCK, 4 * BLOCK
-    )
-    homes = homes.astype(F32)
+    results = finish(*encoder_backward(z_size, kept))
+    output, loss, input_grad, g_query, g_key, g_value, g_out, g_up, g_down = results[:9]
+    g_b_query, g_b_value, g_b_out, g_gain1, g_bias1, g_b_down, g_gain2, g_bias2, g_b_up = (
+        vector.reshape(-1) for vector in results[9:]
+    )
     return (
-        homes[0],
-        jnp.sum(small[12]),
-        homes[1],
-        grads[9],
-        own[0],
-        grads[10],
-        grads[11],
-        own[1],
-        grads[8],
-        own[2],
-        own[3],
-        own[4],
-        jnp.concatenate(list(grads[4:8]), axis=1),
-        own_up,
-        grads[:4].reshape(4 * BLOCK, width),
-        own[5],
-        own[6],
-        own[7],
+        output,
+        loss.reshape(()),
+        input_grad,
+        g_query,
+        g_b_query,
+        g_key,
+        g_value,
+        g_b_value,
+        g_out,
+        g_b_out,
+        g_gain1,
+        g_bias1,
+        g_up,
+        g_b_up,
+        g_down,
+        g_b_down,
+        g_gain2,
+        g_bias2,
     )
 
 

time: 206 us -> 188 us (0.913)
  local copies, waits for them, and re-layouts: 9.38 us -> 0 us
  Pallas kernels: 192 us -> 186 us
  other arithmetic: 3.79 us -> 0 us
    pallas_call x1, Pallas kernels: 103 us -> 96.3 us  [encoder_backward(): pl.pallas_call(partial(backward_kernel, z_size), out_shape=(jax.ShapeDtyp...]
    pallas_call x0 -> x1, Pallas kernels: none -> 5.17 us  [finish(): pl.pallas_call(finish_kernel, out_shape=(row, jax.ShapeDtypeStruct((1, 1)...]
    pallas_call x1, Pallas kernels: 89.4 us -> 84.9 us  [encoder_forward(): pl.pallas_call(partial(forward_kernel, z_size), out_shape=tuple((jax.Shap...]
    another operation x2 -> x0, local copies, waits for them, and re-layouts: 3.45 us -> none  [the longest x1 2.65 us: per_device_fast(): list(grads[4:8])]
    slice x3 -> x0, local copies, waits for them, and re-layouts: 2.37 us -> none  [the longest x1 2.37 us: per_device_fast(): grads[:4].reshape(4 * BLOCK, width)]
where the time goes in v5:
time: 188 us; the launch traced here: 187 us
  Pallas kernels  186 us (99%)
    pallas_call x1, Pallas kernels, encoder_backward(): pl.pallas_call(partial(backward_kernel, z_size), out_shape=(jax.ShapeDtyp...  96.3 us
    pallas_call x1, Pallas kernels, encoder_forward(): pl.pallas_call(partial(forward_kernel, z_size), out_shape=tuple((jax.Shap...  84.9 us
    pallas_call x1, Pallas kernels, finish(): pl.pallas_call(finish_kernel, out_shape=(row, jax.ShapeDtypeStruct((1, 1)...  5.17 us

profile of v5, /device:TPU:0, one launch (start us, length us, event | category | flops | bytes accessed | tf_op | source)
XLA Modules:
  0.0 187.3 jit_solution(15861425481329077392)
XLA Ops:
  0.7 84.9 %encoder_forward.1 = (bf16[9216,768]{1,0:T(8,128)(2,1)}, bf16[12,4,256,256]{3,2,1,0:T(8,128)(2,1)}, bf16[4,768,256]{2,1,0:T(8,128)(2,1)}, bf16[4,256,768]{2,1,0:...) custom-call(s32[1,256]{1,0:T(1,128)} %bitcast.23, ...), custom_call_target="tpu_custom_call" | custom-call | tf_op jit(solution)/shard_map/encoder_forward/pallas_call | solution.py:634
  85.6 96.3 %encoder_backward.1 = (f32[12,96,768]{2,1,0:T(8,128)}, bf16[2,256,768]{2,1,0:T(8,128)(2,1)}, f32[16,768]{1,0:T(8,128)}) custom-call(bf16[9216,768]{1,0:T(8,128)(2,1)} %get-tuple-element.56.refs_0_, bf16[12,4,256,256]{3,2,1,0:T(8,128)(2,1)} %get-tuple-element.57.refs_1_, bf16[4,768,256]{2,1,0:T(8,128)(2,1)} %get-tuple-element.58.refs_2_, ...), custom_call_target="tpu_custom_call" | custom-call | tf_op jit(solution)/shard_map/encoder_backward/pallas_call | solution.py:1308
  181.9 5.2 %finish.1 = (f32[256,768]{1,0:T(8,128)}, f32[1,1]{1,0:T(1,128)}, f32[256,768]{1,0:T(8,128)}, f32[96,768]{1,0:T(8,128)}, f32[96,768]{1,0:T(8,128)}, /*index=5*/f3...) custom-call(f32[12,96,768]{2,1,0:T(8,128)} %get-tuple-element.73.gra, ...), custom_call_target="tpu_custom_call" | custom-call | tf_op jit(solution)/shard_map/finish/pallas_call | solution.py:1373
